TPU v7x, 32 devices: a whole 2x2x4 slice. The times are simulated.
32 devices in a mesh: dp: 8 (over y, x, core), tensor: 4 (over z).
Axes of the slice: x: 2, y: 2, z: 4, core: 2. Of those that a mesh axis runs over, the one named last changes fastest.
Arguments:
- tokens: bfloat16 [8192, 768], P(('dp', 'tensor')), may hold values from -6 to 6
- lengths: int32 [8], P('dp'), may hold values from 128 to 1024, as said below
- cotangent: bfloat16 [8192, 768], P(('dp', 'tensor')), may hold values from -6 to 6
- ln1_gain: float32 [768], replicated, may hold values from 0.25 to 1.75
- ln1_shift: float32 [768], replicated, may hold values from -1.75 to 1.75
- w_qkv: bfloat16 [3, 768, 768], P(None, None, 'tensor'), may hold values from -0.21875 to 0.21875
- b_qv: float32 [2, 768], P(None, 'tensor'), may hold values from -3 to 3
- w_out: bfloat16 [768, 768], P('tensor'), may hold values from -0.875 to 0.875
- b_out: float32 [768], replicated, may hold values from -1.75 to 1.75
- ln2_gain: float32 [768], replicated, may hold values from 0.25 to 1.75
- ln2_shift: float32 [768], replicated, may hold values from -1.75 to 1.75
- w_fc: bfloat16 [768, 3072], P(None, 'tensor'), may hold values from -0.21875 to 0.21875
- b_fc: float32 [3072], P('tensor'), may hold values from -3 to 3
- w_proj: bfloat16 [3072, 768], P('tensor'), may hold values from -0.21875 to 0.21875
- b_proj: float32 [768], replicated, may hold values from -1.75 to 1.75
Outputs:
- output: bfloat16 [8192, 768], P(('dp', 'tensor'))
- grad_tokens: float32 [8192, 768], P(('dp', 'tensor'))
- grad_ln1_gain: float32 [768], replicated
- grad_ln1_shift: float32 [768], replicated
- grad_w_qkv: float32 [3, 768, 768], P(None, None, 'tensor')
- grad_b_qv: float32 [2, 768], P(None, 'tensor')
- grad_w_out: float32 [768, 768], P('tensor')
- grad_b_out: float32 [768], replicated
- grad_ln2_gain: float32 [768], replicated
- grad_ln2_shift: float32 [768], replicated
- grad_w_fc: float32 [768, 3072], P(None, 'tensor')
- grad_b_fc: float32 [3072], P('tensor')
- grad_w_proj: float32 [3072, 768], P('tensor')
- grad_b_proj: float32 [768], replicated
Inputs may be any that keep to these rules, and one draw needn't show every extreme that they name: lengths of the 8 sequences; positions at or beyond a sequence's length are padding; some sequence has exactly 1024 real tokens and some exactly 128.
All inputs are finite; a program needn't handle non-finite values.
Results may differ from a plain program's by a relative error of at most 0.018.
Values may be sent and summed in bfloat16 or wider, within the bound.
No kernel may reach another device: no remote copies, remote signals or barrier semaphores. Data moves between devices by JAX's collectives and lax.ppermute only.
A program may use at most 128 MiB of HBM per device.

v0:
```python
import math

import jax
import jax.numpy as jnp
from jax import lax
from jax.experimental import pallas as pl
from jax.experimental.pallas import tpu as pltpu
from jax.sharding import PartitionSpec as P

HD = 64
LEN = 1024
BLOCKS = 8

EPSILON = 1e-05
NEGATIVE = -1e30
BF = jnp.bfloat16
F32 = jnp.float32


def dot(a, b, ca, cb):
    return lax.dot_general(a, b, (((ca,), (cb,)), ((), ())), preferred_element_type=F32)


def centre(stream):
    average = jnp.mean(stream, axis=-1, keepdims=True)
    centered = stream - average
    variance = jnp.mean(centered * centered, axis=-1, keepdims=True)
    inverse = lax.rsqrt(variance + EPSILON)
    return centered * inverse, inverse


def normalize(stream, gain, shift):
    return centre(stream)[0] * gain + shift


def normalize_back(stream, gain, grad):
    hat, inverse = centre(stream)
    scaled = grad * gain
    mean = jnp.mean(scaled, axis=-1, keepdims=True)
    along = jnp.mean(scaled * hat, axis=-1, keepdims=True)
    back = (scaled - mean - hat * along) * inverse
    return back, jnp.sum(grad * hat, axis=0, keepdims=True), jnp.sum(grad, axis=0, keepdims=True)


SCALE2 = math.log2(math.e) / math.sqrt(HD)
BLOCK = 256
VM = pl.BlockSpec(memory_space=pltpu.VMEM)
SM = pl.BlockSpec(memory_space=pltpu.SMEM)


def whole(shape):
    return pl.BlockSpec(shape, lambda j: (0,) * len(shape))


def allowed(first, length, diagonal):
    key = first + lax.broadcasted_iota(jnp.int32, (BLOCK, BLOCK), 0)
    real = key < length
    if diagonal:
        query = first + lax.broadcasted_iota(jnp.int32, (BLOCK, BLOCK), 1)
        real = real & (key <= query)
    return real


def slot(index, quarter):
    return pl.ds(pl.multiple_of((index ^ quarter) * BLOCK, BLOCK), BLOCK)


def attend_kernel(
    scalar_ref, own_ref, near_ref, far_ref, both_ref, w_ref, bias_ref, rows_ref, qkv_ref, out_ref, lse_ref
):
    length = scalar_ref[0]
    quarter = scalar_ref[1]
    width = qkv_ref.shape[0] // 3
    span = qkv_ref.shape[1]
    for index, ref in enumerate((own_ref, near_ref, far_ref, both_ref)):
        rows_ref[slot(index, quarter), :] = ref[...]
    for part in range(3):
        block = pl.ds(part * width, width)
        value = dot(w_ref[block, :], rows_ref[...], 1, 1) + bias_ref[block, :]
        qkv_ref[block, :] = value.astype(BF)

    def head(h, carry):
        at = pl.multiple_of(h * HD, HD)
        for index in range(span // BLOCK):
            offset = index * BLOCK
            query = qkv_ref[pl.ds(at, HD), pl.ds(offset, BLOCK)]
            scores = []
            for first in range(0, offset + BLOCK, BLOCK):
                key = qkv_ref[pl.ds(width + at, HD), pl.ds(first, BLOCK)]
                value = dot(key, query, 0, 0) * SCALE2
                scores.append(jnp.where(allowed(first, length, first == offset), value, NEGATIVE))
            top = scores[0].max(axis=0, keepdims=True)
            for value in scores[1:]:
                top = jnp.maximum(top, value.max(axis=0, keepdims=True))
            weights = [jnp.exp2(value - top) for value in scores]
            total = sum(value.sum(axis=0, keepdims=True) for value in weights)
            inverse = 1.0 / total
            acc = None
            for other, value in enumerate(weights):
                probs = (value * inverse).astype(BF)
                part = dot(qkv_ref[pl.ds(2 * width + at, HD), pl.ds(other * BLOCK, BLOCK)], probs, 1, 0)
                acc = part if acc is None else acc + part
            out_ref[pl.ds(at, HD), slot(index, quarter)] = acc.astype(BF)
            lse_ref[pl.ds(h, 1), pl.ds(offset, BLOCK)] = top + jnp.log2(total)
        return carry

    lax.fori_loop(0, width // HD, head, 0)


def attend(scalars, blocks, w, bias):
    rows, width = w.shape
    span = 4 * BLOCK
    return pl.pallas_call(
        attend_kernel,
        in_specs=[SM] + [VM] * 6,
        out_specs=[VM] * 4,
        out_shape=[
            jax.ShapeDtypeStruct((span, width), BF),
            jax.ShapeDtypeStruct((rows, span), BF),
            jax.ShapeDtypeStruct((rows // 3, span), BF),
            jax.ShapeDtypeStruct((rows // 3 // HD, span), F32),
        ],
        cost_estimate=pl.CostEstimate(
            flops=2 * rows * span * width + 2 * rows * span * span,
            bytes_accessed=8 * rows * span,
            transcendentals=2 * span * span,
        ),
        name="attend",
    )(scalars, *blocks, w, bias)


def attend_back_kernel(
    scalar_ref, qkv_ref, grad_ref, lse_ref, w_ref, out_ref, bias_ref, back_ref, acc_k, acc_v
):
    length = scalar_ref[0]
    quarter = scalar_ref[1]
    width = qkv_ref.shape[0] // 3
    span = qkv_ref.shape[1]
    scaling = 1.0 / math.sqrt(HD)

    def head(h, carry):
        at = pl.multiple_of(h * HD, HD)
        for index in range(span // BLOCK):
            offset = index * BLOCK
            block = pl.ds(offset, BLOCK)
            query = qkv_ref[pl.ds(at, HD), block]
            grad = grad_ref[pl.ds(at, HD), slot(index, quarter)]
            lse = lse_ref[pl.ds(h, 1), block]
            probs = []
            g_probs = []
            inner = None
            for first in range(0, offset + BLOCK, BLOCK):
                keys = pl.ds(first, BLOCK)
                value = dot(qkv_ref[pl.ds(width + at, HD), keys], query, 0, 0) * SCALE2 - lse
                value = jnp.exp2(jnp.where(allowed(first, length, first == offset), value, NEGATIVE))
                g_value = dot(qkv_ref[pl.ds(2 * width + at, HD), keys], grad, 0, 0)
                part = (value * g_value).sum(axis=0, keepdims=True)
                inner = part if inner is None else inner + part
                probs.append(value)
                g_probs.append(g_value)
            acc_q = None
            for other, (value, g_value) in enumerate(zip(probs, g_probs)):
                keys = pl.ds(other * BLOCK, BLOCK)
                g_score = (value * (g_value - inner)).astype(BF)
                part = dot(qkv_ref[pl.ds(width + at, HD), keys], g_score, 1, 0)
                acc_q = part if acc_q is None else acc_q + part
                part_k = dot(query, g_score, 1, 1)
                part_v = dot(grad, value.astype(BF), 1, 1)
                if other == index:
                    acc_k[:, keys] = part_k
                    acc_v[:, keys] = part_v
                else:
                    acc_k[:, keys] += part_k
                    acc_v[:, keys] += part_v
            out_ref[pl.ds(at, HD), block] = (acc_q * scaling).astype(BF)
        out_ref[pl.ds(width + at, HD), :] = (acc_k[...] * scaling).astype(BF)
        out_ref[pl.ds(2 * width + at, HD), :] = acc_v[...].astype(BF)
        return carry

    lax.fori_loop(0, width // HD, head, 0)
    bias_ref[...] = jnp.sum(out_ref[...].astype(F32), axis=1, keepdims=True)
    for index in range(span // BLOCK):
        value = dot(out_ref[:, pl.ds(index * BLOCK, BLOCK)], w_ref[...], 0, 0)
        back_ref[slot(index, quarter), :] = value.astype(BF)


def attend_back(scalars, qkv, grad, lse, w):
    rows, span = qkv.shape
    width = w.shape[1]
    return pl.pallas_call(
        attend_back_kernel,
        in_specs=[SM] + [VM] * 4,
        out_specs=[VM] * 3,
        out_shape=[
            jax.ShapeDtypeStruct((rows, span), BF),
            jax.ShapeDtypeStruct((rows, 1), F32),
            jax.ShapeDtypeStruct((span, width), BF),
        ],
        scratch_shapes=[pltpu.VMEM((HD, span), F32), pltpu.VMEM((HD, span), F32)],
        cost_estimate=pl.CostEstimate(
            flops=2 * rows * span * width + 4 * rows * span * span,
            bytes_accessed=10 * rows * span,
            transcendentals=2 * span * span,
        ),
        name="attend_back",
    )(scalars, qkv, grad, lse, w)


CURVE = math.sqrt(2.0 / math.pi)
CUBE = 0.044715


def feed_kernel(
    att_ref, stream_ref, out_w_ref, fc_ref, proj_ref, vec_ref, bias_ref,
    mid_ref, low_ref, act_ref, slope_ref, next_ref, norm_ref,
):
    step_at = pl.program_id(0)

    @pl.when(step_at == 0)
    def _():
        middle = stream_ref[...] + dot(att_ref[...], out_w_ref[...], 0, 0) + vec_ref[0:1, :]
        mid_ref[...] = middle
        low_ref[...] = normalize(middle, vec_ref[1:2, :], vec_ref[2:3, :]).astype(BF)
        next_ref[...] = middle + vec_ref[3:4, :]

    value = dot(low_ref[...], fc_ref[...], 1, 1) + bias_ref[...]
    square = value * value
    bent = jnp.tanh(value * (CURVE + CURVE * CUBE * square))
    half = 0.5 * (1.0 + bent)
    act = (value * half).astype(BF)
    act_ref[...] = act
    slope_ref[...] = half + (0.5 * value) * (1.0 - bent * bent) * (CURVE + 3.0 * CURVE * CUBE * square)
    next_ref[...] += dot(act, proj_ref[...], 1, 0)

    @pl.when(step_at == pl.num_programs(0) - 1)
    def _():
        norm_ref[...] = normalize(next_ref[...], vec_ref[4:5, :], vec_ref[5:6, :]).astype(BF)


def feed(attended, stream, w, vectors):
    rows, width = stream.shape
    hidden = w["fc"].shape[0]
    step_size = 768
    block = pl.BlockSpec((rows, step_size), lambda j: (0, j))
    weight = pl.BlockSpec((step_size, width), lambda j: (j, 0))
    return pl.pallas_call(
        feed_kernel,
        grid=(hidden // step_size,),
        in_specs=[
            whole((width, rows)), whole((rows, width)), whole((width, width)), weight, weight,
            whole((6, width)), pl.BlockSpec((1, step_size), lambda j: (0, j)),
        ],
        out_specs=[
            whole((rows, width)), whole((rows, width)), block, block, whole((rows, width)), whole((rows, width)),
        ],
        out_shape=[
            jax.ShapeDtypeStruct((rows, width), F32),
            jax.ShapeDtypeStruct((rows, width), BF),
            jax.ShapeDtypeStruct((rows, hidden), BF),
            jax.ShapeDtypeStruct((rows, hidden), F32),
            jax.ShapeDtypeStruct((rows, width), F32),
            jax.ShapeDtypeStruct((rows, width), BF),
        ],
        cost_estimate=pl.CostEstimate(
            flops=4 * rows * width * hidden, bytes_accessed=6 * width * hidden, transcendentals=rows * hidden
        ),
        name="feed",
    )(attended, stream, w["out"], w["fc"], w["proj"], vectors, w["b_fc"])


def feed_back_kernel(
    grad_ref, slope_ref, proj_ref, fc_ref, mid_ref, out_w_ref, gain_ref,
    pre_ref, bias_ref, back_ref, low_ref, heads_ref, sums_ref, acc_ref,
):
    step_at = pl.program_id(0)
    pre = (dot(grad_ref[...].astype(BF), proj_ref[...], 1, 1) * slope_ref[...]).astype(BF)
    pre_ref[...] = pre
    bias_ref[...] = jnp.sum(pre.astype(F32), axis=0, keepdims=True)
    part = dot(pre, fc_ref[...], 1, 0)

    @pl.when(step_at == 0)
    def _():
        acc_ref[...] = part

    @pl.when(step_at > 0)
    def _():
        acc_ref[...] += part

    @pl.when(step_at == pl.num_programs(0) - 1)
    def _():
        grad = grad_ref[...]
        back, gain_sum, shift_sum = normalize_back(mid_ref[...], gain_ref[...], acc_ref[...])
        back = grad + back
        back_ref[...] = back
        low = back.astype(BF)
        low_ref[...] = low
        heads_ref[...] = dot(out_w_ref[...], low, 1, 1).astype(BF)
        sums_ref[0:1, :] = jnp.sum(back, axis=0, keepdims=True)
        sums_ref[1:2, :] = gain_sum
        sums_ref[2:3, :] = shift_sum
        sums_ref[3:4, :] = jnp.sum(grad, axis=0, keepdims=True)


def feed_back(gradient, slope, middle, w, gain):
    rows, width = gradient.shape
    hidden = w["fc"].shape[0]
    step_size = 768
    block = pl.BlockSpec((rows, step_size), lambda j: (0, j))
    weight = pl.BlockSpec((step_size, width), lambda j: (j, 0))
    return pl.pallas_call(
        feed_back_kernel,
        grid=(hidden // step_size,),
        in_specs=[
            whole((rows, width)), block, weight, weight, whole((rows, width)), whole((width, width)),
            whole((1, width)),
        ],
        out_specs=[
            block, pl.BlockSpec((1, step_size), lambda j: (0, j)), whole((rows, width)), whole((rows, width)),
            whole((width, rows)), whole((4, width)),
        ],
        out_shape=[
            jax.ShapeDtypeStruct((rows, hidden), BF),
            jax.ShapeDtypeStruct((1, hidden), F32),
            jax.ShapeDtypeStruct((rows, width), F32),
            jax.ShapeDtypeStruct((rows, width), BF),
            jax.ShapeDtypeStruct((width, rows), BF),
            jax.ShapeDtypeStruct((4, width), F32),
        ],
        scratch_shapes=[pltpu.VMEM((rows, width), F32)],
        cost_estimate=pl.CostEstimate(
            flops=4 * rows * width * hidden, bytes_accessed=6 * width * hidden, transcendentals=0
        ),
        name="feed_back",
    )(gradient, slope, w["proj"], w["fc"], middle, w["out"], gain)


def norm_back_kernel(own_ref, far_ref, mid_ref, stream_ref, gain_ref, out_ref, low_ref, sums_ref):
    grad = own_ref[...] + far_ref[...].astype(F32)
    back, gain_sum, shift_sum = normalize_back(stream_ref[...], gain_ref[...], grad)
    back = mid_ref[...] + back
    out_ref[...] = back
    low_ref[...] = back.astype(BF)
    sums_ref[0:1, :] = gain_sum
    sums_ref[1:2, :] = shift_sum


def norm_back(own, far, grad_middle, stream, gain):
    shape = stream.shape
    return pl.pallas_call(
        norm_back_kernel,
        in_specs=[VM] * 5,
        out_specs=[VM] * 3,
        out_shape=[
            jax.ShapeDtypeStruct(shape, F32),
            jax.ShapeDtypeStruct(shape, BF),
            jax.ShapeDtypeStruct((2, shape[1]), F32),
        ],
        cost_estimate=pl.CostEstimate(
            flops=20 * shape[0] * shape[1], bytes_accessed=20 * shape[0] * shape[1], transcendentals=0
        ),
        name="norm_back",
    )(own, far, grad_middle, stream, gain)


class Place:
    def __init__(self, members, shards):
        self.members = members
        self.shards = shards
        self.d = lax.axis_index("dp")
        self.t = lax.axis_index("tensor")
        self.core = self.d & 1
        self.half = self.t & 1
        self.seq = self.t >> 1
        self.quarter = 2 * self.half + self.core

    def dp(self, value, bit):
        return lax.ppermute(value, "dp", [(i, i ^ bit) for i in range(self.members)])

    def tensor(self, value, bit):
        return lax.ppermute(value, "tensor", [(i, i ^ bit) for i in range(self.shards)])

    def placing(self):
        pairs = []
        for d in range(self.members):
            for t in range(self.shards):
                target = ((d >> 1) * 2 + (t & 1)) * self.shards + 2 * (d & 1) + (t >> 1)
                pairs.append((d * self.shards + t, target))
        return pairs

    def place(self, value):
        return lax.ppermute(value, ("dp", "tensor"), self.placing())

    def unplace(self, value):
        return lax.ppermute(value, ("dp", "tensor"), [(b, a) for a, b in self.placing()])

    def flags(self):
        return (self.t & 2, self.t & 1, self.d & 4, self.d & 2, self.d & 1)

    def cross(self, value, own):
        pairs = []
        for d in range(self.members):
            for t in range(self.shards):
                if ((t >> 1) == (d & 1)) == own:
                    pairs.append((d * self.shards + t, d * self.shards + (t ^ 2)))
        return lax.ppermute(value, ("dp", "tensor"), pairs)

    def heads_weight(self, shard):
        rows = shard.shape[0] // 4
        piece = lax.dynamic_slice_in_dim(shard, ((self.d & 6) >> 1) * rows, rows, axis=0)
        value = self.cross(piece, True)
        value = ordered(self.d & 2, value, self.dp(value, 2))
        value = ordered(self.d & 4, value, self.dp(value, 4))
        return jnp.where(self.seq == self.core, shard, value)


def ordered(flag, first, second, axis=0):
    return jnp.where(
        flag == 0,
        jnp.concatenate([first, second], axis),
        jnp.concatenate([second, first], axis),
    )


def tie(*values):
    return lax.optimization_barrier(values)


def gather_rows(place, rows):
    near = place.dp(rows, 1)
    far = place.tensor(rows, 1)
    return rows, near, far, place.dp(far, 1)


def heads_to_rows(place, attended):
    span = attended.shape[1] // 2
    far = place.tensor(attended[:, span:], 1)
    near = jnp.concatenate([attended[:, span // 2 : span], far[:, span // 2 :]])
    return jnp.concatenate([attended[:, : span // 2], far[:, : span // 2], place.dp(near, 1)])


def rows_to_pair(place, value):
    rows = value.shape[0] // 2
    return jnp.concatenate([value[:rows], place.dp(value[rows:], 1)], axis=1)


def pair_to_heads(place, pair):
    rows = pair.shape[0] // 2
    return jnp.concatenate([pair[:rows], place.tensor(pair[rows:], 1)], axis=1)


def flip(value, axis, flag):
    return jnp.where(flag == 0, value, jnp.flip(value, axis))


def from_heads(place, value):
    parts = value.reshape(2, 2, 2, 2, 2, -1, value.shape[1])
    for axis, flag in ((0, place.core ^ place.seq), (2, place.d & 4), (3, place.d & 2), (4, place.d & 1)):
        parts = flip(parts, axis, flag)
    return parts.transpose(4, 2, 3, 1, 0, 5, 6).reshape(value.shape)


def to_heads(place, value):
    parts = value.reshape(2, 2, 2, 2, 2, -1, value.shape[1])
    parts = parts.transpose(4, 3, 1, 2, 0, 5, 6)
    for axis, flag in ((0, place.core ^ place.seq), (2, place.d & 4), (3, place.d & 2), (4, place.d & 1)):
        parts = flip(parts, axis, flag)
    return parts.reshape(value.shape)


def to_natural(place, value):
    tail = value.shape[1:]
    parts = value.reshape((2, 2, 2, 2, 2, -1) + tail)
    order = (4, 3, 1, 2, 0, 5) + tuple(range(6, parts.ndim))
    parts = parts.transpose(order)
    for axis, flag in enumerate(place.flags()):
        parts = flip(parts, axis, flag)
    return parts.reshape(value.shape)


def own_pieces(place, shard):
    tail = shard.shape[1:]
    pieces = shard.reshape((2, 2, 2, -1) + tail)
    for axis, flag in enumerate(place.flags()[2:]):
        pieces = flip(pieces, axis, flag)
    order = (2, 0, 1, 3) + tuple(range(4, pieces.ndim))
    return pieces.transpose(order).reshape((BLOCKS, -1) + tail)


def my_piece(place, shard):
    rows = shard.shape[0] // BLOCKS
    return lax.dynamic_slice_in_dim(shard, (place.d & 7) * rows, rows, axis=0)


def split(value):
    high = lax.reduce_precision(value, 8, 7)
    return high.astype(BF), (value - high).astype(BF)


def over_tensor(place, mine):
    two = place.tensor(mine, 2)
    rest = place.tensor(jnp.stack([mine, two]), 1)
    return jnp.concatenate([two[None], rest])


def over_dp(place, zero, first, second):
    one = place.dp(zero, first)
    far = place.dp(jnp.stack([zero, one]), second)
    if first == 2:
        four = jnp.stack([zero, one, far[0], far[1]])
    else:
        four = jnp.stack([zero, far[0], one, far[1]])
    return jnp.concatenate([four, place.dp(four, 1)])


def plus(left, right):
    return (left.astype(F32) + right.astype(F32)).astype(BF)


def layer_forward(place, stream, normed, scalars, w):
    blocks = gather_rows(place, normed)
    rows, qkv, attended, log_sums = attend(scalars, blocks, w["qkv"], w["b_qkv"])
    attended = from_heads(place, heads_to_rows(place, attended))
    middle, normed2, activated, slope, result, normed = feed(attended, stream, w, w["vectors"])
    return result, normed, (stream, rows, qkv, log_sums, attended, middle, normed2, activated, slope)


def pieces(value):
    return value.reshape(BLOCKS, 4, -1, value.shape[-1])


def both_layers(left, right, ca, cb):
    return dot(jnp.concatenate(left, ca), jnp.concatenate(right, cb), ca, cb).astype(BF)


def second_backward(place, gradient, scalars, w, cache, output):
    stream, rows, qkv, log_sums, attended, middle, normed2, activated, slope = cache
    grad_pre, bias, grad_middle, mid_low, grad_heads, sums = feed_back(gradient, slope, middle, w, w["ln2_gain"])
    pair = rows_to_pair(place, to_heads(place, grad_heads))
    grad_qkv, qkv_sums, parts = attend_back(scalars, qkv, pair_to_heads(place, pair), log_sums, w["qkv"])
    parts = parts.reshape(4, -1, parts.shape[1])
    moved = place.dp(jnp.stack([parts[1], parts[3]]), 1)
    far = place.tensor(plus(parts[2], moved[1]), 1)
    own = parts[0].astype(F32) + moved[0].astype(F32)
    far, output = tie(far, output)
    gradient_in, low, norms = norm_back(own, far, grad_middle, stream, w["ln1_gain"])
    left = (gradient.astype(BF), activated, grad_pre, normed2, attended, mid_low, grad_qkv, rows)
    return gradient_in, low, left, (norms, sums, bias, qkv_sums), output


def choose(flag, value):
    return jnp.where(flag == 0, value[0], value[1]), jnp.where(flag == 0, value[1], value[0])


def chunks(value):
    return value.reshape((2, 2, 2, 2) + value.shape[2:])


def first_step(place, value):
    return place.dp(value[:, 1, 1], 2), place.dp(value[1, :, 0], 4)


def second_step(place, value, moved):
    one = plus(value[:, 0, 1], moved[0])
    other = plus(value[0, :, 0], moved[1])
    return one[0], other[0], place.dp(one[1], 4), place.dp(other[1], 2)


def first_backward(place, gradient, low, scalars, w, cache, later, later_small):
    stream, rows, qkv, log_sums, attended, middle, normed2, activated, slope = cache
    heads = qkv.shape[0] // 3
    proj = pieces(both_layers((activated, later[1]), (low, later[0]), 0, 0))
    proj_far = place.dp(proj[4:], 1)
    grad_pre, bias, grad_middle, mid_low, grad_heads, sums = feed_back(gradient, slope, middle, w, w["ln2_gain"])
    proj, proj_far, grad_pre, mid_low, grad_heads = tie(proj, proj_far, grad_pre, mid_low, grad_heads)
    proj = chunks(plus(proj[:4], proj_far))
    moved = first_step(place, proj)
    pair = rows_to_pair(place, to_heads(place, grad_heads))
    grad_attended = pair_to_heads(place, pair)
    fc = jnp.concatenate(
        [
            pieces(both_layers((grad_pre, later[2]), (normed2, later[3]), 0, 0)),
            pieces(both_layers((attended, later[4]), (mid_low, later[5]), 1, 0)),
        ],
        2,
    )
    fc_far = place.dp(fc[4:], 1)
    fc, fc_far, grad_attended, *moved = tie(fc, fc_far, grad_attended, *moved)
    proj1, proj0, *moved = second_step(place, proj, moved)
    fc = chunks(plus(fc[:4], fc_far))
    fc, grad_attended, proj1, proj0, *moved = tie(fc, grad_attended, proj1, proj0, *moved)
    fc_moved = first_step(place, fc)
    proj1 = plus(proj1, moved[0])
    proj0 = plus(proj0, moved[1])
    proj_t = place.tensor(proj1, 1)
    grad_qkv, qkv_sums, parts = attend_back(scalars, qkv, grad_attended, log_sums, w["qkv"])
    grad_qkv, parts, proj_t, *fc_moved = tie(grad_qkv, parts, proj_t, *fc_moved)
    parts = parts.reshape(4, -1, parts.shape[1])
    moved = place.dp(jnp.stack([parts[1], parts[3]]), 1)
    fc1, fc0, *fc_moved = second_step(place, fc, fc_moved)
    grad_wqkv = both_layers((grad_qkv, later[6]), (rows, later[7]), 1, 0)
    moved, grad_wqkv, *fc_moved = tie(moved, grad_wqkv, *fc_moved)
    width = grad_wqkv.shape[1]
    value = grad_wqkv.reshape(2, 2, 2, -1, width)
    keep_x, send = choose(place.d & 2, value[0])
    qkv_x = place.dp(send, 2)
    keep_y, send = choose(place.d & 4, value[1])
    qkv_y = place.dp(send, 4)
    far = place.tensor(plus(parts[2], moved[1]), 1)
    own = parts[0].astype(F32) + moved[0].astype(F32)
    fc1 = plus(fc1, fc_moved[0])
    fc0 = plus(fc0, fc_moved[1])
    proj = plus(proj0, proj_t)
    far, fc1, fc0, proj, qkv_x, qkv_y = tie(far, fc1, fc0, proj, qkv_x, qkv_y)
    fc_t = place.tensor(fc1, 1)
    proj_t = place.tensor(proj[1], 2)
    keep_x, send = choose(place.d & 4, plus(keep_x, qkv_x))
    qkv_x = place.dp(send, 4)
    keep_y, send = choose(place.d & 2, plus(keep_y, qkv_y))
    qkv_y = place.dp(send, 2)
    gradient_in, low, norms = norm_back(own, far, grad_middle, stream, w["ln1_gain"])
    small = [a + b for a, b in zip((norms, sums, bias, qkv_sums), later_small)]
    small = pack_small(place, small, heads)
    small = small + place.dp(small, 1)
    low, small, fc_t, proj_t, qkv_x, qkv_y = tie(low, small, fc_t, proj_t, qkv_x, qkv_y)
    both = jnp.stack([plus(keep_x, qkv_x), plus(keep_y, qkv_y)])
    for bit in place.extra:
        both = plus(both, place.dp(both, bit))
    both_far = place.cross(both, False)
    fc = plus(fc0, fc_t)
    fc_t = place.tensor(fc[1], 2)
    placed = place.unplace(low)
    small_far = place.dp(small, 2)
    fc_t, both_far, proj_t, small_far = tie(fc_t, both_far, proj_t, small_far)
    small = small + small_far
    small_far = place.dp(small, 4)
    large = jnp.concatenate([plus(fc[0], fc_t), plus(proj[0], proj_t)])
    for bit in place.extra:
        large = plus(large, place.dp(large, bit))
    both = plus(both, both_far)
    count = large.shape[0] // 16 * 8
    one = jnp.concatenate([large[:count], both[0]])[None]
    two = jnp.concatenate([large[count:], both[1]])[None]
    one, two, one_far, two_far, small_far, placed = tie(
        one, two, place.dp(one, 4), place.dp(two, 2), small_far, placed
    )
    small = small + small_far
    small_far = [place.tensor(small, bit) for bit in (1, 2, 3)]
    one = ordered(place.d & 4, one, one_far)
    two = ordered(place.d & 2, two, two_far)
    one, two, one_far, two_far, *small_far = tie(one, two, place.dp(one, 2), place.dp(two, 4), *small_far)
    small = small + small_far[0] + small_far[1] + small_far[2]
    bit = 8
    while bit < place.members:
        small = small + place.dp(small, bit)
        bit *= 2
    one = ordered(place.d & 2, one[None], one_far[None]).swapaxes(0, 1)
    two = ordered(place.d & 4, two[None], two_far[None])
    one, two, one_far, two_far = tie(one, two, place.dp(one, 1), place.dp(two, 1))
    rest = large.shape[0] - count
    mine = place.seq == place.core
    first = jnp.where(mine, one[:, :, count:], one_far[:, :, count:])
    second = jnp.where(mine, two[:, :, rest:], two_far[:, :, rest:])
    full = jnp.concatenate([first.swapaxes(0, 1).reshape(-1, width), second.reshape(-1, width)])
    one = ordered(place.d & 1, one[:, :, None, :count], one_far[:, :, None, :count], 2)
    two = ordered(place.d & 1, two[:, :, None, :rest], two_far[:, :, None, :rest], 2)
    return placed, one.reshape(BLOCKS, count, width), two.reshape(BLOCKS, rest, width), full, small


def pack_small(place, small, heads):
    norms, sums, bias, qkv_sums = small
    g_bfc = to_natural(place, bias[0]).reshape(4, -1)
    group = 2 * place.core + place.half
    slots = lax.broadcasted_iota(jnp.int32, (1, 4, 1), 1)
    g_bqv = qkv_sums.reshape(3, 1, heads)
    g_bqv = jnp.where(slots == group, jnp.concatenate([g_bqv[:1], g_bqv[2:]]), 0.0)
    return jnp.concatenate([norms, sums, g_bfc, g_bqv.reshape(2, -1)])


def on_device(members, shards, *arguments):
    (
        tokens, lengths, cotangent, ln1_gain, ln1_shift, w_qkv, b_qv, w_out, b_out,
        ln2_gain, ln2_shift, w_fc, b_fc, w_proj, b_proj,
    ) = arguments
    place = Place(members, shards)
    place.extra = [1 << bit for bit in range(3, members.bit_length() - 1)]
    row_total, width = tokens.shape
    stream = place.place(tokens).astype(F32)
    length = jnp.where(place.seq == place.core, lengths, place.dp(lengths, 1))

    heads = w_qkv.shape[2]
    high, low = split(b_qv)
    biases = jnp.zeros((32, width), BF)
    biases = biases.at[0, : 2 * heads].set(high.reshape(-1)).at[1, : 2 * heads].set(low.reshape(-1))
    shard = jnp.concatenate([w_qkv.transpose(0, 2, 1).reshape(-1, width), biases])
    shard = place.heads_weight(shard)
    b_low = shard[3 * heads :, : 2 * heads].astype(F32)
    b_low = (b_low[0] + b_low[1])[:, None]
    b_qkv = jnp.concatenate([b_low[:heads], jnp.zeros((heads, 1), F32), b_low[heads:]])

    fc_rows = w_fc.T
    units = w_fc.shape[1] // BLOCKS
    biases = jnp.stack(split(b_fc) + (jnp.zeros((width,), BF),) * 6)
    mine = jnp.concatenate([my_piece(place, fc_rows), biases])
    zero = over_tensor(place, mine)
    bias = jnp.concatenate([mine[None], zero])[:, units : units + 2].astype(F32)
    bias = (bias[:, 0] + bias[:, 1]).reshape(4, width)
    bias = jax.vmap(lambda b: own_pieces(place, b), out_axes=1)(bias).reshape(-1)
    fc_far = over_dp(place, zero[:, :units], 2, 4)
    mine = jnp.concatenate([my_piece(place, w_proj), my_piece(place, w_out)])
    far = over_dp(place, over_tensor(place, mine), 4, 2)

    def full(shard, others):
        own = own_pieces(place, shard)
        return jnp.concatenate([own[:, None], others], axis=1).reshape(-1, width)

    def row(value):
        return value[None]

    w = dict(
        vectors=jnp.stack([b_out, ln2_gain, ln2_shift, b_proj, ln1_gain, ln1_shift]),
        ln1_gain=row(ln1_gain), ln2_gain=row(ln2_gain), b_fc=row(bias), qkv=shard[: 3 * heads], b_qkv=b_qkv,
        fc=full(fc_rows, fc_far), proj=full(w_proj, far[:, :, :units]), out=full(w_out, far[:, :, units:]),
    )
    scalars = jnp.concatenate([length, place.quarter[None]])
    normed = normalize(stream, ln1_gain, ln1_shift).astype(BF)
    layer_one, normed, cache_first = layer_forward(place, stream, normed, scalars, w)
    layer_two, _, cache_second = layer_forward(place, layer_one, normed, scalars, w)
    position = place.quarter * row_total + lax.broadcasted_iota(jnp.int32, (row_total, 1), 0)
    gradient = jnp.where(position < length[0], place.place(cotangent).astype(F32), 0.0)
    output = place.unplace(layer_two.astype(BF))
    gradient, low, later, later_small, output = second_backward(place, gradient, scalars, w, cache_second, output)
    placed, one, two, g_qkv, packed = first_backward(
        place, gradient, low, scalars, w, cache_first, later, later_small
    )
    grad_tokens = placed.astype(F32)
    g_qkv = g_qkv.reshape(3, heads, width).transpose(0, 2, 1)
    total = units + w_out.shape[0] // BLOCKS
    split_at = one.shape[1]
    g_fc = one[:, :units].reshape(-1, width)
    g_out = jnp.concatenate([one[:, units:], two[:, : total - split_at]], 1).reshape(-1, width)
    g_proj = two[:, total - split_at :].reshape(-1, width)
    grad_bfc = lax.dynamic_index_in_dim(packed, 6 + place.t, 0, keepdims=False)
    grad_bqv = lax.dynamic_index_in_dim(packed[10:].reshape(2, 4, -1), place.t, 1, keepdims=False)
    return (
        output, grad_tokens, packed[0], packed[1], g_qkv.astype(F32), grad_bqv, g_out.astype(F32),
        packed[2], packed[3], packed[4], g_fc.T.astype(F32), grad_bfc, g_proj.astype(F32), packed[5],
    )


def solution(mesh):
    rows = P(("dp", "tensor"), None)
    placed = (
        rows, P("dp"), rows, P(), P(), P(None, None, "tensor"), P(None, "tensor"),
        P("tensor", None), P(), P(), P(), P(None, "tensor"), P("tensor"), P("tensor", None), P(),
    )
    out_specs = (
        rows, rows, P(), P(), P(None, None, "tensor"), P(None, "tensor"), P("tensor", None),
        P(), P(), P(), P(None, "tensor"), P("tensor"), P("tensor", None), P(),
    )

    def body(*arguments):
        return on_device(mesh.shape["dp"], mesh.shape["tensor"], *arguments)

    return jax.shard_map(body, mesh=mesh, in_specs=placed, out_specs=out_specs, check_vma=False)
```

profile of v0, /device:TPU:0, one launch (start us, length us, event | category | flops | bytes accessed | tf_op | source)
XLA Modules:
  0.0 423.7 jit_solution(2514719915890021642)
XLA Ops:
  2.6 4.1 collective-permute-start.15
  10.3 5.6 %collective-permute-start.5 = (bf16[152,768]{1,0:T(8,128)(2,1)}, bf16[152,768]{1,0:T(8,128)(2,1)}, u32[]{:S(2)}, u32[]{:S(2)}) collective-permute-start(bf16[152,768]{1,0:T(8,128)(2,1)} %fusion.51), channel_id=1, source_target_pairs={{0,2},{1,3},{6,4},{7,5},{8,10},{9,11},{14,12},{15,13},{16,18},{17,... | collective-permute-start | bytes 700424 | tf_op jit(solution)/shard_map/ppermute | solution.py:405
  25.7 2.5 collective-permute-start.16
  29.9 1.9 collective-permute-start.6
  33.2 4.4 %collective-permute-start.3 = (bf16[256,768]{1,0:T(8,128)(2,1)}, bf16[256,768]{1,0:T(8,128)(2,1)}, u32[]{:S(2)}, u32[]{:S(2)}) collective-permute-start(bf16[256,768]{1,0:T(8,128)(2,1)} %add_convert_fusion.2.own_ref), channel_id=1, source_target_pairs={{0,1},{1,0},{2,3},{3,2},{4,5},{5,4},{6,7},{7,6},{8,9},{9,8},{10,11... | collective-permute-start | bytes 1179656 | tf_op jit(solution)/shard_map/ppermute | solution.py:380
  38.6 2.0 maximum_select_fusion.7
  44.6 1.7 collective-permute-done.11
  49.0 1.8 constant_dynamic-update-slice_fusion.4
  50.9 3.8 collective-permute-done.3.far_ref
  57.3 1.9 fusion.26
  59.2 7.0 %collective-permute-done.12 = bf16[3,120,768]{2,1,0:T(8,128)(2,1)S(1)} collective-permute-done((bf16[3,120,768]{2,1,0:T(8,128)(2,1)S(1)}, bf16[3,120,768]{2,1,0:T(8,128)(2,1)S(1)}, u32[]{:S(2)}, u32[]{:S(2)}) %collective-permute-start.12) | collective-permute-done | bytes 552992 | tf_op jit(solution)/shard_map/ppermute | solution.py:377
  70.7 10.5 %attend.2 = (bf16[1024,768]{1,0:T(8,128)(2,1)}, bf16[576,1024]{1,0:T(8,128)(2,1)}, bf16[192,1024]{1,0:T(8,128)(2,1)}, f32[3,1024]{1,0:T(4,128)}) custom-call(s32[2]{0:T(128)} %pad_add_fusion.scalar_ref, bf16[256,768]{1,0:T(8,128)(2,1)} %add_convert_fusion.2.own_ref, bf16[256,768]{1,0:T(8,128)(2,1)} %collective-permute-done.2.near_ref, ...), custom_call_target="tpu_custom_call" | custom-call | flops 2113929216 | bytes 4718592 | tf_op jit(solution)/shard_map/attend/pallas_call | solution.py:113
  82.2 2.5 collective-permute-start.8
  85.6 2.8 collective-permute-done.8
  89.1 2.5 pad_maximum_fusion.3
  93.3 2.1 fusion.71
  101.3 4.6 %maximum_maximum_fusion = bf16[8,4,96,768]{3,2,1,0:T(8,128)(2,1)} fusion(bf16[4,3,96,768]{3,2,1,0:T(8,128)(2,1)} %collective-permute-done.19, bf16[2,3,96,768]{3,2,1,0:T(8,128)(2,1)} %collective-permute-done.18, bf16[1,3,96,768]{3,2,1,0:T(8,128)(2,1)S(1)} %bitcast.276, bf16[1,3,96,768]{3,2,1,0:T(8,128)(2,1)S(1)} %fusion.78, ...), kind=kLoop, calls=%fused_computation.6 | loop fusion | flops 9437184 | bytes 9437184 | tf_op jit(solution)/shard_map/concatenate | solution.py:714
  105.9 1.8 constant_dynamic-update-slice_fusion
  108.1 2.7 pad_maximum_fusion.1
  112.0 11.5 %feed.2 = (f32[256,768]{1,0:T(8,128)}, bf16[256,768]{1,0:T(8,128)(2,1)}, bf16[256,3072]{1,0:T(8,128)(2,1)}, f32[256,3072]{1,0:T(8,128)}, f32[256,768]{1,0:T(8,128)}, /*index=5*/bf16[256,768]{1,0:T(8,128)(2,1)}) custom-call(bf16[768,256]{1,0:T(8,128)(2,1)} %bitcast.292, f32[256,768]{1,0:T(8,128)} %convert_element_type.327.stream_ref, ...), custom_call_target="tpu_custom_call" | custom-call | flops 2415919104 | bytes 14155776 | tf_op jit(solution)/shard_map/feed/pallas_call | solution.py:246
  124.6 10.7 %collective-permute-done.21.far_ref = bf16[256,768]{1,0:T(8,128)(2,1)S(1)} collective-permute-done((bf16[256,768]{1,0:T(8,128)(2,1)}, bf16[256,768]{1,0:T(8,128)(2,1)S(1)}, u32[]{:S(2)}, u32[]{:S(2)}) %collective-permute-start.21) | collective-permute-done | bytes 393248 | tf_op jit(solution)/shard_map/ppermute | solution.py:380
  137.7 10.3 %attend.3 = (bf16[1024,768]{1,0:T(8,128)(2,1)}, bf16[576,1024]{1,0:T(8,128)(2,1)}, bf16[192,1024]{1,0:T(8,128)(2,1)}, f32[3,1024]{1,0:T(4,128)}) custom-call(s32[2]{0:T(128)} %pad_add_fusion.scalar_ref, bf16[256,768]{1,0:T(8,128)(2,1)} %get-tuple-element.141.own_ref, bf16[256,768]{1,0:T(8,128)(2,1)} %copy-done.53, bf16[256,768]{1,0:T(8,128)(2,1)} %copy-done.52, ...), custom_call_target="tpu_custom_call" | custom-call | flops 2113929216 | bytes 4718592 | tf_op jit(solution)/shard_map/attend/pallas_call | solution.py:113
  149.0 3.2 collective-permute-start.24
  153.1 3.5 collective-permute-done.24
  160.2 11.4 %feed.3 = (f32[256,768]{1,0:T(8,128)}, bf16[256,768]{1,0:T(8,128)(2,1)}, bf16[256,3072]{1,0:T(8,128)(2,1)}, f32[256,3072]{1,0:T(8,128)}, f32[256,768]{1,0:T(8,128)}, /*index=5*/bf16[256,768]{1,0:T(8,128)(2,1)}) custom-call(bf16[768,256]{1,0:T(8,128)(2,1)} %bitcast.294, f32[256,768]{1,0:T(8,128)} %get-tuple-element.144.stream_ref, ...), custom_call_target="tpu_custom_call" | custom-call | flops 2415919104 | bytes 14155776 | tf_op jit(solution)/shard_map/feed/pallas_call | solution.py:246
  171.6 10.8 %feed_back.2 = (bf16[256,3072]{1,0:T(8,128)(2,1)}, f32[1,3072]{1,0:T(1,128)}, f32[256,768]{1,0:T(8,128)}, bf16[256,768]{1,0:T(8,128)(2,1)}, bf16[768,256]{1,0:T(8,128)(2,1)}, /*index=5*/f32[4,768]{1,0:T(4,128)}) custom-call(f32[256,768]{1,0:T(8,128)} %get-tuple-element.331.grad_ref, f32[256,3072]{1,0:T(8,128)} %get-tuple-element.145.slope_ref, ...), custom_call_target="tpu_custom_call" | custom-call | flops 2415919104 | bytes 14155776 | tf_op jit(solution)/shard_map/feed_back/pallas_call | solution.py:310
  185.4 2.0 collective-permute-start.27
  187.3 5.4 %collective-permute-done.27 = bf16[192,512]{1,0:T(8,128)(2,1)S(1)} collective-permute-done((bf16[192,512]{1,0:T(8,128)(2,1)S(1)}, bf16[192,512]{1,0:T(8,128)(2,1)S(1)}, u32[]{:S(2)}, u32[]{:S(2)}) %collective-permute-start.27) | collective-permute-done | bytes 196640 | tf_op jit(solution)/shard_map/ppermute | solution.py:380
  193.6 12.5 %attend_back.2 = (bf16[576,1024]{1,0:T(8,128)(2,1)}, f32[576,1]{1,0:T(8,128)}, bf16[1024,768]{1,0:T(8,128)(2,1)}) custom-call(s32[2]{0:T(128)} %pad_add_fusion.scalar_ref, bf16[576,1024]{1,0:T(8,128)(2,1)} %get-tuple-element.142.qkv_ref, bf16[192,1024]{1,0:T(8,128)(2,1)} %pad_maximum_fusion.15.grad_ref, f32[3,1024]{1,0:T(4,128)} %get-tuple-element.148.lse_ref, ...), custom_call_target="tpu_custom_call" | custom-call | flops 3321888768 | bytes 5898240 | tf_op jit(solution)/shard_map/attend_back/pallas_call | solution.py:190
  207.6 1.7 collective-permute-start.30
  210.8 3.6 collective-permute-start.29
  214.4 13.0 %collective-permute-done.29.far_ref = bf16[256,768]{1,0:T(8,128)(2,1)S(1)} collective-permute-done((bf16[256,768]{1,0:T(8,128)(2,1)S(1)}, bf16[256,768]{1,0:T(8,128)(2,1)S(1)}, u32[]{:S(2)}, u32[]{:S(2)}) %collective-permute-start.29) | collective-permute-done | bytes 393248 | tf_op jit(solution)/shard_map/ppermute | solution.py:380
  228.2 3.3 norm_back.2
  231.5 4.1 convolution_convert_fusion.1
  235.8 2.0 copy-done.3
  238.6 10.8 %feed_back.3 = (bf16[256,3072]{1,0:T(8,128)(2,1)}, f32[1,3072]{1,0:T(1,128)}, f32[256,768]{1,0:T(8,128)}, bf16[256,768]{1,0:T(8,128)(2,1)}, bf16[768,256]{1,0:T(8,128)(2,1)}, /*index=5*/f32[4,768]{1,0:T(4,128)}) custom-call(f32[256,768]{1,0:T(8,128)} %get-tuple-element.158.grad_ref, f32[256,3072]{1,0:T(8,128)} %get-tuple-element.159.slope_ref, ...), custom_call_target="tpu_custom_call" | custom-call | flops 2415919104 | bytes 14155776 | tf_op jit(solution)/shard_map/feed_back/pallas_call | solution.py:310
  250.4 2.0 convolution_convert_fusion.2
  252.6 2.9 convolution_convert_fusion
  255.5 1.8 fusion.10
  259.7 3.1 add_convert_fusion.1
  272.2 2.8 pad_maximum_fusion
  275.0 4.5 %collective-permute-done.34 = bf16[192,512]{1,0:T(8,128)(2,1)S(1)} collective-permute-done((bf16[192,512]{1,0:T(8,128)(2,1)S(1)}, bf16[192,512]{1,0:T(8,128)(2,1)S(1)}, u32[]{:S(2)}, u32[]{:S(2)}) %collective-permute-start.34) | collective-permute-done | bytes 196640 | tf_op jit(solution)/shard_map/ppermute | solution.py:380
  285.2 2.7 add_convert_fusion
  287.8 2.7 collective-permute-done.37
  296.8 12.8 %attend_back.3 = (bf16[576,1024]{1,0:T(8,128)(2,1)}, f32[576,1]{1,0:T(8,128)}, bf16[1024,768]{1,0:T(8,128)(2,1)}) custom-call(s32[2]{0:T(128)} %pad_add_fusion.scalar_ref, bf16[576,1024]{1,0:T(8,128)(2,1)} %get-tuple-element.152.qkv_ref, bf16[192,1024]{1,0:T(8,128)(2,1)} %pad_maximum_fusion.16.grad_ref, f32[3,1024]{1,0:T(4,128)} %get-tuple-element.179.lse_ref, ...), custom_call_target="tpu_custom_call" | custom-call | flops 3321888768 | bytes 5898240 | tf_op jit(solution)/shard_map/attend_back/pallas_call | solution.py:190
  318.8 2.0 fusion.16
  321.5 6.0 %collective-permute-done.43 = bf16[2,120,768]{2,1,0:T(8,128)(2,1)S(1)} collective-permute-done((bf16[2,120,768]{2,1,0:T(8,128)(2,1)S(1)}, bf16[2,120,768]{2,1,0:T(8,128)(2,1)S(1)}, u32[]{:S(2)}, u32[]{:S(2)}) %collective-permute-start.43) | collective-permute-done | bytes 368672 | tf_op jit(solution)/shard_map/ppermute | solution.py:377
  332.1 4.6 %collective-permute-done.46 = bf16[2,72,768]{2,1,0:T(8,128)(2,1)S(1)} collective-permute-done((bf16[2,72,768]{2,1,0:T(8,128)(2,1)S(1)}, bf16[2,72,768]{2,1,0:T(8,128)(2,1)S(1)}, u32[]{:S(2)}, u32[]{:S(2)}) %collective-permute-start.46) | collective-permute-done | bytes 221216 | tf_op jit(solution)/shard_map/ppermute | solution.py:377
  337.1 2.0 collective-permute-done.45.far_ref
  342.1 3.3 norm_back.3
  348.1 10.4 %collective-permute-done.50 = bf16[96,768]{1,0:T(8,128)(2,1)S(1)} collective-permute-done((bf16[96,768]{1,0:T(8,128)(2,1)S(1)}, bf16[96,768]{1,0:T(8,128)(2,1)S(1)}, u32[]{:S(2)}, u32[]{:S(2)}) %collective-permute-start.50) | collective-permute-done | bytes 147488 | tf_op jit(solution)/shard_map/ppermute | solution.py:380
  358.6 1.8 collective-permute-done.49
  361.9 3.6 collective-permute-start.53
  366.9 2.8 collective-permute-done.55
  369.6 11.9 %collective-permute-done.53 = bf16[120,768]{1,0:T(8,128)(2,1)S(1)} collective-permute-done((bf16[120,768]{1,0:T(8,128)(2,1)S(1)}, bf16[120,768]{1,0:T(8,128)(2,1)S(1)}, u32[]{:S(2)}, u32[]{:S(2)}) %collective-permute-start.53) | collective-permute-done | bytes 184352 | tf_op jit(solution)/shard_map/ppermute | solution.py:380
  384.6 5.0 %collective-permute-done.58 = f32[12,768]{1,0:T(8,128)S(1)} collective-permute-done((f32[12,768]{1,0:T(8,128)S(1)}, f32[12,768]{1,0:T(8,128)S(1)}, u32[]{:S(2)}, u32[]{:S(2)}) %collective-permute-start.58) | collective-permute-done | bytes 36896 | tf_op jit(solution)/shard_map/ppermute | solution.py:377
  393.2 3.7 collective-permute-start.64
  397.8 1.8 collective-permute-done.64
  399.6 3.6 collective-permute-done.60
  404.2 1.9 convert_element_type.425
  412.1 2.2 slice_select_fusion
  414.5 2.0 copy.153
  418.4 1.7 bitcast_convert_fusion
  421.5 1.8 copy.182
  (424 shorter events, 126.5 us)
Async XLA Ops:
  2.6 23.1 %collective-permute-start.15 = (bf16[104,768]{1,0:T(8,128)(2,1)S(1)}, bf16[104,768]{1,0:T(8,128)(2,1)S(1)}, u32[]{:S(2)}, u32[]{:S(2)}) collective-permute-start(bf16[104,768]{1,0:T(8,128)(2,1)S(1)} %concatenate.188), channel_id=1, source_target_pairs={{0,2},{1,3},{2,0},{3,1},{4,6},{5,7},{6,4},{7,5},{8,10},{9,11},{10,... | collective-permute-start | bytes 479240 | tf_op jit(solution)/shard_map/ppermute | solution.py:380
  9.1 20.7 %collective-permute-start.10 = (bf16[120,768]{1,0:T(8,128)(2,1)}, bf16[120,768]{1,0:T(8,128)(2,1)S(1)}, u32[]{:S(2)}, u32[]{:S(2)}) collective-permute-start(bf16[120,768]{1,0:T(8,128)(2,1)} %get-tuple-element.351), channel_id=1, source_target_pairs={{0,2},{1,3},{2,0},{3,1},{4,6},{5,7},{6,4},{7,5},{8,10},{9,11},{10,... | collective-permute-start | bytes 552968 | tf_op jit(solution)/shard_map/ppermute | solution.py:380
  10.3 19.6 %collective-permute-start.5 = (bf16[152,768]{1,0:T(8,128)(2,1)}, bf16[152,768]{1,0:T(8,128)(2,1)}, u32[]{:S(2)}, u32[]{:S(2)}) collective-permute-start(bf16[152,768]{1,0:T(8,128)(2,1)} %fusion.51), channel_id=1, source_target_pairs={{0,2},{1,3},{6,4},{7,5},{8,10},{9,11},{14,12},{15,13},{16,18},{17,... | collective-permute-start | bytes 700424 | tf_op jit(solution)/shard_map/ppermute | solution.py:405
  16.0 8.5 %collective-permute-start = (s32[1]{0:T(128)}, s32[1]{0:T(128)}, u32[]{:S(2)}, u32[]{:S(2)}) collective-permute-start(s32[1]{0:T(128)} %param.20), channel_id=1, source_target_pairs={{0,4},{4,0},{8,12},{12,8},{16,20},{20,16},{24,28},{28,24},{1,5},{5... | collective-permute-start | bytes 20 | tf_op jit(solution)/shard_map/ppermute | solution.py:377
  16.0 15.9 %collective-permute-start.1 = (bf16[256,768]{1,0:T(8,128)(2,1)}, bf16[256,768]{1,0:T(8,128)(2,1)S(1)}, u32[]{:S(2)}, u32[]{:S(2)}) collective-permute-start(bf16[256,768]{1,0:T(8,128)(2,1)} %param.19), channel_id=1, source_target_pairs={{0,0},{1,4},{2,1},{3,5},{4,2},{5,6},{6,3},{7,7},{8,8},{9,12},{10,9... | collective-permute-start | bytes 1179656 | tf_op jit(solution)/shard_map/ppermute | solution.py:391
  25.7 16.4 %collective-permute-start.16 = (bf16[2,104,768]{2,1,0:T(8,128)(2,1)S(1)}, bf16[2,104,768]{2,1,0:T(8,128)(2,1)S(1)}, u32[]{:S(2)}, u32[]{:S(2)}) collective-permute-start(bf16[2,104,768]{2,1,0:T(8,128)(2,1)S(1)} %pad_maximum_fusion.18), channel_id=1, source_target_pairs={{0,1},{1,0},{2,3},{3,2},{4,5},{5,4},{6,7},{7,6},{8,9},{9,8},{10,11... | collective-permute-start | bytes 958472 | tf_op jit(solution)/shard_map/ppermute | solution.py:380
  29.8 16.5 %collective-permute-start.11 = (bf16[2,120,768]{2,1,0:T(8,128)(2,1)S(1)}, bf16[2,120,768]{2,1,0:T(8,128)(2,1)}, u32[]{:S(2)}, u32[]{:S(2)}) collective-permute-start(bf16[2,120,768]{2,1,0:T(8,128)(2,1)S(1)} %pad_maximum_fusion.17), channel_id=1, source_target_pairs={{0,1},{1,0},{2,3},{3,2},{4,5},{5,4},{6,7},{7,6},{8,9},{9,8},{10,11... | collective-permute-start | bytes 1105928 | tf_op jit(solution)/shard_map/ppermute | solution.py:380
  29.9 8.7 %collective-permute-start.6 = (bf16[152,768]{1,0:T(8,128)(2,1)}, bf16[152,768]{1,0:T(8,128)(2,1)S(1)}, u32[]{:S(2)}, u32[]{:S(2)}) collective-permute-start(bf16[152,768]{1,0:T(8,128)(2,1)} %collective-permute-done.5), channel_id=1, source_target_pairs={{0,8},{4,12},{8,0},{12,4},{16,24},{20,28},{24,16},{28,20},{1,9},{5... | collective-permute-start | bytes 700424 | tf_op jit(solution)/shard_map/ppermute | solution.py:377
  33.2 21.4 %collective-permute-start.3 = (bf16[256,768]{1,0:T(8,128)(2,1)}, bf16[256,768]{1,0:T(8,128)(2,1)}, u32[]{:S(2)}, u32[]{:S(2)}) collective-permute-start(bf16[256,768]{1,0:T(8,128)(2,1)} %add_convert_fusion.2.own_ref), channel_id=1, source_target_pairs={{0,1},{1,0},{2,3},{3,2},{4,5},{5,4},{6,7},{7,6},{8,9},{9,8},{10,11... | collective-permute-start | bytes 1179656 | tf_op jit(solution)/shard_map/ppermute | solution.py:380
  37.7 33.0 %collective-permute-start.2 = (bf16[256,768]{1,0:T(8,128)(2,1)}, bf16[256,768]{1,0:T(8,128)(2,1)}, u32[]{:S(2)}, u32[]{:S(2)}) collective-permute-start(bf16[256,768]{1,0:T(8,128)(2,1)} %add_convert_fusion.2.own_ref), channel_id=1, source_target_pairs={{0,4},{4,0},{8,12},{12,8},{16,20},{20,16},{24,28},{28,24},{1,5},{5... | collective-permute-start | bytes 1179656 | tf_op jit(solution)/shard_map/ppermute | solution.py:377
  40.6 16.7 %collective-permute-start.7 = (bf16[304,768]{1,0:T(8,128)(2,1)}, bf16[304,768]{1,0:T(8,128)(2,1)}, u32[]{:S(2)}, u32[]{:S(2)}) collective-permute-start(bf16[304,768]{1,0:T(8,128)(2,1)} %maximum_select_fusion.7), channel_id=1, source_target_pairs={{0,16},{4,20},{8,24},{12,28},{16,0},{20,4},{24,8},{28,12},{1,17},{... | collective-permute-start | bytes 1400840 | tf_op jit(solution)/shard_map/ppermute | solution.py:377
  42.9 12.7 %collective-permute-start.17 = (bf16[3,96,768]{2,1,0:T(8,128)(2,1)}, bf16[3,96,768]{2,1,0:T(8,128)(2,1)S(1)}, u32[]{:S(2)}, u32[]{:S(2)}) collective-permute-start(bf16[3,96,768]{2,1,0:T(8,128)(2,1)} %pad_maximum_fusion.12), channel_id=1, source_target_pairs={{0,8},{4,12},{8,0},{12,4},{16,24},{20,28},{24,16},{28,20},{1,9},{5... | collective-permute-start | bytes 1327112 | tf_op jit(solution)/shard_map/ppermute | solution.py:377
  47.4 18.8 %collective-permute-start.12 = (bf16[3,120,768]{2,1,0:T(8,128)(2,1)S(1)}, bf16[3,120,768]{2,1,0:T(8,128)(2,1)S(1)}, u32[]{:S(2)}, u32[]{:S(2)}) collective-permute-start(bf16[3,120,768]{2,1,0:T(8,128)(2,1)S(1)} %get-tuple-element.329), channel_id=1, source_target_pairs={{0,16},{4,20},{8,24},{12,28},{16,0},{20,4},{24,8},{28,12},{1,17},{... | collective-permute-start | bytes 1658888 | tf_op jit(solution)/shard_map/ppermute | solution.py:377
  54.7 16.0 %collective-permute-start.4 = (bf16[256,768]{1,0:T(8,128)(2,1)}, bf16[256,768]{1,0:T(8,128)(2,1)}, u32[]{:S(2)}, u32[]{:S(2)}) collective-permute-start(bf16[256,768]{1,0:T(8,128)(2,1)} %collective-permute-done.3.far_ref), channel_id=1, source_target_pairs={{0,4},{4,0},{8,12},{12,8},{16,20},{20,16},{24,28},{28,24},{1,5},{5... | collective-permute-start | bytes 1179656 | tf_op jit(solution)/shard_map/ppermute | solution.py:377
  56.6 32.5 %collective-permute-start.18 = (bf16[2,3,96,768]{3,2,1,0:T(8,128)(2,1)}, bf16[2,3,96,768]{3,2,1,0:T(8,128)(2,1)}, u32[]{:S(2)}, u32[]{:S(2)}) collective-permute-start(bf16[2,3,96,768]{3,2,1,0:T(8,128)(2,1)} %pad_maximum_fusion.7), channel_id=1, source_target_pairs={{0,16},{4,20},{8,24},{12,28},{16,0},{20,4},{24,8},{28,12},{1,17},{... | collective-permute-start | bytes 2654216 | tf_op jit(solution)/shard_map/ppermute | solution.py:377
  67.3 26.0 %collective-permute-start.13 = (bf16[2,3,120,768]{3,2,1,0:T(8,128)(2,1)}, bf16[2,3,120,768]{3,2,1,0:T(8,128)(2,1)}, u32[]{:S(2)}, u32[]{:S(2)}) collective-permute-start(bf16[2,3,120,768]{3,2,1,0:T(8,128)(2,1)} %pad_maximum_fusion.6), channel_id=1, source_target_pairs={{0,8},{4,12},{8,0},{12,4},{16,24},{20,28},{24,16},{28,20},{1,9},{5... | collective-permute-start | bytes 3317768 | tf_op jit(solution)/shard_map/ppermute | solution.py:377
  82.2 6.3 %collective-permute-start.8 = (bf16[192,512]{1,0:T(8,128)(2,1)S(1)}, bf16[192,512]{1,0:T(8,128)(2,1)S(1)}, u32[]{:S(2)}, u32[]{:S(2)}) collective-permute-start(bf16[192,512]{1,0:T(8,128)(2,1)S(1)} %slice.416), channel_id=1, source_target_pairs={{0,1},{1,0},{2,3},{3,2},{4,5},{5,4},{6,7},{7,6},{8,9},{9,8},{10,11... | collective-permute-start | bytes 589832 | tf_op jit(solution)/shard_map/ppermute | solution.py:380
  89.1 8.7 %collective-permute-start.9 = (bf16[384,256]{1,0:T(8,128)(2,1)}, bf16[384,256]{1,0:T(8,128)(2,1)}, u32[]{:S(2)}, u32[]{:S(2)}) collective-permute-start(bf16[384,256]{1,0:T(8,128)(2,1)} %pad_maximum_fusion.24), channel_id=1, source_target_pairs={{0,4},{4,0},{8,12},{12,8},{16,20},{20,16},{24,28},{28,24},{1,5},{5... | collective-permute-start | bytes 589832 | tf_op jit(solution)/shard_map/ppermute | solution.py:377
  91.7 9.6 %collective-permute-start.19 = (bf16[4,3,96,768]{3,2,1,0:T(8,128)(2,1)}, bf16[4,3,96,768]{3,2,1,0:T(8,128)(2,1)}, u32[]{:S(2)}, u32[]{:S(2)}) collective-permute-start(bf16[4,3,96,768]{3,2,1,0:T(8,128)(2,1)} %pad_maximum_fusion.3), channel_id=1, source_target_pairs={{0,4},{4,0},{8,12},{12,8},{16,20},{20,16},{24,28},{28,24},{1,5},{5... | collective-permute-start | bytes 5308424 | tf_op jit(solution)/shard_map/ppermute | solution.py:377
  97.1 8.8 %collective-permute-start.14 = (bf16[4,3,120,768]{3,2,1,0:T(8,128)(2,1)}, bf16[4,3,120,768]{3,2,1,0:T(8,128)(2,1)}, u32[]{:S(2)}, u32[]{:S(2)}) collective-permute-start(bf16[4,3,120,768]{3,2,1,0:T(8,128)(2,1)} %pad_maximum_fusion.2), channel_id=1, source_target_pairs={{0,4},{4,0},{8,12},{12,8},{16,20},{20,16},{24,28},{28,24},{1,5},{5... | collective-permute-start | bytes 6635528 | tf_op jit(solution)/shard_map/ppermute | solution.py:377
  123.4 11.8 %collective-permute-start.21 = (bf16[256,768]{1,0:T(8,128)(2,1)}, bf16[256,768]{1,0:T(8,128)(2,1)S(1)}, u32[]{:S(2)}, u32[]{:S(2)}) collective-permute-start(bf16[256,768]{1,0:T(8,128)(2,1)} %get-tuple-element.141.own_ref), channel_id=1, source_target_pairs={{0,1},{1,0},{2,3},{3,2},{4,5},{5,4},{6,7},{7,6},{8,9},{9,8},{10,11... | collective-permute-start | bytes 1179656 | tf_op jit(solution)/shard_map/ppermute | solution.py:380
  124.4 11.6 %collective-permute-start.20 = (bf16[256,768]{1,0:T(8,128)(2,1)}, bf16[256,768]{1,0:T(8,128)(2,1)S(1)}, u32[]{:S(2)}, u32[]{:S(2)}) collective-permute-start(bf16[256,768]{1,0:T(8,128)(2,1)} %get-tuple-element.141.own_ref), channel_id=1, source_target_pairs={{0,4},{4,0},{8,12},{12,8},{16,20},{20,16},{24,28},{28,24},{1,5},{5... | collective-permute-start | bytes 1179656 | tf_op jit(solution)/shard_map/ppermute | solution.py:377
  135.3 22.7 %collective-permute-start.23 = (bf16[256,768]{1,0:T(8,128)(2,1)S(1)}, bf16[256,768]{1,0:T(8,128)(2,1)S(1)}, u32[]{:S(2)}, u32[]{:S(2)}) collective-permute-start(bf16[256,768]{1,0:T(8,128)(2,1)S(1)} %copy-done.48), channel_id=1, source_target_pairs={{0,0},{1,4},{2,1},{3,5},{4,2},{5,6},{6,3},{7,7},{8,8},{9,12},{10,9... | collective-permute-start | bytes 1179656 | tf_op jit(solution)/shard_map/ppermute | solution.py:391
  149.0 7.6 %collective-permute-start.24 = (bf16[192,512]{1,0:T(8,128)(2,1)S(1)}, bf16[192,512]{1,0:T(8,128)(2,1)S(1)}, u32[]{:S(2)}, u32[]{:S(2)}) collective-permute-start(bf16[192,512]{1,0:T(8,128)(2,1)S(1)} %slice.429), channel_id=1, source_target_pairs={{0,1},{1,0},{2,3},{3,2},{4,5},{5,4},{6,7},{7,6},{8,9},{9,8},{10,11... | collective-permute-start | bytes 589832 | tf_op jit(solution)/shard_map/ppermute | solution.py:380
  156.6 2.4 collective-permute-start.25
  185.4 7.4 %collective-permute-start.27 = (bf16[192,512]{1,0:T(8,128)(2,1)S(1)}, bf16[192,512]{1,0:T(8,128)(2,1)S(1)}, u32[]{:S(2)}, u32[]{:S(2)}) collective-permute-start(bf16[192,512]{1,0:T(8,128)(2,1)S(1)} %get-tuple-element.337), channel_id=1, source_target_pairs={{0,1},{1,0},{2,3},{3,2},{4,5},{5,4},{6,7},{7,6},{8,9},{9,8},{10,11... | collective-permute-start | bytes 589832 | tf_op jit(solution)/shard_map/ppermute | solution.py:380
  207.4 2.4 collective-permute-start.28
  207.6 6.9 %collective-permute-start.30 = (bf16[256,768]{1,0:T(8,128)(2,1)S(1)}, bf16[256,768]{1,0:T(8,128)(2,1)}, u32[]{:S(2)}, u32[]{:S(2)}) collective-permute-start(bf16[256,768]{1,0:T(8,128)(2,1)S(1)} %convert_element_type.340), channel_id=1, source_target_pairs={{0,0},{4,1},{1,2},{5,3},{2,4},{6,5},{3,6},{7,7},{8,8},{12,9},{9,10... | collective-permute-start | bytes 1179656 | tf_op jit(solution)/shard_map/ppermute | solution.py:394
  210.8 16.6 %collective-permute-start.29 = (bf16[256,768]{1,0:T(8,128)(2,1)S(1)}, bf16[256,768]{1,0:T(8,128)(2,1)S(1)}, u32[]{:S(2)}, u32[]{:S(2)}) collective-permute-start(bf16[256,768]{1,0:T(8,128)(2,1)S(1)} %get-tuple-element.312), channel_id=1, source_target_pairs={{0,1},{1,0},{2,3},{3,2},{4,5},{5,4},{6,7},{7,6},{8,9},{9,8},{10,11... | collective-permute-start | bytes 1179656 | tf_op jit(solution)/shard_map/ppermute | solution.py:380
  237.8 12.5 %collective-permute-start.31 = (bf16[4,4,96,768]{3,2,1,0:T(8,128)(2,1)S(1)}, bf16[4,4,96,768]{3,2,1,0:T(8,128)(2,1)}, u32[]{:S(2)}, u32[]{:S(2)}) collective-permute-start(bf16[4,4,96,768]{3,2,1,0:T(8,128)(2,1)S(1)} %bitcast.284), channel_id=1, source_target_pairs={{0,4},{4,0},{8,12},{12,8},{16,20},{20,16},{24,28},{28,24},{1,5},{5... | collective-permute-start | bytes 7077896 | tf_op jit(solution)/shard_map/ppermute | solution.py:377
  258.6 22.4 %collective-permute-start.32 = (bf16[4,4,120,768]{3,2,1,0:T(8,128)(2,1)}, bf16[4,4,120,768]{3,2,1,0:T(8,128)(2,1)}, u32[]{:S(2)}, u32[]{:S(2)}) collective-permute-start(bf16[4,4,120,768]{3,2,1,0:T(8,128)(2,1)} %fusion.10), channel_id=1, source_target_pairs={{0,4},{4,0},{8,12},{12,8},{16,20},{20,16},{24,28},{28,24},{1,5},{5... | collective-permute-start | bytes 8847368 | tf_op jit(solution)/shard_map/ppermute | solution.py:377
  263.7 16.6 %collective-permute-start.35 = (bf16[2,2,96,768]{3,2,1,0:T(8,128)(2,1)}, bf16[2,2,96,768]{3,2,1,0:T(8,128)(2,1)}, u32[]{:S(2)}, u32[]{:S(2)}) collective-permute-start(bf16[2,2,96,768]{3,2,1,0:T(8,128)(2,1)} %slice_bitcast_fusion.10), channel_id=1, source_target_pairs={{0,8},{4,12},{8,0},{12,4},{16,24},{20,28},{24,16},{28,20},{1,9},{5... | collective-permute-start | bytes 1769480 | tf_op jit(solution)/shard_map/ppermute | solution.py:377
  265.6 15.4 %collective-permute-start.36 = (bf16[2,2,96,768]{3,2,1,0:T(8,128)(2,1)}, bf16[2,2,96,768]{3,2,1,0:T(8,128)(2,1)}, u32[]{:S(2)}, u32[]{:S(2)}) collective-permute-start(bf16[2,2,96,768]{3,2,1,0:T(8,128)(2,1)} %slice_bitcast_fusion.9), channel_id=1, source_target_pairs={{0,16},{4,20},{8,24},{12,28},{16,0},{20,4},{24,8},{28,12},{1,17},{... | collective-permute-start | bytes 1769480 | tf_op jit(solution)/shard_map/ppermute | solution.py:377
  268.2 2.8 collective-permute-start.33
  272.1 7.4 %collective-permute-start.34 = (bf16[192,512]{1,0:T(8,128)(2,1)S(1)}, bf16[192,512]{1,0:T(8,128)(2,1)S(1)}, u32[]{:S(2)}, u32[]{:S(2)}) collective-permute-start(bf16[192,512]{1,0:T(8,128)(2,1)S(1)} %get-tuple-element.333), channel_id=1, source_target_pairs={{0,1},{1,0},{2,3},{3,2},{4,5},{5,4},{6,7},{7,6},{8,9},{9,8},{10,11... | collective-permute-start | bytes 589832 | tf_op jit(solution)/shard_map/ppermute | solution.py:380
  282.5 8.0 %collective-permute-start.37 = (bf16[2,96,768]{2,1,0:T(8,128)(2,1)S(1)}, bf16[2,96,768]{2,1,0:T(8,128)(2,1)S(1)}, u32[]{:S(2)}, u32[]{:S(2)}) collective-permute-start(bf16[2,96,768]{2,1,0:T(8,128)(2,1)S(1)} %get-tuple-element.326), channel_id=1, source_target_pairs={{0,16},{4,20},{8,24},{12,28},{16,0},{20,4},{24,8},{28,12},{1,17},{... | collective-permute-start | bytes 884744 | tf_op jit(solution)/shard_map/ppermute | solution.py:377
  284.2 7.7 %collective-permute-start.38 = (bf16[2,96,768]{2,1,0:T(8,128)(2,1)S(1)}, bf16[2,96,768]{2,1,0:T(8,128)(2,1)S(1)}, u32[]{:S(2)}, u32[]{:S(2)}) collective-permute-start(bf16[2,96,768]{2,1,0:T(8,128)(2,1)S(1)} %get-tuple-element.324), channel_id=1, source_target_pairs={{0,8},{4,12},{8,0},{12,4},{16,24},{20,28},{24,16},{28,20},{1,9},{5... | collective-permute-start | bytes 884744 | tf_op jit(solution)/shard_map/ppermute | solution.py:377
  294.6 16.3 %collective-permute-start.39 = (bf16[2,96,768]{2,1,0:T(8,128)(2,1)}, bf16[2,96,768]{2,1,0:T(8,128)(2,1)}, u32[]{:S(2)}, u32[]{:S(2)}) collective-permute-start(bf16[2,96,768]{2,1,0:T(8,128)(2,1)} %add_convert_fusion.6), channel_id=1, source_target_pairs={{0,1},{1,0},{2,3},{3,2},{4,5},{5,4},{6,7},{7,6},{8,9},{9,8},{10,11... | collective-permute-start | bytes 884744 | tf_op jit(solution)/shard_map/ppermute | solution.py:380
  294.9 16.6 %collective-permute-start.40 = (bf16[2,2,120,768]{3,2,1,0:T(8,128)(2,1)}, bf16[2,2,120,768]{3,2,1,0:T(8,128)(2,1)}, u32[]{:S(2)}, u32[]{:S(2)}) collective-permute-start(bf16[2,2,120,768]{3,2,1,0:T(8,128)(2,1)} %slice_bitcast_fusion.2), channel_id=1, source_target_pairs={{0,8},{4,12},{8,0},{12,4},{16,24},{20,28},{24,16},{28,20},{1,9},{5... | collective-permute-start | bytes 2211848 | tf_op jit(solution)/shard_map/ppermute | solution.py:377
  295.4 16.8 %collective-permute-start.41 = (bf16[2,2,120,768]{3,2,1,0:T(8,128)(2,1)}, bf16[2,2,120,768]{3,2,1,0:T(8,128)(2,1)}, u32[]{:S(2)}, u32[]{:S(2)}) collective-permute-start(bf16[2,2,120,768]{3,2,1,0:T(8,128)(2,1)} %slice_bitcast_fusion.1), channel_id=1, source_target_pairs={{0,16},{4,20},{8,24},{12,28},{16,0},{20,4},{24,8},{28,12},{1,17},{... | collective-permute-start | bytes 2211848 | tf_op jit(solution)/shard_map/ppermute | solution.py:377
  313.6 7.8 %collective-permute-start.44 = (bf16[2,120,768]{2,1,0:T(8,128)(2,1)S(1)}, bf16[2,120,768]{2,1,0:T(8,128)(2,1)S(1)}, u32[]{:S(2)}, u32[]{:S(2)}) collective-permute-start(bf16[2,120,768]{2,1,0:T(8,128)(2,1)S(1)} %slice_bitcast_fusion.19), channel_id=1, source_target_pairs={{0,8},{4,12},{8,0},{12,4},{16,24},{20,28},{24,16},{28,20},{1,9},{5... | collective-permute-start | bytes 1105928 | tf_op jit(solution)/shard_map/ppermute | solution.py:377
  316.3 11.2 %collective-permute-start.42 = (bf16[2,256,768]{2,1,0:T(8,128)(2,1)S(1)}, bf16[2,256,768]{2,1,0:T(8,128)(2,1)S(1)}, u32[]{:S(2)}, u32[]{:S(2)}) collective-permute-start(bf16[2,256,768]{2,1,0:T(8,128)(2,1)S(1)} %pad_maximum_fusion.10), channel_id=1, source_target_pairs={{0,4},{4,0},{8,12},{12,8},{16,20},{20,16},{24,28},{28,24},{1,5},{5... | collective-permute-start | bytes 2359304 | tf_op jit(solution)/shard_map/ppermute | solution.py:377
  316.4 11.0 %collective-permute-start.43 = (bf16[2,120,768]{2,1,0:T(8,128)(2,1)S(1)}, bf16[2,120,768]{2,1,0:T(8,128)(2,1)S(1)}, u32[]{:S(2)}, u32[]{:S(2)}) collective-permute-start(bf16[2,120,768]{2,1,0:T(8,128)(2,1)S(1)} %slice_bitcast_fusion.20), channel_id=1, source_target_pairs={{0,16},{4,20},{8,24},{12,28},{16,0},{20,4},{24,8},{28,12},{1,17},{... | collective-permute-start | bytes 1105928 | tf_op jit(solution)/shard_map/ppermute | solution.py:377
  328.5 10.7 %collective-permute-start.45 = (bf16[256,768]{1,0:T(8,128)(2,1)S(1)}, bf16[256,768]{1,0:T(8,128)(2,1)S(1)}, u32[]{:S(2)}, u32[]{:S(2)}) collective-permute-start(bf16[256,768]{1,0:T(8,128)(2,1)S(1)} %get-tuple-element.307), channel_id=1, source_target_pairs={{0,1},{1,0},{2,3},{3,2},{4,5},{5,4},{6,7},{7,6},{8,9},{9,8},{10,11... | collective-permute-start | bytes 1179656 | tf_op jit(solution)/shard_map/ppermute | solution.py:380
  329.9 6.8 %collective-permute-start.46 = (bf16[2,72,768]{2,1,0:T(8,128)(2,1)S(1)}, bf16[2,72,768]{2,1,0:T(8,128)(2,1)S(1)}, u32[]{:S(2)}, u32[]{:S(2)}) collective-permute-start(bf16[2,72,768]{2,1,0:T(8,128)(2,1)S(1)} %bitcast.314), channel_id=1, source_target_pairs={{0,8},{4,12},{8,0},{12,4},{16,24},{20,28},{24,16},{28,20},{1,9},{5... | collective-permute-start | bytes 663560 | tf_op jit(solution)/shard_map/ppermute | solution.py:377
  330.7 6.4 %collective-permute-start.47 = (bf16[2,72,768]{2,1,0:T(8,128)(2,1)S(1)}, bf16[2,72,768]{2,1,0:T(8,128)(2,1)S(1)}, u32[]{:S(2)}, u32[]{:S(2)}) collective-permute-start(bf16[2,72,768]{2,1,0:T(8,128)(2,1)S(1)} %bitcast.313), channel_id=1, source_target_pairs={{0,16},{4,20},{8,24},{12,28},{16,0},{20,4},{24,8},{28,12},{1,17},{... | collective-permute-start | bytes 663560 | tf_op jit(solution)/shard_map/ppermute | solution.py:377
  339.2 8.9 %collective-permute-start.52 = (bf16[72,768]{1,0:T(8,128)(2,1)S(1)}, bf16[72,768]{1,0:T(8,128)(2,1)S(1)}, u32[]{:S(2)}, u32[]{:S(2)}) collective-permute-start(bf16[72,768]{1,0:T(8,128)(2,1)S(1)} %select_bitcast_fusion.1), channel_id=1, source_target_pairs={{0,8},{4,12},{8,0},{12,4},{16,24},{20,28},{24,16},{28,20},{1,9},{5... | collective-permute-start | bytes 331784 | tf_op jit(solution)/shard_map/ppermute | solution.py:377
  340.4 7.7 %collective-permute-start.51 = (bf16[72,768]{1,0:T(8,128)(2,1)S(1)}, bf16[72,768]{1,0:T(8,128)(2,1)S(1)}, u32[]{:S(2)}, u32[]{:S(2)}) collective-permute-start(bf16[72,768]{1,0:T(8,128)(2,1)S(1)} %select_bitcast_fusion.2), channel_id=1, source_target_pairs={{0,16},{4,20},{8,24},{12,28},{16,0},{20,4},{24,8},{28,12},{1,17},{... | collective-permute-start | bytes 331784 | tf_op jit(solution)/shard_map/ppermute | solution.py:377
  346.2 14.2 %collective-permute-start.49 = (bf16[2,120,768]{2,1,0:T(8,128)(2,1)S(1)}, bf16[2,120,768]{2,1,0:T(8,128)(2,1)S(1)}, u32[]{:S(2)}, u32[]{:S(2)}) collective-permute-start(bf16[2,120,768]{2,1,0:T(8,128)(2,1)S(1)} %fusion.42), channel_id=1, source_target_pairs={{0,1},{1,0},{2,3},{3,2},{4,5},{5,4},{6,7},{7,6},{8,9},{9,8},{10,11... | collective-permute-start | bytes 1105928 | tf_op jit(solution)/shard_map/ppermute | solution.py:380
  347.0 11.6 %collective-permute-start.50 = (bf16[96,768]{1,0:T(8,128)(2,1)S(1)}, bf16[96,768]{1,0:T(8,128)(2,1)S(1)}, u32[]{:S(2)}, u32[]{:S(2)}) collective-permute-start(bf16[96,768]{1,0:T(8,128)(2,1)S(1)} %slice_bitcast_fusion.27), channel_id=1, source_target_pairs={{0,2},{1,3},{2,0},{3,1},{4,6},{5,7},{6,4},{7,5},{8,10},{9,11},{10,... | collective-permute-start | bytes 442376 | tf_op jit(solution)/shard_map/ppermute | solution.py:380
  360.5 21.1 %collective-permute-start.54 = (bf16[2,72,768]{2,1,0:T(8,128)(2,1)S(1)}, bf16[2,72,768]{2,1,0:T(8,128)(2,1)S(1)}, u32[]{:S(2)}, u32[]{:S(2)}) collective-permute-start(bf16[2,72,768]{2,1,0:T(8,128)(2,1)S(1)} %pad_maximum_fusion.21), channel_id=1, source_target_pairs={{2,0},{3,1},{4,6},{5,7},{10,8},{11,9},{12,14},{13,15},{18,16},{19,... | collective-permute-start | bytes 663560 | tf_op jit(solution)/shard_map/ppermute | solution.py:405
  361.9 19.6 %collective-permute-start.53 = (bf16[120,768]{1,0:T(8,128)(2,1)S(1)}, bf16[120,768]{1,0:T(8,128)(2,1)S(1)}, u32[]{:S(2)}, u32[]{:S(2)}) collective-permute-start(bf16[120,768]{1,0:T(8,128)(2,1)S(1)} %slice_bitcast_fusion.25), channel_id=1, source_target_pairs={{0,2},{1,3},{2,0},{3,1},{4,6},{5,7},{6,4},{7,5},{8,10},{9,11},{10,... | collective-permute-start | bytes 552968 | tf_op jit(solution)/shard_map/ppermute | solution.py:380
  365.5 4.1 collective-permute-start.55
  366.2 23.3 %collective-permute-start.59 = (bf16[256,768]{1,0:T(8,128)(2,1)S(1)}, bf16[256,768]{1,0:T(8,128)(2,1)S(1)}, u32[]{:S(2)}, u32[]{:S(2)}) collective-permute-start(bf16[256,768]{1,0:T(8,128)(2,1)S(1)} %copy-done.51), channel_id=1, source_target_pairs={{0,0},{4,1},{1,2},{5,3},{2,4},{6,5},{3,6},{7,7},{8,8},{12,9},{9,10... | collective-permute-start | bytes 1179656 | tf_op jit(solution)/shard_map/ppermute | solution.py:394
  381.8 8.5 %collective-permute-start.57 = (bf16[1,184,768]{2,1,0:T(8,128)(2,1)S(1)}, bf16[1,184,768]{2,1,0:T(8,128)(2,1)S(1)}, u32[]{:S(2)}, u32[]{:S(2)}) collective-permute-start(bf16[1,184,768]{2,1,0:T(8,128)(2,1)S(1)} %fusion.50), channel_id=1, source_target_pairs={{0,8},{4,12},{8,0},{12,4},{16,24},{20,28},{24,16},{28,20},{1,9},{5... | collective-permute-start | bytes 847880 | tf_op jit(solution)/shard_map/ppermute | solution.py:377
  382.5 7.1 %collective-permute-start.56 = (bf16[1,176,768]{2,1,0:T(8,128)(2,1)S(1)}, bf16[1,176,768]{2,1,0:T(8,128)(2,1)S(1)}, u32[]{:S(2)}, u32[]{:S(2)}) collective-permute-start(bf16[1,176,768]{2,1,0:T(8,128)(2,1)S(1)} %maximum_bitcast_fusion), channel_id=1, source_target_pairs={{0,16},{4,20},{8,24},{12,28},{16,0},{20,4},{24,8},{28,12},{1,17},{... | collective-permute-start | bytes 811016 | tf_op jit(solution)/shard_map/ppermute | solution.py:377
  383.5 6.1 %collective-permute-start.58 = (f32[12,768]{1,0:T(8,128)S(1)}, f32[12,768]{1,0:T(8,128)S(1)}, u32[]{:S(2)}, u32[]{:S(2)}) collective-permute-start(f32[12,768]{1,0:T(8,128)S(1)} %add.217), channel_id=1, source_target_pairs={{0,16},{4,20},{8,24},{12,28},{16,0},{20,4},{24,8},{28,12},{1,17},{... | collective-permute-start | bytes 110600 | tf_op jit(solution)/shard_map/ppermute | solution.py:377
  390.4 12.8 %collective-permute-start.61 = (bf16[2,184,768]{2,1,0:T(8,128)(2,1)S(1)}, bf16[2,184,768]{2,1,0:T(8,128)(2,1)S(1)}, u32[]{:S(2)}, u32[]{:S(2)}) collective-permute-start(bf16[2,184,768]{2,1,0:T(8,128)(2,1)S(1)} %maximum_select_fusion.5), channel_id=1, source_target_pairs={{0,16},{4,20},{8,24},{12,28},{16,0},{20,4},{24,8},{28,12},{1,17},{... | collective-permute-start | bytes 1695752 | tf_op jit(solution)/shard_map/ppermute | solution.py:377
  391.4 11.7 %collective-permute-start.60 = (bf16[2,176,768]{2,1,0:T(8,128)(2,1)S(1)}, bf16[2,176,768]{2,1,0:T(8,128)(2,1)S(1)}, u32[]{:S(2)}, u32[]{:S(2)}) collective-permute-start(bf16[2,176,768]{2,1,0:T(8,128)(2,1)S(1)} %maximum_select_fusion.6), channel_id=1, source_target_pairs={{0,8},{4,12},{8,0},{12,4},{16,24},{20,28},{24,16},{28,20},{1,9},{5... | collective-permute-start | bytes 1622024 | tf_op jit(solution)/shard_map/ppermute | solution.py:377
  392.5 4.4 %collective-permute-start.62 = (f32[12,768]{1,0:T(8,128)S(1)}, f32[12,768]{1,0:T(8,128)S(1)}, u32[]{:S(2)}, u32[]{:S(2)}) collective-permute-start(f32[12,768]{1,0:T(8,128)S(1)} %add.218), channel_id=1, source_target_pairs={{0,1},{1,0},{2,3},{3,2},{4,5},{5,4},{6,7},{7,6},{8,9},{9,8},{10,11... | collective-permute-start | bytes 110600 | tf_op jit(solution)/shard_map/ppermute | solution.py:380
  392.5 5.3 %collective-permute-start.63 = (f32[12,768]{1,0:T(8,128)S(1)}, f32[12,768]{1,0:T(8,128)S(1)}, u32[]{:S(2)}, u32[]{:S(2)}) collective-permute-start(f32[12,768]{1,0:T(8,128)S(1)} %add.218), channel_id=1, source_target_pairs={{0,2},{1,3},{2,0},{3,1},{4,6},{5,7},{6,4},{7,5},{8,10},{9,11},{10,... | collective-permute-start | bytes 110600 | tf_op jit(solution)/shard_map/ppermute | solution.py:380
  393.2 6.4 %collective-permute-start.64 = (f32[12,768]{1,0:T(8,128)S(1)}, f32[12,768]{1,0:T(8,128)S(1)}, u32[]{:S(2)}, u32[]{:S(2)}) collective-permute-start(f32[12,768]{1,0:T(8,128)S(1)} %add.218), channel_id=1, source_target_pairs={{0,3},{1,2},{2,1},{3,0},{4,7},{5,6},{6,5},{7,4},{8,11},{9,10},{10,... | collective-permute-start | bytes 110600 | tf_op jit(solution)/shard_map/ppermute | solution.py:380
  403.4 4.9 %collective-permute-start.66 = (bf16[2,2,184,768]{3,2,1,0:T(8,128)(2,1)S(1)}, bf16[2,2,184,768]{3,2,1,0:T(8,128)(2,1)S(1)}, u32[]{:S(2)}, u32[]{:S(2)}) collective-permute-start(bf16[2,2,184,768]{3,2,1,0:T(8,128)(2,1)S(1)} %maximum_select_fusion.2), channel_id=1, source_target_pairs={{0,4},{4,0},{8,12},{12,8},{16,20},{20,16},{24,28},{28,24},{1,5},{5... | collective-permute-start | bytes 3391496 | tf_op jit(solution)/shard_map/ppermute | solution.py:377
  403.6 4.6 %collective-permute-start.65 = (bf16[2,2,176,768]{3,2,1,0:T(8,128)(2,1)S(1)}, bf16[2,2,176,768]{3,2,1,0:T(8,128)(2,1)}, u32[]{:S(2)}, u32[]{:S(2)}) collective-permute-start(bf16[2,2,176,768]{3,2,1,0:T(8,128)(2,1)S(1)} %fusion.25), channel_id=1, source_target_pairs={{0,4},{4,0},{8,12},{12,8},{16,20},{20,16},{24,28},{28,24},{1,5},{5... | collective-permute-start | bytes 3244040 | tf_op jit(solution)/shard_map/ppermute | solution.py:377
  (62 other events, 338.8 us)
where the time goes:
time: 431 us; the launch traced here: 424 us
  waiting for transfers between devices  116 us (27%)
  Pallas kernels  97.3 us (23%)
  starting transfers between devices  78.6 us (18%)
  other arithmetic  70.9 us (16%)
  local copies, waits for them, and re-layouts  45.4 us (11%)
  matrix products  11.1 us (3%)
    ppermute x19, waiting for transfers between devices, tensor(): lax.ppermute(value, 'tensor', [(i, i ^ bit) for i in range(self.shards)])  75.7 us
    ppermute x42, waiting for transfers between devices, dp(): lax.ppermute(value, 'dp', [(i, i ^ bit) for i in range(self.members)])  40.7 us
    ppermute x19, starting transfers between devices, tensor(): lax.ppermute(value, 'tensor', [(i, i ^ bit) for i in range(self.shards)])  34.9 us
    ppermute x42, starting transfers between devices, dp(): lax.ppermute(value, 'dp', [(i, i ^ bit) for i in range(self.members)])  32 us
    pallas_call x2, Pallas kernels, attend_back(): pl.pallas_call(attend_back_kernel, in_specs=[SM] + [VM] * 4, out_specs=[V...  25.3 us
    pallas_call x2, Pallas kernels, feed(): pl.pallas_call(feed_kernel, grid=(hidden // step_size,), in_specs=[whole(...  22.9 us
    pallas_call x2, Pallas kernels, feed_back(): pl.pallas_call(feed_back_kernel, grid=(hidden // step_size,), in_specs=[w...  21.6 us
    pallas_call x2, Pallas kernels, attend(): pl.pallas_call(attend_kernel, in_specs=[SM] + [VM] * 6, out_specs=[VM] *...  20.8 us
  transfers between devices with their start and end apart: 67, of which 33 were waited for; matrix products, arithmetic and copies ran while one was open for 18% of the time, Pallas kernels for 11%

commit v1 on v0

--- a/solution.py
+++ b/solution.py
@@ -210,17 +210,41 @@
 CUBE = 0.044715
 
 
+def keep_or_send(step_at, value, keep_ref, send_ref):
+    size = value.shape[1]
+    steps = keep_ref.shape[1] // size
+    for step in range(steps):
+        block = slice(step * size, (step + 1) * size)
+
+        @pl.when(step_at == step)
+        def _(block=block):
+            keep_ref[:, block] = value
+
+        @pl.when(step_at == step + steps)
+        def _(block=block):
+            send_ref[:, block] = value
+
+
 def feed_kernel(
     att_ref, stream_ref, out_w_ref, fc_ref, proj_ref, vec_ref, bias_ref,
-    mid_ref, low_ref, act_ref, slope_ref, next_ref, norm_ref,
+    mid_ref, low_ref, act_ref, heads_ref, send_ref, slope_ref, next_ref, norm_ref,
 ):
     step_at = pl.program_id(0)
+    width = mid_ref.shape[1]
+    hidden = act_ref.shape[1]
+    step_size = slope_ref.shape[1]
 
     @pl.when(step_at == 0)
     def _():
-        middle = stream_ref[...] + dot(att_ref[...], out_w_ref[...], 0, 0) + vec_ref[0:1, :]
+        heads = att_ref[...].T
+        half = width // 2
+        heads_ref[...] = heads[:, :half]
+        send_ref[:, hidden + width :] = heads[:, half:]
+        middle = stream_ref[...] + dot(heads, out_w_ref[...], 1, 0) + vec_ref[0:1, :]
         mid_ref[...] = middle
-        low_ref[...] = normalize(middle, vec_ref[1:2, :], vec_ref[2:3, :]).astype(BF)
+        low = normalize(middle, vec_ref[1:2, :], vec_ref[2:3, :]).astype(BF)
+        low_ref[...] = low
+        send_ref[:, hidden : hidden + width] = low
         next_ref[...] = middle + vec_ref[3:4, :]
 
     value = dot(low_ref[...], fc_ref[...], 1, 1) + bias_ref[...]
@@ -228,7 +252,7 @@
     bent = jnp.tanh(value * (CURVE + CURVE * CUBE * square))
     half = 0.5 * (1.0 + bent)
     act = (value * half).astype(BF)
-    act_ref[...] = act
+    keep_or_send(step_at, act, act_ref, send_ref)
     slope_ref[...] = half + (0.5 * value) * (1.0 - bent * bent) * (CURVE + 3.0 * CURVE * CUBE * square)
     next_ref[...] += dot(act, proj_ref[...], 1, 0)
 
@@ -251,12 +275,15 @@
             whole((6, width)), pl.BlockSpec((1, step_size), lambda j: (0, j)),
         ],
         out_specs=[
-            whole((rows, width)), whole((rows, width)), block, block, whole((rows, width)), whole((rows, width)),
+            whole((rows, width)), whole((rows, width)), whole((rows, hidden // 2)), whole((rows, width // 2)),
+            whole((rows, hidden // 2 + width + width // 2)), block, whole((rows, width)), whole((rows, width)),
         ],
         out_shape=[
             jax.ShapeDtypeStruct((rows, width), F32),
             jax.ShapeDtypeStruct((rows, width), BF),
-            jax.ShapeDtypeStruct((rows, hidden), BF),
+            jax.ShapeDtypeStruct((rows, hidden // 2), BF),
+            jax.ShapeDtypeStruct((rows, width // 2), BF),
+            jax.ShapeDtypeStruct((rows, hidden // 2 + width + width // 2), BF),
             jax.ShapeDtypeStruct((rows, hidden), F32),
             jax.ShapeDtypeStruct((rows, width), F32),
             jax.ShapeDtypeStruct((rows, width), BF),
@@ -270,11 +297,12 @@
 
 def feed_back_kernel(
     grad_ref, slope_ref, proj_ref, fc_ref, mid_ref, out_w_ref, gain_ref,
-    pre_ref, bias_ref, back_ref, low_ref, heads_ref, sums_ref, acc_ref,
+    pre_ref, send_ref, bias_ref, back_ref, low_ref, heads_ref, sums_ref, acc_ref,
 ):
     step_at = pl.program_id(0)
+    hidden = pre_ref.shape[1]
     pre = (dot(grad_ref[...].astype(BF), proj_ref[...], 1, 1) * slope_ref[...]).astype(BF)
-    pre_ref[...] = pre
+    keep_or_send(step_at, pre, pre_ref, send_ref)
     bias_ref[...] = jnp.sum(pre.astype(F32), axis=0, keepdims=True)
     part = dot(pre, fc_ref[...], 1, 0)
 
@@ -294,6 +322,7 @@
         back_ref[...] = back
         low = back.astype(BF)
         low_ref[...] = low
+        send_ref[:, hidden:] = low
         heads_ref[...] = dot(out_w_ref[...], low, 1, 1).astype(BF)
         sums_ref[0:1, :] = jnp.sum(back, axis=0, keepdims=True)
         sums_ref[1:2, :] = gain_sum
@@ -315,11 +344,13 @@
             whole((1, width)),
         ],
         out_specs=[
-            block, pl.BlockSpec((1, step_size), lambda j: (0, j)), whole((rows, width)), whole((rows, width)),
+            whole((rows, hidden // 2)), whole((rows, hidden // 2 + width)),
+            pl.BlockSpec((1, step_size), lambda j: (0, j)), whole((rows, width)), whole((rows, width)),
             whole((width, rows)), whole((4, width)),
         ],
         out_shape=[
-            jax.ShapeDtypeStruct((rows, hidden), BF),
+            jax.ShapeDtypeStruct((rows, hidden // 2), BF),
+            jax.ShapeDtypeStruct((rows, hidden // 2 + width), BF),
             jax.ShapeDtypeStruct((1, hidden), F32),
             jax.ShapeDtypeStruct((rows, width), F32),
             jax.ShapeDtypeStruct((rows, width), BF),
@@ -516,123 +547,158 @@
     return (left.astype(F32) + right.astype(F32)).astype(BF)
 
 
-def layer_forward(place, stream, normed, scalars, w):
+def layer_forward(place, stream, normed, scalars, w, fed):
     blocks = gather_rows(place, normed)
+    if fed is not None:
+        *blocks, fed = tie(*blocks, fed)
+        fed = place.dp(fed, 1)
     rows, qkv, attended, log_sums = attend(scalars, blocks, w["qkv"], w["b_qkv"])
+    if fed is not None:
+        attended, fed = tie(attended, fed)
     attended = from_heads(place, heads_to_rows(place, attended))
-    middle, normed2, activated, slope, result, normed = feed(attended, stream, w, w["vectors"])
-    return result, normed, (stream, rows, qkv, log_sums, attended, middle, normed2, activated, slope)
+    middle, normed2, activated, heads, send, slope, result, normed = feed(attended, stream, w, w["vectors"])
+    return result, normed, (stream, rows, qkv, log_sums, middle, slope), (normed2, activated, heads), send, fed
 
 
 def pieces(value):
-    return value.reshape(BLOCKS, 4, -1, value.shape[-1])
+    return value.reshape((2, 2, 2, 2, -1) + value.shape[1:])
+
+
+def over_tokens(left, right):
+    return dot(jnp.concatenate(left), jnp.concatenate(right), 0, 0).astype(BF)
 
 
 def both_layers(left, right, ca, cb):
     return dot(jnp.concatenate(left, ca), jnp.concatenate(right, cb), ca, cb).astype(BF)
 
 
-def second_backward(place, gradient, scalars, w, cache, output):
-    stream, rows, qkv, log_sums, attended, middle, normed2, activated, slope = cache
-    grad_pre, bias, grad_middle, mid_low, grad_heads, sums = feed_back(gradient, slope, middle, w, w["ln2_gain"])
+def second_backward(place, gradient, scalars, w, cache, output, fed):
+    stream, rows, qkv, log_sums, middle, slope = cache
+    low = gradient.astype(BF)
+    gradient, low, output, fed = tie(gradient, low, output, fed)
+    low_near = place.dp(low, 1)
+    fed = place.dp(fed, 1)
+    output = place.unplace(output)
+    grad_pre, send, bias, grad_middle, mid_low, grad_heads, sums = feed_back(
+        gradient, slope, middle, w, w["ln2_gain"]
+    )
+    grad_heads, send, low_near, fed, output = tie(grad_heads, send, low_near, fed, output)
     pair = rows_to_pair(place, to_heads(place, grad_heads))
-    grad_qkv, qkv_sums, parts = attend_back(scalars, qkv, pair_to_heads(place, pair), log_sums, w["qkv"])
+    grad_attended, send = tie(pair_to_heads(place, pair), send)
+    near = place.dp(send, 1)
+    grad_qkv, qkv_sums, parts = attend_back(scalars, qkv, grad_attended, log_sums, w["qkv"])
+    parts, near = tie(parts, near)
     parts = parts.reshape(4, -1, parts.shape[1])
     moved = place.dp(jnp.stack([parts[1], parts[3]]), 1)
     far = place.tensor(plus(parts[2], moved[1]), 1)
     own = parts[0].astype(F32) + moved[0].astype(F32)
-    far, output = tie(far, output)
-    gradient_in, low, norms = norm_back(own, far, grad_middle, stream, w["ln1_gain"])
-    left = (gradient.astype(BF), activated, grad_pre, normed2, attended, mid_low, grad_qkv, rows)
-    return gradient_in, low, left, (norms, sums, bias, qkv_sums), output
+    gradient_in, low_in, norms = norm_back(own, far, grad_middle, stream, w["ln1_gain"])
+    later = (low, low_near, grad_pre, mid_low, near, grad_qkv, rows)
+    return gradient_in, low_in, later, (norms, sums, bias, qkv_sums), output, fed
 
 
 def choose(flag, value):
     return jnp.where(flag == 0, value[0], value[1]), jnp.where(flag == 0, value[1], value[0])
 
 
-def chunks(value):
-    return value.reshape((2, 2, 2, 2) + value.shape[2:])
-
-
 def first_step(place, value):
-    return place.dp(value[:, 1, 1], 2), place.dp(value[1, :, 0], 4)
-
-
-def second_step(place, value, moved):
+    return value[:, 1, 1], value[1, :, 0]
+
+
+def step_two(place, value, moved):
     one = plus(value[:, 0, 1], moved[0])
     other = plus(value[0, :, 0], moved[1])
-    return one[0], other[0], place.dp(one[1], 4), place.dp(other[1], 2)
-
-
-def first_backward(place, gradient, low, scalars, w, cache, later, later_small):
-    stream, rows, qkv, log_sums, attended, middle, normed2, activated, slope = cache
+    return one[0], other[0], one[1], other[1]
+
+
+def first_backward(place, gradient, low, scalars, w, cache, products, later, later_small):
+    stream, rows, qkv, log_sums, middle, slope = cache
+    (norm_one, act_one, heads_one, near_one), (norm_two, act_two, heads_two, near_two) = products
+    low_two, low_near_two, pre_two, mid_two, back_two, grad_qkv_two, rows_two = later
+    hidden = act_one.shape[1]
+    width = low.shape[1]
     heads = qkv.shape[0] // 3
-    proj = pieces(both_layers((activated, later[1]), (low, later[0]), 0, 0))
-    proj_far = place.dp(proj[4:], 1)
-    grad_pre, bias, grad_middle, mid_low, grad_heads, sums = feed_back(gradient, slope, middle, w, w["ln2_gain"])
-    proj, proj_far, grad_pre, mid_low, grad_heads = tie(proj, proj_far, grad_pre, mid_low, grad_heads)
-    proj = chunks(plus(proj[:4], proj_far))
-    moved = first_step(place, proj)
+    low_near = place.dp(low, 1)
+    proj = over_tokens(
+        (act_one, near_one[:, :hidden], act_two, near_two[:, :hidden]), (low, low_near, low_two, low_near_two)
+    )
+    proj = pieces(proj)
+    send_x, send_y = first_step(place, proj)
+    gradient, send_x, send_y = tie(gradient, send_x, send_y)
+    proj_moved = place.dp(send_x, 2), place.dp(send_y, 4)
+    grad_pre, send, bias, grad_middle, mid_low, grad_heads, sums = feed_back(
+        gradient, slope, middle, w, w["ln2_gain"]
+    )
+
+    grad_heads, send, grad_pre, mid_low, *proj_moved = tie(grad_heads, send, grad_pre, mid_low, *proj_moved)
     pair = rows_to_pair(place, to_heads(place, grad_heads))
+    near = place.dp(send, 1)
+    proj1, proj0, over_y, over_x = step_two(place, proj, proj_moved)
+    pair, over_y, over_x, near = tie(pair, over_y, over_x, near)
     grad_attended = pair_to_heads(place, pair)
-    fc = jnp.concatenate(
-        [
-            pieces(both_layers((grad_pre, later[2]), (normed2, later[3]), 0, 0)),
-            pieces(both_layers((attended, later[4]), (mid_low, later[5]), 1, 0)),
-        ],
-        2,
-    )
-    fc_far = place.dp(fc[4:], 1)
-    fc, fc_far, grad_attended, *moved = tie(fc, fc_far, grad_attended, *moved)
-    proj1, proj0, *moved = second_step(place, proj, moved)
-    fc = chunks(plus(fc[:4], fc_far))
-    fc, grad_attended, proj1, proj0, *moved = tie(fc, grad_attended, proj1, proj0, *moved)
-    fc_moved = first_step(place, fc)
-    proj1 = plus(proj1, moved[0])
-    proj0 = plus(proj0, moved[1])
+    proj_moved = place.dp(over_y, 4), place.dp(over_x, 2)
+    fc = over_tokens(
+        (grad_pre, near[:, :hidden], pre_two, back_two[:, :hidden]),
+        (norm_one, near_one[:, hidden : hidden + width], norm_two, near_two[:, hidden : hidden + width]),
+    )
+    out = over_tokens(
+        (heads_one, near_one[:, hidden + width :], heads_two, near_two[:, hidden + width :]),
+        (mid_low, near[:, hidden:], mid_two, back_two[:, hidden:]),
+    )
+    fc = jnp.concatenate([pieces(fc), pieces(out)], 4)
+    send_x, send_y = first_step(place, fc)
+    send_x, send_y, *proj_moved = tie(send_x, send_y, *proj_moved)
+    fc_moved = place.dp(send_x, 2), place.dp(send_y, 4)
+    proj1 = plus(proj1, proj_moved[0])
+    proj0 = plus(proj0, proj_moved[1])
+    grad_attended, proj1, send_x, bias, sums = tie(grad_attended, proj1, send_x, bias, sums)
     proj_t = place.tensor(proj1, 1)
     grad_qkv, qkv_sums, parts = attend_back(scalars, qkv, grad_attended, log_sums, w["qkv"])
-    grad_qkv, parts, proj_t, *fc_moved = tie(grad_qkv, parts, proj_t, *fc_moved)
+
+    grad_qkv, qkv_sums, parts, proj_t, *fc_moved = tie(grad_qkv, qkv_sums, parts, proj_t, *fc_moved)
     parts = parts.reshape(4, -1, parts.shape[1])
     moved = place.dp(jnp.stack([parts[1], parts[3]]), 1)
-    fc1, fc0, *fc_moved = second_step(place, fc, fc_moved)
-    grad_wqkv = both_layers((grad_qkv, later[6]), (rows, later[7]), 1, 0)
-    moved, grad_wqkv, *fc_moved = tie(moved, grad_wqkv, *fc_moved)
-    width = grad_wqkv.shape[1]
+    send = plus(parts[2], moved[1])
+    fc1, fc0, over_y, over_x = step_two(place, fc, fc_moved)
+    send, over_y, over_x, grad_qkv = tie(send, over_y, over_x, grad_qkv)
+    far = place.tensor(send, 1)
+    fc_moved = place.dp(over_y, 4), place.dp(over_x, 2)
+    grad_wqkv = both_layers((grad_qkv, grad_qkv_two), (rows, rows_two), 1, 0)
+    proj = plus(proj0, proj_t)
+    proj, grad_wqkv = tie(proj, grad_wqkv)
+    proj_t = place.tensor(proj[1], 2)
     value = grad_wqkv.reshape(2, 2, 2, -1, width)
-    keep_x, send = choose(place.d & 2, value[0])
-    qkv_x = place.dp(send, 2)
-    keep_y, send = choose(place.d & 4, value[1])
-    qkv_y = place.dp(send, 4)
-    far = place.tensor(plus(parts[2], moved[1]), 1)
+    keep_x, send_x = choose(place.d & 2, value[0])
+    keep_y, send_y = choose(place.d & 4, value[1])
     own = parts[0].astype(F32) + moved[0].astype(F32)
+    send_x, send_y, own, *fc_moved = tie(send_x, send_y, own, *fc_moved)
+    qkv_x = place.dp(send_x, 2)
+    qkv_y = place.dp(send_y, 4)
     fc1 = plus(fc1, fc_moved[0])
     fc0 = plus(fc0, fc_moved[1])
-    proj = plus(proj0, proj_t)
-    far, fc1, fc0, proj, qkv_x, qkv_y = tie(far, fc1, fc0, proj, qkv_x, qkv_y)
+    fc1, own = tie(fc1, own)
     fc_t = place.tensor(fc1, 1)
-    proj_t = place.tensor(proj[1], 2)
-    keep_x, send = choose(place.d & 4, plus(keep_x, qkv_x))
-    qkv_x = place.dp(send, 4)
-    keep_y, send = choose(place.d & 2, plus(keep_y, qkv_y))
-    qkv_y = place.dp(send, 2)
     gradient_in, low, norms = norm_back(own, far, grad_middle, stream, w["ln1_gain"])
-    small = [a + b for a, b in zip((norms, sums, bias, qkv_sums), later_small)]
-    small = pack_small(place, small, heads)
-    small = small + place.dp(small, 1)
-    low, small, fc_t, proj_t, qkv_x, qkv_y = tie(low, small, fc_t, proj_t, qkv_x, qkv_y)
+    low, proj_t, qkv_x, qkv_y, bias, qkv_sums, sums = tie(low, proj_t, qkv_x, qkv_y, bias, qkv_sums, sums)
+    keep_x, send_x = choose(place.d & 4, plus(keep_x, qkv_x))
+    qkv_x = place.dp(send_x, 4)
+    keep_y, send_y = choose(place.d & 2, plus(keep_y, qkv_y))
+    qkv_y = place.dp(send_y, 2)
+    fc_t, proj, proj_t, low = tie(fc_t, proj, proj_t, low)
+    fc = plus(fc0, fc_t)
+    fc_t = place.tensor(fc[1], 2)
+    low, sums, bias, qkv_sums, qkv_x, qkv_y = tie(low, sums, bias, qkv_sums, qkv_x, qkv_y)
     both = jnp.stack([plus(keep_x, qkv_x), plus(keep_y, qkv_y)])
     for bit in place.extra:
         both = plus(both, place.dp(both, bit))
     both_far = place.cross(both, False)
-    fc = plus(fc0, fc_t)
-    fc_t = place.tensor(fc[1], 2)
+    both, low = tie(both, low)
     placed = place.unplace(low)
+    small = [a + b for a, b in zip((norms, sums, bias, qkv_sums), later_small)]
+    small = pack_small(place, small, heads)
+    small = small + place.dp(small, 1)
     small_far = place.dp(small, 2)
-    fc_t, both_far, proj_t, small_far = tie(fc_t, both_far, proj_t, small_far)
-    small = small + small_far
-    small_far = place.dp(small, 4)
+    fc_t, both_far, small_far = tie(fc_t, both_far, small_far)
     large = jnp.concatenate([plus(fc[0], fc_t), plus(proj[0], proj_t)])
     for bit in place.extra:
         large = plus(large, place.dp(large, bit))
@@ -640,14 +706,17 @@
     count = large.shape[0] // 16 * 8
     one = jnp.concatenate([large[:count], both[0]])[None]
     two = jnp.concatenate([large[count:], both[1]])[None]
-    one, two, one_far, two_far, small_far, placed = tie(
-        one, two, place.dp(one, 4), place.dp(two, 2), small_far, placed
-    )
+    one, two, small, small_far = tie(one, two, small, small_far)
+    one_far, two_far = place.dp(one, 4), place.dp(two, 2)
     small = small + small_far
-    small_far = [place.tensor(small, bit) for bit in (1, 2, 3)]
+    small_far = place.dp(small, 4)
+    one, two, one_far, two_far, small_far, placed = tie(one, two, one_far, two_far, small_far, placed)
+    small = small + small_far
     one = ordered(place.d & 4, one, one_far)
     two = ordered(place.d & 2, two, two_far)
-    one, two, one_far, two_far, *small_far = tie(one, two, place.dp(one, 2), place.dp(two, 4), *small_far)
+    one_far, two_far = place.dp(one, 2), place.dp(two, 4)
+    small_far = [place.tensor(small, bit) for bit in (1, 2, 3)]
+    one, two, one_far, two_far, *small_far = tie(one, two, one_far, two_far, *small_far)
     small = small + small_far[0] + small_far[1] + small_far[2]
     bit = 8
     while bit < place.members:
@@ -723,14 +792,16 @@
     )
     scalars = jnp.concatenate([length, place.quarter[None]])
     normed = normalize(stream, ln1_gain, ln1_shift).astype(BF)
-    layer_one, normed, cache_first = layer_forward(place, stream, normed, scalars, w)
-    layer_two, _, cache_second = layer_forward(place, layer_one, normed, scalars, w)
+    layer_one, normed, cache_first, one, fed, _ = layer_forward(place, stream, normed, scalars, w, None)
+    layer_two, _, cache_second, two, fed_two, near_one = layer_forward(place, layer_one, normed, scalars, w, fed)
     position = place.quarter * row_total + lax.broadcasted_iota(jnp.int32, (row_total, 1), 0)
     gradient = jnp.where(position < length[0], place.place(cotangent).astype(F32), 0.0)
-    output = place.unplace(layer_two.astype(BF))
-    gradient, low, later, later_small, output = second_backward(place, gradient, scalars, w, cache_second, output)
+    gradient, low, later, later_small, output, near_two = second_backward(
+        place, gradient, scalars, w, cache_second, layer_two.astype(BF), fed_two
+    )
+    products = (*one, near_one), (*two, near_two)
     placed, one, two, g_qkv, packed = first_backward(
-        place, gradient, low, scalars, w, cache_first, later, later_small
+        place, gradient, low, scalars, w, cache_first, products, later, later_small
     )
     grad_tokens = placed.astype(F32)
     g_qkv = g_qkv.reshape(3, heads, width).transpose(0, 2, 1)

time: 431 us -> 410 us (0.951)
  waiting for transfers between devices: 116 us -> 88.3 us
  starting transfers between devices: 78.6 us -> 84.9 us
  other arithmetic: 70.9 us -> 65.4 us
  Pallas kernels: 97.3 us -> 102 us
    ppermute x19, waiting for transfers between devices: 75.7 us -> 51.5 us  [tensor(): lax.ppermute(value, 'tensor', [(i, i ^ bit) for i in range(self.shards)])]
    convert_element_type x16 -> x12, other arithmetic: 13.4 us -> 8.4 us  [plus(): return (left.astype(F32) + right.astype(F32)).astype(BF)]
    slice x1 -> x17, local copies, waits for them, and re-layouts: 0.15 us -> 4.82 us  [the longest x1 2.08 us: first_backward(): back_two[:, :hidden]]
    concatenate x2 -> x0, other arithmetic: 4.6 us -> none  [first_backward(): jnp.concatenate([pieces(both_layers((grad_pre, later[2]), (normed2, later...]
    ppermute x42 -> x46, waiting for transfers between devices: 40.7 us -> 36.7 us  [dp(): lax.ppermute(value, 'dp', [(i, i ^ bit) for i in range(self.members)])]
    ppermute x42 -> x46, starting transfers between devices: 32 us -> 35.8 us  [dp(): lax.ppermute(value, 'dp', [(i, i ^ bit) for i in range(self.members)])]
    unnamed x125 -> x159, local copies, waits for them, and re-layouts: 14.4 us -> 13.6 us
  transfers between devices with their start and end apart: 67 -> 71, of which waited for: 33 -> 26; matrix products, arithmetic and copies ran while one was open for 18% -> 18% of each run, Pallas kernels for 11% -> 18%
where the time goes in v1:
time: 410 us; the launch traced here: 403 us
  Pallas kernels  102 us (25%)
  waiting for transfers between devices  88.3 us (22%)
  starting transfers between devices  84.9 us (21%)
  other arithmetic  65.4 us (16%)
  local copies, waits for them, and re-layouts  48.5 us (12%)
  matrix products  9.17 us (2%)
  between operations  4.34 us (1%)
    ppermute x19, waiting for transfers between devices, tensor(): lax.ppermute(value, 'tensor', [(i, i ^ bit) for i in range(self.shards)])  51.5 us
    ppermute x19, starting transfers between devices, tensor(): lax.ppermute(value, 'tensor', [(i, i ^ bit) for i in range(self.shards)])  37.6 us
    ppermute x46, waiting for transfers between devices, dp(): lax.ppermute(value, 'dp', [(i, i ^ bit) for i in range(self.members)])  36.7 us
    ppermute x46, starting transfers between devices, dp(): lax.ppermute(value, 'dp', [(i, i ^ bit) for i in range(self.members)])  35.8 us
    pallas_call x2, Pallas kernels, feed(): pl.pallas_call(feed_kernel, grid=(hidden // step_size,), in_specs=[whole(...  25.6 us
    pallas_call x2, Pallas kernels, attend_back(): pl.pallas_call(attend_back_kernel, in_specs=[SM] + [VM] * 4, out_specs=[V...  25.2 us
    pallas_call x2, Pallas kernels, feed_back(): pl.pallas_call(feed_back_kernel, grid=(hidden // step_size,), in_specs=[w...  24.1 us
    pallas_call x2, Pallas kernels, attend(): pl.pallas_call(attend_kernel, in_specs=[SM] + [VM] * 6, out_specs=[VM] *...  20.7 us
  transfers between devices with their start and end apart: 71, of which 26 were waited for; matrix products, arithmetic and copies ran while one was open for 18% of the time, Pallas kernels for 18%

profile of v1, /device:TPU:0, one launch (start us, length us, event | category | flops | bytes accessed | tf_op | source)
XLA Modules:
  0.0 402.8 jit_solution(9182149761709177878)
XLA Ops:
  2.6 4.1 %collective-permute-start.16 = (bf16[104,768]{1,0:T(8,128)(2,1)S(1)}, bf16[104,768]{1,0:T(8,128)(2,1)S(1)}, u32[]{:S(2)}, u32[]{:S(2)}) collective-permute-start(bf16[104,768]{1,0:T(8,128)(2,1)S(1)} %concatenate.188), channel_id=1, source_target_pairs={{0,2},{1,3},{2,0},{3,1},{4,6},{5,7},{6,4},{7,5},{8,10},{9,11},{10,... | collective-permute-start | bytes 479240 | tf_op jit(solution)/shard_map/ppermute | solution.py:411
  10.3 5.5 %collective-permute-start.6 = (bf16[152,768]{1,0:T(8,128)(2,1)}, bf16[152,768]{1,0:T(8,128)(2,1)}, u32[]{:S(2)}, u32[]{:S(2)}) collective-permute-start(bf16[152,768]{1,0:T(8,128)(2,1)} %fusion.87), channel_id=1, source_target_pairs={{0,2},{1,3},{6,4},{7,5},{8,10},{9,11},{14,12},{15,13},{16,18},{17,... | collective-permute-start | bytes 700424 | tf_op jit(solution)/shard_map/ppermute | solution.py:436
  17.7 1.9 reverse_select_fusion.2
  27.5 2.5 collective-permute-start.17
  33.1 4.5 %collective-permute-start.4 = (bf16[256,768]{1,0:T(8,128)(2,1)}, bf16[256,768]{1,0:T(8,128)(2,1)}, u32[]{:S(2)}, u32[]{:S(2)}) collective-permute-start(bf16[256,768]{1,0:T(8,128)(2,1)} %add_convert_fusion.own_ref), channel_id=1, source_target_pairs={{0,1},{1,0},{2,3},{3,2},{4,5},{5,4},{6,7},{7,6},{8,9},{9,8},{10,11... | collective-permute-start | bytes 1179656 | tf_op jit(solution)/shard_map/ppermute | solution.py:411
  38.6 2.0 maximum_select_fusion.7
  44.6 2.5 collective-permute-done.12
  49.7 1.9 constant_dynamic-update-slice_fusion.4
  51.6 3.7 collective-permute-done.4.far_ref
  57.7 2.1 fusion.58
  59.8 6.4 %collective-permute-done.13 = bf16[3,120,768]{2,1,0:T(8,128)(2,1)S(1)} collective-permute-done((bf16[3,120,768]{2,1,0:T(8,128)(2,1)S(1)}, bf16[3,120,768]{2,1,0:T(8,128)(2,1)S(1)}, u32[]{:S(2)}, u32[]{:S(2)}) %collective-permute-start.13) | collective-permute-done | bytes 552992 | tf_op jit(solution)/shard_map/ppermute | solution.py:408
  70.8 10.5 %attend.2 = (bf16[1024,768]{1,0:T(8,128)(2,1)}, bf16[576,1024]{1,0:T(8,128)(2,1)}, bf16[192,1024]{1,0:T(8,128)(2,1)}, f32[3,1024]{1,0:T(4,128)}) custom-call(s32[2]{0:T(128)} %pad_add_fusion.scalar_ref, bf16[256,768]{1,0:T(8,128)(2,1)} %add_convert_fusion.own_ref, bf16[256,768]{1,0:T(8,128)(2,1)} %collective-permute-done.3.near_ref, ...), custom_call_target="tpu_custom_call" | custom-call | flops 2113929216 | bytes 4718592 | tf_op jit(solution)/shard_map/attend/pallas_call | solution.py:113
  82.3 2.5 collective-permute-start.9
  85.8 2.7 collective-permute-done.9
  89.2 2.5 pad_maximum_fusion.2
  93.1 2.1 fusion.106
  101.1 4.6 %maximum_maximum_fusion = bf16[8,4,96,768]{3,2,1,0:T(8,128)(2,1)} fusion(bf16[4,3,96,768]{3,2,1,0:T(8,128)(2,1)} %collective-permute-done.20, bf16[2,3,96,768]{3,2,1,0:T(8,128)(2,1)} %collective-permute-done.19, bf16[1,3,96,768]{3,2,1,0:T(8,128)(2,1)S(1)} %bitcast.289, bf16[1,3,96,768]{3,2,1,0:T(8,128)(2,1)S(1)} %fusion.114, ...), kind=kLoop, calls=%fused_computation | loop fusion | flops 9437184 | bytes 9437184 | tf_op jit(solution)/shard_map/concatenate | solution.py:783
  105.7 1.8 constant_dynamic-update-slice_fusion
  108.0 2.6 pad_maximum_fusion
  111.7 12.8 %feed.2 = (f32[256,768]{1,0:T(8,128)}, bf16[256,768]{1,0:T(8,128)(2,1)}, bf16[256,1536]{1,0:T(8,128)(2,1)}, bf16[256,384]{1,0:T(8,128)(2,1)}, bf16[256,2688]{1,0...) custom-call(bf16[768,256]{1,0:T(8,128)(2,1)} %bitcast.307, ...), custom_call_target="tpu_custom_call" | custom-call | flops 2415919104 | bytes 14155776 | tf_op jit(solution)/shard_map/feed/pallas_call | solution.py:270
  126.0 10.4 %collective-permute-done.22.far_ref = bf16[256,768]{1,0:T(8,128)(2,1)S(1)} collective-permute-done((bf16[256,768]{1,0:T(8,128)(2,1)}, bf16[256,768]{1,0:T(8,128)(2,1)S(1)}, u32[]{:S(2)}, u32[]{:S(2)}) %collective-permute-start.22) | collective-permute-done | bytes 393248 | tf_op jit(solution)/shard_map/ppermute | solution.py:411
  138.9 10.2 %attend.3 = (bf16[1024,768]{1,0:T(8,128)(2,1)}, bf16[576,1024]{1,0:T(8,128)(2,1)}, bf16[192,1024]{1,0:T(8,128)(2,1)}, f32[3,1024]{1,0:T(4,128)}) custom-call(s32[2]{0:T(128)} %pad_add_fusion.scalar_ref, bf16[256,768]{1,0:T(8,128)(2,1)} %get-tuple-element.192.own_ref, bf16[256,768]{1,0:T(8,128)(2,1)} %copy-done.67, bf16[256,768]{1,0:T(8,128)(2,1)} %copy-done.66, ...), custom_call_target="tpu_custom_call" | custom-call | flops 2113929216 | bytes 4718592 | tf_op jit(solution)/shard_map/attend/pallas_call | solution.py:113
  150.2 3.3 collective-permute-start.25
  154.5 3.3 collective-permute-done.25
  157.8 1.8 collective-permute-start.26
  161.8 12.8 %feed.3 = (f32[256,768]{1,0:T(8,128)}, bf16[256,768]{1,0:T(8,128)(2,1)}, bf16[256,1536]{1,0:T(8,128)(2,1)}, bf16[256,384]{1,0:T(8,128)(2,1)}, bf16[256,2688]{1,0...) custom-call(bf16[768,256]{1,0:T(8,128)(2,1)} %bitcast.308, ...), custom_call_target="tpu_custom_call" | custom-call | flops 2415919104 | bytes 14155776 | tf_op jit(solution)/shard_map/feed/pallas_call | solution.py:270
  174.6 1.9 convert_element_type.325
  178.7 12.0 %feed_back.2 = (bf16[256,1536]{1,0:T(8,128)(2,1)}, bf16[256,2304]{1,0:T(8,128)(2,1)}, f32[1,3072]{1,0:T(1,128)}, f32[256,768]{1,0:T(8,128)}, bf16[256,768]{1,0:T...) custom-call(f32[256,768]{1,0:T(8,128)} %get-tuple-element.202.grad_ref, ...), custom_call_target="tpu_custom_call" | custom-call | flops 2415919104 | bytes 14155776 | tf_op jit(solution)/shard_map/feed_back/pallas_call | solution.py:339
  192.5 2.1 collective-permute-start.30
  195.6 2.6 collective-permute-start.31
  198.2 5.4 %collective-permute-done.31 = bf16[192,512]{1,0:T(8,128)(2,1)S(1)} collective-permute-done((bf16[192,512]{1,0:T(8,128)(2,1)S(1)}, bf16[192,512]{1,0:T(8,128)(2,1)S(1)}, u32[]{:S(2)}, u32[]{:S(2)}) %collective-permute-start.31) | collective-permute-done | bytes 196640 | tf_op jit(solution)/shard_map/ppermute | solution.py:411
  204.4 12.5 %attend_back.2 = (bf16[576,1024]{1,0:T(8,128)(2,1)}, f32[576,1]{1,0:T(8,128)}, bf16[1024,768]{1,0:T(8,128)(2,1)}) custom-call(s32[2]{0:T(128)} %pad_add_fusion.scalar_ref, bf16[576,1024]{1,0:T(8,128)(2,1)} %get-tuple-element.211.qkv_ref, bf16[192,1024]{1,0:T(8,128)(2,1)} %pad_maximum_fusion.15.grad_ref, f32[3,1024]{1,0:T(4,128)} %get-tuple-element.215.lse_ref, ...), custom_call_target="tpu_custom_call" | custom-call | flops 3321888768 | bytes 5898240 | tf_op jit(solution)/shard_map/attend_back/pallas_call | solution.py:190
  218.9 1.9 collective-permute-done.33
  223.6 9.7 %collective-permute-done.34.far_ref = bf16[256,768]{1,0:T(8,128)(2,1)S(1)} collective-permute-done((bf16[256,768]{1,0:T(8,128)(2,1)S(1)}, bf16[256,768]{1,0:T(8,128)(2,1)S(1)}, u32[]{:S(2)}, u32[]{:S(2)}) %collective-permute-start.34) | collective-permute-done | bytes 393248 | tf_op jit(solution)/shard_map/ppermute | solution.py:411
  234.0 3.3 norm_back.2
  237.5 1.8 collective-permute-done.35
  239.3 3.7 convolution_convert_fusion.1
  247.7 1.8 slice.481
  249.5 2.1 slice.475
  251.5 12.1 %feed_back.3 = (bf16[256,1536]{1,0:T(8,128)(2,1)}, bf16[256,2304]{1,0:T(8,128)(2,1)}, f32[1,3072]{1,0:T(1,128)}, f32[256,768]{1,0:T(8,128)}, bf16[256,768]{1,0:T...) custom-call(f32[256,768]{1,0:T(8,128)} %get-tuple-element.227.grad_ref, ...), custom_call_target="tpu_custom_call" | custom-call | flops 2415919104 | bytes 14155776 | tf_op jit(solution)/shard_map/feed_back/pallas_call | solution.py:339
  272.6 2.7 convolution_convert_fusion
  281.0 1.8 pad_maximum_fusion.17.grad_ref
  282.8 1.8 fusion.78
  284.6 1.7 collective-permute-start.43
  286.3 12.7 %attend_back.3 = (bf16[576,1024]{1,0:T(8,128)(2,1)}, f32[576,1]{1,0:T(8,128)}, bf16[1024,768]{1,0:T(8,128)(2,1)}) custom-call(s32[2]{0:T(128)} %pad_add_fusion.scalar_ref, bf16[576,1024]{1,0:T(8,128)(2,1)} %get-tuple-element.250.qkv_ref, bf16[192,1024]{1,0:T(8,128)(2,1)} %pad_maximum_fusion.17.grad_ref, f32[3,1024]{1,0:T(4,128)} %get-tuple-element.259.lse_ref, ...), custom_call_target="tpu_custom_call" | custom-call | flops 3321888768 | bytes 5898240 | tf_op jit(solution)/shard_map/attend_back/pallas_call | solution.py:190
  300.5 1.8 fusion.44
  305.8 2.0 fusion.45
  312.0 6.8 %collective-permute-done.47 = bf16[2,120,768]{2,1,0:T(8,128)(2,1)S(1)} collective-permute-done((bf16[2,120,768]{2,1,0:T(8,128)(2,1)S(1)}, bf16[2,120,768]{2,1,0:T(8,128)(2,1)S(1)}, u32[]{:S(2)}, u32[]{:S(2)}) %collective-permute-start.47) | collective-permute-done | bytes 368672 | tf_op jit(solution)/shard_map/ppermute | solution.py:408
  324.1 3.3 norm_back.3
  332.4 2.2 collective-permute-start.55
  334.9 2.7 collective-permute-done.55
  340.1 3.6 collective-permute-start.54
  346.0 3.0 collective-permute-done.59
  349.0 10.2 %collective-permute-done.54 = bf16[120,768]{1,0:T(8,128)(2,1)S(1)} collective-permute-done((bf16[120,768]{1,0:T(8,128)(2,1)S(1)}, bf16[120,768]{1,0:T(8,128)(2,1)S(1)}, u32[]{:S(2)}, u32[]{:S(2)}) %collective-permute-start.54) | collective-permute-done | bytes 184352 | tf_op jit(solution)/shard_map/ppermute | solution.py:411
  360.0 1.8 collective-permute-start.60
  362.0 4.9 %collective-permute-done.62 = f32[12,768]{1,0:T(8,128)S(1)} collective-permute-done((f32[12,768]{1,0:T(8,128)S(1)}, f32[12,768]{1,0:T(8,128)S(1)}, u32[]{:S(2)}, u32[]{:S(2)}) %collective-permute-start.62) | collective-permute-done | bytes 36896 | tf_op jit(solution)/shard_map/ppermute | solution.py:408
  367.8 1.9 collective-permute-start.65
  372.6 3.2 collective-permute-start.68
  376.5 2.0 collective-permute-done.68
  378.5 3.3 collective-permute-done.64
  382.8 1.9 convert_element_type.409
  390.8 1.8 slice_select_fusion.1
  392.6 1.8 slice_select_fusion
  394.7 2.0 copy.130
  (477 shorter events, 123.3 us)
Async XLA Ops:
  2.6 24.9 %collective-permute-start.16 = (bf16[104,768]{1,0:T(8,128)(2,1)S(1)}, bf16[104,768]{1,0:T(8,128)(2,1)S(1)}, u32[]{:S(2)}, u32[]{:S(2)}) collective-permute-start(bf16[104,768]{1,0:T(8,128)(2,1)S(1)} %concatenate.188), channel_id=1, source_target_pairs={{0,2},{1,3},{2,0},{3,1},{4,6},{5,7},{6,4},{7,5},{8,10},{9,11},{10,... | collective-permute-start | bytes 479240 | tf_op jit(solution)/shard_map/ppermute | solution.py:411
  9.1 20.9 %collective-permute-start.11 = (bf16[120,768]{1,0:T(8,128)(2,1)}, bf16[120,768]{1,0:T(8,128)(2,1)S(1)}, u32[]{:S(2)}, u32[]{:S(2)}) collective-permute-start(bf16[120,768]{1,0:T(8,128)(2,1)} %get-tuple-element.433), channel_id=1, source_target_pairs={{0,2},{1,3},{2,0},{3,1},{4,6},{5,7},{6,4},{7,5},{8,10},{9,11},{10,... | collective-permute-start | bytes 552968 | tf_op jit(solution)/shard_map/ppermute | solution.py:411
  10.3 19.8 %collective-permute-start.6 = (bf16[152,768]{1,0:T(8,128)(2,1)}, bf16[152,768]{1,0:T(8,128)(2,1)}, u32[]{:S(2)}, u32[]{:S(2)}) collective-permute-start(bf16[152,768]{1,0:T(8,128)(2,1)} %fusion.87), channel_id=1, source_target_pairs={{0,2},{1,3},{6,4},{7,5},{8,10},{9,11},{14,12},{15,13},{16,18},{17,... | collective-permute-start | bytes 700424 | tf_op jit(solution)/shard_map/ppermute | solution.py:436
  15.8 10.3 %collective-permute-start = (s32[1]{0:T(128)}, s32[1]{0:T(128)}, u32[]{:S(2)}, u32[]{:S(2)}) collective-permute-start(s32[1]{0:T(128)} %param.20), channel_id=1, source_target_pairs={{0,4},{4,0},{8,12},{12,8},{16,20},{20,16},{24,28},{28,24},{1,5},{5... | collective-permute-start | bytes 20 | tf_op jit(solution)/shard_map/ppermute | solution.py:408
  15.9 15.9 %collective-permute-start.2 = (bf16[256,768]{1,0:T(8,128)(2,1)}, bf16[256,768]{1,0:T(8,128)(2,1)S(1)}, u32[]{:S(2)}, u32[]{:S(2)}) collective-permute-start(bf16[256,768]{1,0:T(8,128)(2,1)} %param.19), channel_id=1, source_target_pairs={{0,0},{1,4},{2,1},{3,5},{4,2},{5,6},{6,3},{7,7},{8,8},{9,12},{10,9... | collective-permute-start | bytes 1179656 | tf_op jit(solution)/shard_map/ppermute | solution.py:422
  27.5 14.6 %collective-permute-start.17 = (bf16[2,104,768]{2,1,0:T(8,128)(2,1)S(1)}, bf16[2,104,768]{2,1,0:T(8,128)(2,1)S(1)}, u32[]{:S(2)}, u32[]{:S(2)}) collective-permute-start(bf16[2,104,768]{2,1,0:T(8,128)(2,1)S(1)} %pad_maximum_fusion.19), channel_id=1, source_target_pairs={{0,1},{1,0},{2,3},{3,2},{4,5},{5,4},{6,7},{7,6},{8,9},{9,8},{10,11... | collective-permute-start | bytes 958472 | tf_op jit(solution)/shard_map/ppermute | solution.py:411
  30.0 17.1 %collective-permute-start.12 = (bf16[2,120,768]{2,1,0:T(8,128)(2,1)S(1)}, bf16[2,120,768]{2,1,0:T(8,128)(2,1)}, u32[]{:S(2)}, u32[]{:S(2)}) collective-permute-start(bf16[2,120,768]{2,1,0:T(8,128)(2,1)S(1)} %pad_maximum_fusion.18), channel_id=1, source_target_pairs={{0,1},{1,0},{2,3},{3,2},{4,5},{5,4},{6,7},{7,6},{8,9},{9,8},{10,11... | collective-permute-start | bytes 1105928 | tf_op jit(solution)/shard_map/ppermute | solution.py:411
  30.1 8.5 %collective-permute-start.7 = (bf16[152,768]{1,0:T(8,128)(2,1)}, bf16[152,768]{1,0:T(8,128)(2,1)S(1)}, u32[]{:S(2)}, u32[]{:S(2)}) collective-permute-start(bf16[152,768]{1,0:T(8,128)(2,1)} %collective-permute-done.6), channel_id=1, source_target_pairs={{0,8},{4,12},{8,0},{12,4},{16,24},{20,28},{24,16},{28,20},{1,9},{5... | collective-permute-start | bytes 700424 | tf_op jit(solution)/shard_map/ppermute | solution.py:408
  33.1 22.1 %collective-permute-start.4 = (bf16[256,768]{1,0:T(8,128)(2,1)}, bf16[256,768]{1,0:T(8,128)(2,1)}, u32[]{:S(2)}, u32[]{:S(2)}) collective-permute-start(bf16[256,768]{1,0:T(8,128)(2,1)} %add_convert_fusion.own_ref), channel_id=1, source_target_pairs={{0,1},{1,0},{2,3},{3,2},{4,5},{5,4},{6,7},{7,6},{8,9},{9,8},{10,11... | collective-permute-start | bytes 1179656 | tf_op jit(solution)/shard_map/ppermute | solution.py:411
  37.7 33.1 %collective-permute-start.3 = (bf16[256,768]{1,0:T(8,128)(2,1)}, bf16[256,768]{1,0:T(8,128)(2,1)}, u32[]{:S(2)}, u32[]{:S(2)}) collective-permute-start(bf16[256,768]{1,0:T(8,128)(2,1)} %add_convert_fusion.own_ref), channel_id=1, source_target_pairs={{0,4},{4,0},{8,12},{12,8},{16,20},{20,16},{24,28},{28,24},{1,5},{5... | collective-permute-start | bytes 1179656 | tf_op jit(solution)/shard_map/ppermute | solution.py:408
  40.6 17.1 %collective-permute-start.8 = (bf16[304,768]{1,0:T(8,128)(2,1)}, bf16[304,768]{1,0:T(8,128)(2,1)}, u32[]{:S(2)}, u32[]{:S(2)}) collective-permute-start(bf16[304,768]{1,0:T(8,128)(2,1)} %maximum_select_fusion.7), channel_id=1, source_target_pairs={{0,16},{4,20},{8,24},{12,28},{16,0},{20,4},{24,8},{28,12},{1,17},{... | collective-permute-start | bytes 1400840 | tf_op jit(solution)/shard_map/ppermute | solution.py:408
  42.9 12.6 %collective-permute-start.18 = (bf16[3,96,768]{2,1,0:T(8,128)(2,1)}, bf16[3,96,768]{2,1,0:T(8,128)(2,1)S(1)}, u32[]{:S(2)}, u32[]{:S(2)}) collective-permute-start(bf16[3,96,768]{2,1,0:T(8,128)(2,1)} %pad_maximum_fusion.12), channel_id=1, source_target_pairs={{0,8},{4,12},{8,0},{12,4},{16,24},{20,28},{24,16},{28,20},{1,9},{5... | collective-permute-start | bytes 1327112 | tf_op jit(solution)/shard_map/ppermute | solution.py:408
  48.2 18.0 %collective-permute-start.13 = (bf16[3,120,768]{2,1,0:T(8,128)(2,1)S(1)}, bf16[3,120,768]{2,1,0:T(8,128)(2,1)S(1)}, u32[]{:S(2)}, u32[]{:S(2)}) collective-permute-start(bf16[3,120,768]{2,1,0:T(8,128)(2,1)S(1)} %get-tuple-element.411), channel_id=1, source_target_pairs={{0,16},{4,20},{8,24},{12,28},{16,0},{20,4},{24,8},{28,12},{1,17},{... | collective-permute-start | bytes 1658888 | tf_op jit(solution)/shard_map/ppermute | solution.py:408
  55.3 15.5 %collective-permute-start.5 = (bf16[256,768]{1,0:T(8,128)(2,1)}, bf16[256,768]{1,0:T(8,128)(2,1)}, u32[]{:S(2)}, u32[]{:S(2)}) collective-permute-start(bf16[256,768]{1,0:T(8,128)(2,1)} %collective-permute-done.4.far_ref), channel_id=1, source_target_pairs={{0,4},{4,0},{8,12},{12,8},{16,20},{20,16},{24,28},{28,24},{1,5},{5... | collective-permute-start | bytes 1179656 | tf_op jit(solution)/shard_map/ppermute | solution.py:408
  56.5 32.7 %collective-permute-start.19 = (bf16[2,3,96,768]{3,2,1,0:T(8,128)(2,1)}, bf16[2,3,96,768]{3,2,1,0:T(8,128)(2,1)}, u32[]{:S(2)}, u32[]{:S(2)}) collective-permute-start(bf16[2,3,96,768]{3,2,1,0:T(8,128)(2,1)} %pad_maximum_fusion.6), channel_id=1, source_target_pairs={{0,16},{4,20},{8,24},{12,28},{16,0},{20,4},{24,8},{28,12},{1,17},{... | collective-permute-start | bytes 2654216 | tf_op jit(solution)/shard_map/ppermute | solution.py:408
  67.3 25.8 %collective-permute-start.14 = (bf16[2,3,120,768]{3,2,1,0:T(8,128)(2,1)}, bf16[2,3,120,768]{3,2,1,0:T(8,128)(2,1)}, u32[]{:S(2)}, u32[]{:S(2)}) collective-permute-start(bf16[2,3,120,768]{3,2,1,0:T(8,128)(2,1)} %pad_maximum_fusion.5), channel_id=1, source_target_pairs={{0,8},{4,12},{8,0},{12,4},{16,24},{20,28},{24,16},{28,20},{1,9},{5... | collective-permute-start | bytes 3317768 | tf_op jit(solution)/shard_map/ppermute | solution.py:408
  82.3 6.2 %collective-permute-start.9 = (bf16[192,512]{1,0:T(8,128)(2,1)S(1)}, bf16[192,512]{1,0:T(8,128)(2,1)S(1)}, u32[]{:S(2)}, u32[]{:S(2)}) collective-permute-start(bf16[192,512]{1,0:T(8,128)(2,1)S(1)} %slice.431), channel_id=1, source_target_pairs={{0,1},{1,0},{2,3},{3,2},{4,5},{5,4},{6,7},{7,6},{8,9},{9,8},{10,11... | collective-permute-start | bytes 589832 | tf_op jit(solution)/shard_map/ppermute | solution.py:411
  89.2 8.4 %collective-permute-start.10 = (bf16[384,256]{1,0:T(8,128)(2,1)}, bf16[384,256]{1,0:T(8,128)(2,1)}, u32[]{:S(2)}, u32[]{:S(2)}) collective-permute-start(bf16[384,256]{1,0:T(8,128)(2,1)} %pad_maximum_fusion.24), channel_id=1, source_target_pairs={{0,4},{4,0},{8,12},{12,8},{16,20},{20,16},{24,28},{28,24},{1,5},{5... | collective-permute-start | bytes 589832 | tf_op jit(solution)/shard_map/ppermute | solution.py:408
  91.7 9.4 %collective-permute-start.20 = (bf16[4,3,96,768]{3,2,1,0:T(8,128)(2,1)}, bf16[4,3,96,768]{3,2,1,0:T(8,128)(2,1)}, u32[]{:S(2)}, u32[]{:S(2)}) collective-permute-start(bf16[4,3,96,768]{3,2,1,0:T(8,128)(2,1)} %pad_maximum_fusion.2), channel_id=1, source_target_pairs={{0,4},{4,0},{8,12},{12,8},{16,20},{20,16},{24,28},{28,24},{1,5},{5... | collective-permute-start | bytes 5308424 | tf_op jit(solution)/shard_map/ppermute | solution.py:408
  96.9 8.8 %collective-permute-start.15 = (bf16[4,3,120,768]{3,2,1,0:T(8,128)(2,1)}, bf16[4,3,120,768]{3,2,1,0:T(8,128)(2,1)}, u32[]{:S(2)}, u32[]{:S(2)}) collective-permute-start(bf16[4,3,120,768]{3,2,1,0:T(8,128)(2,1)} %pad_maximum_fusion.1), channel_id=1, source_target_pairs={{0,4},{4,0},{8,12},{12,8},{16,20},{20,16},{24,28},{28,24},{1,5},{5... | collective-permute-start | bytes 6635528 | tf_op jit(solution)/shard_map/ppermute | solution.py:408
  124.5 11.8 %collective-permute-start.22 = (bf16[256,768]{1,0:T(8,128)(2,1)}, bf16[256,768]{1,0:T(8,128)(2,1)S(1)}, u32[]{:S(2)}, u32[]{:S(2)}) collective-permute-start(bf16[256,768]{1,0:T(8,128)(2,1)} %get-tuple-element.192.own_ref), channel_id=1, source_target_pairs={{0,1},{1,0},{2,3},{3,2},{4,5},{5,4},{6,7},{7,6},{8,9},{9,8},{10,11... | collective-permute-start | bytes 1179656 | tf_op jit(solution)/shard_map/ppermute | solution.py:411
  125.7 10.6 %collective-permute-start.21 = (bf16[256,768]{1,0:T(8,128)(2,1)}, bf16[256,768]{1,0:T(8,128)(2,1)S(1)}, u32[]{:S(2)}, u32[]{:S(2)}) collective-permute-start(bf16[256,768]{1,0:T(8,128)(2,1)} %get-tuple-element.192.own_ref), channel_id=1, source_target_pairs={{0,4},{4,0},{8,12},{12,8},{16,20},{20,16},{24,28},{28,24},{1,5},{5... | collective-permute-start | bytes 1179656 | tf_op jit(solution)/shard_map/ppermute | solution.py:408
  138.0 11.0 %collective-permute-start.24 = (bf16[256,2688]{1,0:T(8,128)(2,1)}, bf16[256,2688]{1,0:T(8,128)(2,1)S(1)}, u32[]{:S(2)}, u32[]{:S(2)}) collective-permute-start(bf16[256,2688]{1,0:T(8,128)(2,1)} %get-tuple-element.197), channel_id=1, source_target_pairs={{0,4},{4,0},{8,12},{12,8},{16,20},{20,16},{24,28},{28,24},{1,5},{5... | collective-permute-start | bytes 4128776 | tf_op jit(solution)/shard_map/ppermute | solution.py:408
  138.2 21.4 %collective-permute-start.1 = (bf16[256,768]{1,0:T(8,128)(2,1)S(1)}, bf16[256,768]{1,0:T(8,128)(2,1)S(1)}, u32[]{:S(2)}, u32[]{:S(2)}) collective-permute-start(bf16[256,768]{1,0:T(8,128)(2,1)S(1)} %copy-done.60), channel_id=1, source_target_pairs={{0,0},{1,4},{2,1},{3,5},{4,2},{5,6},{6,3},{7,7},{8,8},{9,12},{10,9... | collective-permute-start | bytes 1179656 | tf_op jit(solution)/shard_map/ppermute | solution.py:422
  150.2 7.5 %collective-permute-start.25 = (bf16[192,512]{1,0:T(8,128)(2,1)S(1)}, bf16[192,512]{1,0:T(8,128)(2,1)S(1)}, u32[]{:S(2)}, u32[]{:S(2)}) collective-permute-start(bf16[192,512]{1,0:T(8,128)(2,1)S(1)} %slice.444), channel_id=1, source_target_pairs={{0,1},{1,0},{2,3},{3,2},{4,5},{5,4},{6,7},{7,6},{8,9},{9,8},{10,11... | collective-permute-start | bytes 589832 | tf_op jit(solution)/shard_map/ppermute | solution.py:411
  176.5 14.2 %collective-permute-start.28 = (bf16[256,2688]{1,0:T(8,128)(2,1)}, bf16[256,2688]{1,0:T(8,128)(2,1)S(1)}, u32[]{:S(2)}, u32[]{:S(2)}) collective-permute-start(bf16[256,2688]{1,0:T(8,128)(2,1)} %get-tuple-element.208), channel_id=1, source_target_pairs={{0,4},{4,0},{8,12},{12,8},{16,20},{20,16},{24,28},{28,24},{1,5},{5... | collective-permute-start | bytes 4128776 | tf_op jit(solution)/shard_map/ppermute | solution.py:408
  176.9 13.8 %collective-permute-start.27 = (bf16[256,768]{1,0:T(8,128)(2,1)S(1)}, bf16[256,768]{1,0:T(8,128)(2,1)}, u32[]{:S(2)}, u32[]{:S(2)}) collective-permute-start(bf16[256,768]{1,0:T(8,128)(2,1)S(1)} %get-tuple-element.207), channel_id=1, source_target_pairs={{0,4},{4,0},{8,12},{12,8},{16,20},{20,16},{24,28},{28,24},{1,5},{5... | collective-permute-start | bytes 1179656 | tf_op jit(solution)/shard_map/ppermute | solution.py:408
  177.0 13.7 %collective-permute-start.29 = (bf16[256,768]{1,0:T(8,128)(2,1)}, bf16[256,768]{1,0:T(8,128)(2,1)S(1)}, u32[]{:S(2)}, u32[]{:S(2)}) collective-permute-start(bf16[256,768]{1,0:T(8,128)(2,1)} %convert_element_type.325), channel_id=1, source_target_pairs={{0,0},{4,1},{1,2},{5,3},{2,4},{6,5},{3,6},{7,7},{8,8},{12,9},{9,10... | collective-permute-start | bytes 1179656 | tf_op jit(solution)/shard_map/ppermute | solution.py:425
  195.6 8.0 %collective-permute-start.31 = (bf16[192,512]{1,0:T(8,128)(2,1)S(1)}, bf16[192,512]{1,0:T(8,128)(2,1)S(1)}, u32[]{:S(2)}, u32[]{:S(2)}) collective-permute-start(bf16[192,512]{1,0:T(8,128)(2,1)S(1)} %get-tuple-element.419), channel_id=1, source_target_pairs={{0,1},{1,0},{2,3},{3,2},{4,5},{5,4},{6,7},{7,6},{8,9},{9,8},{10,11... | collective-permute-start | bytes 589832 | tf_op jit(solution)/shard_map/ppermute | solution.py:411
  204.4 12.5 %collective-permute-start.32 = (bf16[256,2304]{1,0:T(8,128)(2,1)}, bf16[256,2304]{1,0:T(8,128)(2,1)}, u32[]{:S(2)}, u32[]{:S(2)}) collective-permute-start(bf16[256,2304]{1,0:T(8,128)(2,1)} %get-tuple-element.217), channel_id=1, source_target_pairs={{0,4},{4,0},{8,12},{12,8},{16,20},{20,16},{24,28},{28,24},{1,5},{5... | collective-permute-start | bytes 3538952 | tf_op jit(solution)/shard_map/ppermute | solution.py:408
  221.8 11.4 %collective-permute-start.34 = (bf16[256,768]{1,0:T(8,128)(2,1)S(1)}, bf16[256,768]{1,0:T(8,128)(2,1)S(1)}, u32[]{:S(2)}, u32[]{:S(2)}) collective-permute-start(bf16[256,768]{1,0:T(8,128)(2,1)S(1)} %get-tuple-element.397), channel_id=1, source_target_pairs={{0,1},{1,0},{2,3},{3,2},{4,5},{5,4},{6,7},{7,6},{8,9},{9,8},{10,11... | collective-permute-start | bytes 1179656 | tf_op jit(solution)/shard_map/ppermute | solution.py:411
  244.8 18.9 %collective-permute-start.36 = (bf16[2,2,96,768]{3,2,1,0:T(8,128)(2,1)}, bf16[2,2,96,768]{3,2,1,0:T(8,128)(2,1)S(1)}, u32[]{:S(2)}, u32[]{:S(2)}) collective-permute-start(bf16[2,2,96,768]{3,2,1,0:T(8,128)(2,1)} %slice_bitcast_fusion.7), channel_id=1, source_target_pairs={{0,8},{4,12},{8,0},{12,4},{16,24},{20,28},{24,16},{28,20},{1,9},{5... | collective-permute-start | bytes 1769480 | tf_op jit(solution)/shard_map/ppermute | solution.py:408
  246.1 17.5 %collective-permute-start.37 = (bf16[2,2,96,768]{3,2,1,0:T(8,128)(2,1)}, bf16[2,2,96,768]{3,2,1,0:T(8,128)(2,1)S(1)}, u32[]{:S(2)}, u32[]{:S(2)}) collective-permute-start(bf16[2,2,96,768]{3,2,1,0:T(8,128)(2,1)} %slice_bitcast_fusion.6), channel_id=1, source_target_pairs={{0,16},{4,20},{8,24},{12,28},{16,0},{20,4},{24,8},{28,12},{1,17},{... | collective-permute-start | bytes 1769480 | tf_op jit(solution)/shard_map/ppermute | solution.py:408
  268.8 9.3 %collective-permute-start.41 = (bf16[2,96,768]{2,1,0:T(8,128)(2,1)S(1)}, bf16[2,96,768]{2,1,0:T(8,128)(2,1)}, u32[]{:S(2)}, u32[]{:S(2)}) collective-permute-start(bf16[2,96,768]{2,1,0:T(8,128)(2,1)S(1)} %slice_bitcast_fusion.23), channel_id=1, source_target_pairs={{0,16},{4,20},{8,24},{12,28},{16,0},{20,4},{24,8},{28,12},{1,17},{... | collective-permute-start | bytes 884744 | tf_op jit(solution)/shard_map/ppermute | solution.py:408
  269.3 8.8 %collective-permute-start.42 = (bf16[2,96,768]{2,1,0:T(8,128)(2,1)S(1)}, bf16[2,96,768]{2,1,0:T(8,128)(2,1)S(1)}, u32[]{:S(2)}, u32[]{:S(2)}) collective-permute-start(bf16[2,96,768]{2,1,0:T(8,128)(2,1)S(1)} %slice_bitcast_fusion.22), channel_id=1, source_target_pairs={{0,8},{4,12},{8,0},{12,4},{16,24},{20,28},{24,16},{28,20},{1,9},{5... | collective-permute-start | bytes 884744 | tf_op jit(solution)/shard_map/ppermute | solution.py:408
  270.8 10.2 %collective-permute-start.40 = (bf16[192,512]{1,0:T(8,128)(2,1)}, bf16[192,512]{1,0:T(8,128)(2,1)}, u32[]{:S(2)}, u32[]{:S(2)}) collective-permute-start(bf16[192,512]{1,0:T(8,128)(2,1)} %get-tuple-element.415), channel_id=1, source_target_pairs={{0,1},{1,0},{2,3},{3,2},{4,5},{5,4},{6,7},{7,6},{8,9},{9,8},{10,11... | collective-permute-start | bytes 589832 | tf_op jit(solution)/shard_map/ppermute | solution.py:411
  278.8 20.2 %collective-permute-start.44 = (bf16[2,2,120,768]{3,2,1,0:T(8,128)(2,1)}, bf16[2,2,120,768]{3,2,1,0:T(8,128)(2,1)}, u32[]{:S(2)}, u32[]{:S(2)}) collective-permute-start(bf16[2,2,120,768]{3,2,1,0:T(8,128)(2,1)} %fusion.73), channel_id=1, source_target_pairs={{0,8},{4,12},{8,0},{12,4},{16,24},{20,28},{24,16},{28,20},{1,9},{5... | collective-permute-start | bytes 2211848 | tf_op jit(solution)/shard_map/ppermute | solution.py:408
  279.5 19.6 %collective-permute-start.45 = (bf16[2,2,120,768]{3,2,1,0:T(8,128)(2,1)}, bf16[2,2,120,768]{3,2,1,0:T(8,128)(2,1)}, u32[]{:S(2)}, u32[]{:S(2)}) collective-permute-start(bf16[2,2,120,768]{3,2,1,0:T(8,128)(2,1)} %fusion.69), channel_id=1, source_target_pairs={{0,16},{4,20},{8,24},{12,28},{16,0},{20,4},{24,8},{28,12},{1,17},{... | collective-permute-start | bytes 2211848 | tf_op jit(solution)/shard_map/ppermute | solution.py:408
  284.6 14.5 %collective-permute-start.43 = (bf16[2,96,768]{2,1,0:T(8,128)(2,1)}, bf16[2,96,768]{2,1,0:T(8,128)(2,1)S(1)}, u32[]{:S(2)}, u32[]{:S(2)}) collective-permute-start(bf16[2,96,768]{2,1,0:T(8,128)(2,1)} %fusion.78), channel_id=1, source_target_pairs={{0,1},{1,0},{2,3},{3,2},{4,5},{5,4},{6,7},{7,6},{8,9},{9,8},{10,11... | collective-permute-start | bytes 884744 | tf_op jit(solution)/shard_map/ppermute | solution.py:411
  300.4 3.4 collective-permute-start.46
  307.8 11.0 %collective-permute-start.47 = (bf16[2,120,768]{2,1,0:T(8,128)(2,1)S(1)}, bf16[2,120,768]{2,1,0:T(8,128)(2,1)S(1)}, u32[]{:S(2)}, u32[]{:S(2)}) collective-permute-start(bf16[2,120,768]{2,1,0:T(8,128)(2,1)S(1)} %slice_bitcast_fusion.18), channel_id=1, source_target_pairs={{0,16},{4,20},{8,24},{12,28},{16,0},{20,4},{24,8},{28,12},{1,17},{... | collective-permute-start | bytes 1105928 | tf_op jit(solution)/shard_map/ppermute | solution.py:408
  308.4 10.7 %collective-permute-start.48 = (bf16[2,120,768]{2,1,0:T(8,128)(2,1)S(1)}, bf16[2,120,768]{2,1,0:T(8,128)(2,1)S(1)}, u32[]{:S(2)}, u32[]{:S(2)}) collective-permute-start(bf16[2,120,768]{2,1,0:T(8,128)(2,1)S(1)} %slice_bitcast_fusion.17), channel_id=1, source_target_pairs={{0,8},{4,12},{8,0},{12,4},{16,24},{20,28},{24,16},{28,20},{1,9},{5... | collective-permute-start | bytes 1105928 | tf_op jit(solution)/shard_map/ppermute | solution.py:408
  308.9 14.4 %collective-permute-start.50 = (bf16[256,768]{1,0:T(8,128)(2,1)S(1)}, bf16[256,768]{1,0:T(8,128)(2,1)S(1)}, u32[]{:S(2)}, u32[]{:S(2)}) collective-permute-start(bf16[256,768]{1,0:T(8,128)(2,1)S(1)} %get-tuple-element.284), channel_id=1, source_target_pairs={{0,1},{1,0},{2,3},{3,2},{4,5},{5,4},{6,7},{7,6},{8,9},{9,8},{10,11... | collective-permute-start | bytes 1179656 | tf_op jit(solution)/shard_map/ppermute | solution.py:411
  310.8 16.7 %collective-permute-start.51 = (bf16[96,768]{1,0:T(8,128)(2,1)}, bf16[96,768]{1,0:T(8,128)(2,1)}, u32[]{:S(2)}, u32[]{:S(2)}) collective-permute-start(bf16[96,768]{1,0:T(8,128)(2,1)} %slice_bitcast_fusion.26), channel_id=1, source_target_pairs={{0,2},{1,3},{2,0},{3,1},{4,6},{5,7},{6,4},{7,5},{8,10},{9,11},{10,... | collective-permute-start | bytes 442376 | tf_op jit(solution)/shard_map/ppermute | solution.py:411
  319.1 8.4 %collective-permute-start.52 = (bf16[2,72,768]{2,1,0:T(8,128)(2,1)S(1)}, bf16[2,72,768]{2,1,0:T(8,128)(2,1)}, u32[]{:S(2)}, u32[]{:S(2)}) collective-permute-start(bf16[2,72,768]{2,1,0:T(8,128)(2,1)S(1)} %bitcast.327), channel_id=1, source_target_pairs={{0,8},{4,12},{8,0},{12,4},{16,24},{20,28},{24,16},{28,20},{1,9},{5... | collective-permute-start | bytes 663560 | tf_op jit(solution)/shard_map/ppermute | solution.py:408
  319.6 7.9 %collective-permute-start.53 = (bf16[2,72,768]{2,1,0:T(8,128)(2,1)S(1)}, bf16[2,72,768]{2,1,0:T(8,128)(2,1)}, u32[]{:S(2)}, u32[]{:S(2)}) collective-permute-start(bf16[2,72,768]{2,1,0:T(8,128)(2,1)S(1)} %bitcast.326), channel_id=1, source_target_pairs={{0,16},{4,20},{8,24},{12,28},{16,0},{20,4},{24,8},{28,12},{1,17},{... | collective-permute-start | bytes 663560 | tf_op jit(solution)/shard_map/ppermute | solution.py:408
  321.2 13.6 %collective-permute-start.49 = (bf16[2,120,768]{2,1,0:T(8,128)(2,1)S(1)}, bf16[2,120,768]{2,1,0:T(8,128)(2,1)S(1)}, u32[]{:S(2)}, u32[]{:S(2)}) collective-permute-start(bf16[2,120,768]{2,1,0:T(8,128)(2,1)S(1)} %fusion.75), channel_id=1, source_target_pairs={{0,1},{1,0},{2,3},{3,2},{4,5},{5,4},{6,7},{7,6},{8,9},{9,8},{10,11... | collective-permute-start | bytes 1105928 | tf_op jit(solution)/shard_map/ppermute | solution.py:411
  329.3 5.6 %collective-permute-start.56 = (bf16[72,768]{1,0:T(8,128)(2,1)}, bf16[72,768]{1,0:T(8,128)(2,1)S(1)}, u32[]{:S(2)}, u32[]{:S(2)}) collective-permute-start(bf16[72,768]{1,0:T(8,128)(2,1)} %select_bitcast_fusion), channel_id=1, source_target_pairs={{0,8},{4,12},{8,0},{12,4},{16,24},{20,28},{24,16},{28,20},{1,9},{5... | collective-permute-start | bytes 331784 | tf_op jit(solution)/shard_map/ppermute | solution.py:408
  332.4 5.2 %collective-permute-start.55 = (bf16[72,768]{1,0:T(8,128)(2,1)}, bf16[72,768]{1,0:T(8,128)(2,1)S(1)}, u32[]{:S(2)}, u32[]{:S(2)}) collective-permute-start(bf16[72,768]{1,0:T(8,128)(2,1)} %select_bitcast_fusion.1), channel_id=1, source_target_pairs={{0,16},{4,20},{8,24},{12,28},{16,0},{20,4},{24,8},{28,12},{1,17},{... | collective-permute-start | bytes 331784 | tf_op jit(solution)/shard_map/ppermute | solution.py:408
  338.4 6.0 %collective-permute-start.58 = (f32[12,768]{1,0:T(8,128)S(1)}, f32[12,768]{1,0:T(8,128)S(1)}, u32[]{:S(2)}, u32[]{:S(2)}) collective-permute-start(f32[12,768]{1,0:T(8,128)S(1)} %pad_maximum_fusion.27), channel_id=1, source_target_pairs={{0,4},{4,0},{8,12},{12,8},{16,20},{20,16},{24,28},{28,24},{1,5},{5... | collective-permute-start | bytes 110600 | tf_op jit(solution)/shard_map/ppermute | solution.py:408
  338.6 20.6 %collective-permute-start.57 = (bf16[2,72,768]{2,1,0:T(8,128)(2,1)S(1)}, bf16[2,72,768]{2,1,0:T(8,128)(2,1)S(1)}, u32[]{:S(2)}, u32[]{:S(2)}) collective-permute-start(bf16[2,72,768]{2,1,0:T(8,128)(2,1)S(1)} %pad_maximum_fusion.22), channel_id=1, source_target_pairs={{2,0},{3,1},{4,6},{5,7},{10,8},{11,9},{12,14},{13,15},{18,16},{19,... | collective-permute-start | bytes 663560 | tf_op jit(solution)/shard_map/ppermute | solution.py:436
  340.1 19.1 %collective-permute-start.54 = (bf16[120,768]{1,0:T(8,128)(2,1)S(1)}, bf16[120,768]{1,0:T(8,128)(2,1)S(1)}, u32[]{:S(2)}, u32[]{:S(2)}) collective-permute-start(bf16[120,768]{1,0:T(8,128)(2,1)S(1)} %slice_bitcast_fusion.24), channel_id=1, source_target_pairs={{0,2},{1,3},{2,0},{3,1},{4,6},{5,7},{6,4},{7,5},{8,10},{9,11},{10,... | collective-permute-start | bytes 552968 | tf_op jit(solution)/shard_map/ppermute | solution.py:411
  343.7 23.3 %collective-permute-start.63 = (bf16[256,768]{1,0:T(8,128)(2,1)S(1)}, bf16[256,768]{1,0:T(8,128)(2,1)S(1)}, u32[]{:S(2)}, u32[]{:S(2)}) collective-permute-start(bf16[256,768]{1,0:T(8,128)(2,1)S(1)} %copy-done.64), channel_id=1, source_target_pairs={{0,0},{4,1},{1,2},{5,3},{2,4},{6,5},{3,6},{7,7},{8,8},{12,9},{9,10... | collective-permute-start | bytes 1179656 | tf_op jit(solution)/shard_map/ppermute | solution.py:425
  344.4 4.6 %collective-permute-start.59 = (f32[12,768]{1,0:T(8,128)S(1)}, f32[12,768]{1,0:T(8,128)S(1)}, u32[]{:S(2)}, u32[]{:S(2)}) collective-permute-start(f32[12,768]{1,0:T(8,128)S(1)} %fusion.102), channel_id=1, source_target_pairs={{0,8},{4,12},{8,0},{12,4},{16,24},{20,28},{24,16},{28,20},{1,9},{5... | collective-permute-start | bytes 110600 | tf_op jit(solution)/shard_map/ppermute | solution.py:408
  359.4 8.3 %collective-permute-start.61 = (bf16[1,184,768]{2,1,0:T(8,128)(2,1)S(1)}, bf16[1,184,768]{2,1,0:T(8,128)(2,1)S(1)}, u32[]{:S(2)}, u32[]{:S(2)}) collective-permute-start(bf16[1,184,768]{2,1,0:T(8,128)(2,1)S(1)} %fusion.86), channel_id=1, source_target_pairs={{0,8},{4,12},{8,0},{12,4},{16,24},{20,28},{24,16},{28,20},{1,9},{5... | collective-permute-start | bytes 847880 | tf_op jit(solution)/shard_map/ppermute | solution.py:408
  360.0 7.0 %collective-permute-start.60 = (bf16[1,176,768]{2,1,0:T(8,128)(2,1)S(1)}, bf16[1,176,768]{2,1,0:T(8,128)(2,1)S(1)}, u32[]{:S(2)}, u32[]{:S(2)}) collective-permute-start(bf16[1,176,768]{2,1,0:T(8,128)(2,1)S(1)} %maximum_bitcast_fusion), channel_id=1, source_target_pairs={{0,16},{4,20},{8,24},{12,28},{16,0},{20,4},{24,8},{28,12},{1,17},{... | collective-permute-start | bytes 811016 | tf_op jit(solution)/shard_map/ppermute | solution.py:408
  361.8 5.1 %collective-permute-start.62 = (f32[12,768]{1,0:T(8,128)S(1)}, f32[12,768]{1,0:T(8,128)S(1)}, u32[]{:S(2)}, u32[]{:S(2)}) collective-permute-start(f32[12,768]{1,0:T(8,128)S(1)} %add.209), channel_id=1, source_target_pairs={{0,16},{4,20},{8,24},{12,28},{16,0},{20,4},{24,8},{28,12},{1,17},{... | collective-permute-start | bytes 110600 | tf_op jit(solution)/shard_map/ppermute | solution.py:408
  367.8 14.0 %collective-permute-start.65 = (bf16[2,184,768]{2,1,0:T(8,128)(2,1)S(1)}, bf16[2,184,768]{2,1,0:T(8,128)(2,1)S(1)}, u32[]{:S(2)}, u32[]{:S(2)}) collective-permute-start(bf16[2,184,768]{2,1,0:T(8,128)(2,1)S(1)} %maximum_select_fusion.5), channel_id=1, source_target_pairs={{0,16},{4,20},{8,24},{12,28},{16,0},{20,4},{24,8},{28,12},{1,17},{... | collective-permute-start | bytes 1695752 | tf_op jit(solution)/shard_map/ppermute | solution.py:408
  369.8 12.0 %collective-permute-start.64 = (bf16[2,176,768]{2,1,0:T(8,128)(2,1)S(1)}, bf16[2,176,768]{2,1,0:T(8,128)(2,1)S(1)}, u32[]{:S(2)}, u32[]{:S(2)}) collective-permute-start(bf16[2,176,768]{2,1,0:T(8,128)(2,1)S(1)} %maximum_select_fusion.6), channel_id=1, source_target_pairs={{0,8},{4,12},{8,0},{12,4},{16,24},{20,28},{24,16},{28,20},{1,9},{5... | collective-permute-start | bytes 1622024 | tf_op jit(solution)/shard_map/ppermute | solution.py:408
  371.4 4.5 %collective-permute-start.66 = (f32[12,768]{1,0:T(8,128)S(1)}, f32[12,768]{1,0:T(8,128)S(1)}, u32[]{:S(2)}, u32[]{:S(2)}) collective-permute-start(f32[12,768]{1,0:T(8,128)S(1)} %add.210), channel_id=1, source_target_pairs={{0,1},{1,0},{2,3},{3,2},{4,5},{5,4},{6,7},{7,6},{8,9},{9,8},{10,11... | collective-permute-start | bytes 110600 | tf_op jit(solution)/shard_map/ppermute | solution.py:411
  371.4 5.1 %collective-permute-start.67 = (f32[12,768]{1,0:T(8,128)S(1)}, f32[12,768]{1,0:T(8,128)S(1)}, u32[]{:S(2)}, u32[]{:S(2)}) collective-permute-start(f32[12,768]{1,0:T(8,128)S(1)} %add.210), channel_id=1, source_target_pairs={{0,2},{1,3},{2,0},{3,1},{4,6},{5,7},{6,4},{7,5},{8,10},{9,11},{10,... | collective-permute-start | bytes 110600 | tf_op jit(solution)/shard_map/ppermute | solution.py:411
  372.6 5.9 %collective-permute-start.68 = (f32[12,768]{1,0:T(8,128)S(1)}, f32[12,768]{1,0:T(8,128)S(1)}, u32[]{:S(2)}, u32[]{:S(2)}) collective-permute-start(f32[12,768]{1,0:T(8,128)S(1)} %add.210), channel_id=1, source_target_pairs={{0,3},{1,2},{2,1},{3,0},{4,7},{5,6},{6,5},{7,4},{8,11},{9,10},{10,... | collective-permute-start | bytes 110600 | tf_op jit(solution)/shard_map/ppermute | solution.py:411
  382.0 4.9 %collective-permute-start.70 = (bf16[2,2,184,768]{3,2,1,0:T(8,128)(2,1)S(1)}, bf16[2,2,184,768]{3,2,1,0:T(8,128)(2,1)S(1)}, u32[]{:S(2)}, u32[]{:S(2)}) collective-permute-start(bf16[2,2,184,768]{3,2,1,0:T(8,128)(2,1)S(1)} %maximum_select_fusion.2), channel_id=1, source_target_pairs={{0,4},{4,0},{8,12},{12,8},{16,20},{20,16},{24,28},{28,24},{1,5},{5... | collective-permute-start | bytes 3391496 | tf_op jit(solution)/shard_map/ppermute | solution.py:408
  382.3 4.6 %collective-permute-start.69 = (bf16[2,2,176,768]{3,2,0,1:T(8,128)(2,1)S(1)}, bf16[2,2,176,768]{3,2,0,1:T(8,128)(2,1)}, u32[]{:S(2)}, u32[]{:S(2)}) collective-permute-start(bf16[2,2,176,768]{3,2,0,1:T(8,128)(2,1)S(1)} %fusion.57), channel_id=1, source_target_pairs={{0,4},{4,0},{8,12},{12,8},{16,20},{20,16},{24,28},{28,24},{1,5},{5... | collective-permute-start | bytes 3244040 | tf_op jit(solution)/shard_map/ppermute | solution.py:408
  (89 other events, 510.6 us)

commit v2 on v1

--- a/solution.py
+++ b/solution.py
@@ -227,7 +227,7 @@
 
 def feed_kernel(
     att_ref, stream_ref, out_w_ref, fc_ref, proj_ref, vec_ref, bias_ref,
-    mid_ref, low_ref, act_ref, heads_ref, send_ref, slope_ref, next_ref, norm_ref,
+    mid_ref, low_ref, act_ref, heads_ref, send_ref, slope_ref, next_ref, norm_ref, last_ref,
 ):
     step_at = pl.program_id(0)
     width = mid_ref.shape[1]
@@ -259,6 +259,7 @@
     @pl.when(step_at == pl.num_programs(0) - 1)
     def _():
         norm_ref[...] = normalize(next_ref[...], vec_ref[4:5, :], vec_ref[5:6, :]).astype(BF)
+        last_ref[...] = next_ref[...].astype(BF)
 
 
 def feed(attended, stream, w, vectors):
@@ -277,6 +278,7 @@
         out_specs=[
             whole((rows, width)), whole((rows, width)), whole((rows, hidden // 2)), whole((rows, width // 2)),
             whole((rows, hidden // 2 + width + width // 2)), block, whole((rows, width)), whole((rows, width)),
+            whole((rows, width)),
         ],
         out_shape=[
             jax.ShapeDtypeStruct((rows, width), F32),
@@ -287,6 +289,7 @@
             jax.ShapeDtypeStruct((rows, hidden), F32),
             jax.ShapeDtypeStruct((rows, width), F32),
             jax.ShapeDtypeStruct((rows, width), BF),
+            jax.ShapeDtypeStruct((rows, width), BF),
         ],
         cost_estimate=pl.CostEstimate(
             flops=4 * rows * width * hidden, bytes_accessed=6 * width * hidden, transcendentals=rows * hidden
@@ -300,7 +303,6 @@
     pre_ref, send_ref, bias_ref, back_ref, low_ref, heads_ref, sums_ref, acc_ref,
 ):
     step_at = pl.program_id(0)
-    hidden = pre_ref.shape[1]
     pre = (dot(grad_ref[...].astype(BF), proj_ref[...], 1, 1) * slope_ref[...]).astype(BF)
     keep_or_send(step_at, pre, pre_ref, send_ref)
     bias_ref[...] = jnp.sum(pre.astype(F32), axis=0, keepdims=True)
@@ -322,7 +324,6 @@
         back_ref[...] = back
         low = back.astype(BF)
         low_ref[...] = low
-        send_ref[:, hidden:] = low
         heads_ref[...] = dot(out_w_ref[...], low, 1, 1).astype(BF)
         sums_ref[0:1, :] = jnp.sum(back, axis=0, keepdims=True)
         sums_ref[1:2, :] = gain_sum
@@ -344,13 +345,13 @@
             whole((1, width)),
         ],
         out_specs=[
-            whole((rows, hidden // 2)), whole((rows, hidden // 2 + width)),
+            whole((rows, hidden // 2)), whole((rows, hidden // 2)),
             pl.BlockSpec((1, step_size), lambda j: (0, j)), whole((rows, width)), whole((rows, width)),
             whole((width, rows)), whole((4, width)),
         ],
         out_shape=[
             jax.ShapeDtypeStruct((rows, hidden // 2), BF),
-            jax.ShapeDtypeStruct((rows, hidden // 2 + width), BF),
+            jax.ShapeDtypeStruct((rows, hidden // 2), BF),
             jax.ShapeDtypeStruct((1, hidden), F32),
             jax.ShapeDtypeStruct((rows, width), F32),
             jax.ShapeDtypeStruct((rows, width), BF),
@@ -393,6 +394,74 @@
     )(own, far, grad_middle, stream, gain)
 
 
+def finish_kernel(
+    scalar_ref, one_ref, two_ref, one_far_ref, two_far_ref, low_ref,
+    fc_ref, out_ref, proj_ref, qkv_ref, tokens_ref,
+):
+    units = fc_ref.shape[1] // 4
+    count = units + 8
+    rest = proj_ref.shape[0] // 4 + out_ref.shape[0] // 4 - 8
+    y = pl.program_id(0)
+    size = one_ref.shape[2] - count
+    fc = []
+    for x in range(2):
+        one = one_ref[x, 0].astype(F32)
+        two = two_ref[0, x].astype(F32)
+        one_far = one_far_ref[x, 0].astype(F32)
+        two_far = two_far_ref[0, x].astype(F32)
+        mine = scalar_ref[1] == 1
+        first = jnp.where(mine, one[count:], one_far[count:])
+        second = jnp.where(mine, two[rest:], two_far[rest:])
+        qkv_ref[pl.ds(pl.multiple_of((2 * x + y) * size, 8), size), :] = first
+        qkv_ref[pl.ds(pl.multiple_of((4 + 2 * y + x) * size, 8), size), :] = second
+        for core in range(2):
+            own = scalar_ref[0] == core
+            left = jnp.where(own, one[:count], one_far[:count])
+            right = jnp.where(own, two[:rest], two_far[:rest])
+            fc.append(left[:units])
+            piece = 2 * x + core
+            middle = rest - units
+            row = piece * (middle + 8)
+            out_ref[row : row + 8, :] = left[units:]
+            out_ref[row + 8 : row + 8 + middle, :] = right[:middle]
+            proj_ref[piece * units : (piece + 1) * units, :] = right[middle:]
+    fc_ref[...] = jnp.concatenate(fc).T
+    tokens_ref[...] = low_ref[...].astype(F32)
+
+
+def finish(scalars, one, two, one_far, two_far, low, units, outs):
+    tokens, width = low.shape
+    size = one.shape[2] - (units + 8)
+
+    def block(value, first):
+        if first:
+            return pl.BlockSpec((2, 1) + value.shape[2:], lambda y: (0, y, 0, 0))
+        return pl.BlockSpec((1, 2) + value.shape[2:], lambda y: (y, 0, 0, 0))
+
+    return pl.pallas_call(
+        finish_kernel,
+        grid=(2,),
+        in_specs=[SM] + [block(one, True), block(two, False), block(one_far, True), block(two_far, False)]
+        + [pl.BlockSpec((tokens // 2, width), lambda y: (y, 0))],
+        out_specs=[
+            pl.BlockSpec((width, 4 * units), lambda y: (0, y)),
+            pl.BlockSpec((4 * outs, width), lambda y: (y, 0)),
+            pl.BlockSpec((4 * units, width), lambda y: (y, 0)),
+            whole((8 * size, width)),
+            pl.BlockSpec((tokens // 2, width), lambda y: (y, 0)),
+        ],
+        out_shape=[
+            jax.ShapeDtypeStruct((width, 8 * units), F32),
+            jax.ShapeDtypeStruct((8 * outs, width), F32),
+            jax.ShapeDtypeStruct((8 * units, width), F32),
+            jax.ShapeDtypeStruct((8 * size, width), F32),
+            jax.ShapeDtypeStruct((tokens, width), F32),
+        ],
+        cost_estimate=pl.CostEstimate(flops=0, bytes_accessed=16 * 8 * units * width, transcendentals=0),
+        name="finish",
+    )(scalars, one, two, one_far, two_far, low)
+
+
 class Place:
     def __init__(self, members, shards):
         self.members = members
@@ -556,8 +625,8 @@
     if fed is not None:
         attended, fed = tie(attended, fed)
     attended = from_heads(place, heads_to_rows(place, attended))
-    middle, normed2, activated, heads, send, slope, result, normed = feed(attended, stream, w, w["vectors"])
-    return result, normed, (stream, rows, qkv, log_sums, middle, slope), (normed2, activated, heads), send, fed
+    middle, normed2, activated, heads, send, slope, result, normed, last = feed(attended, stream, w, w["vectors"])
+    return result, normed, (stream, rows, qkv, log_sums, middle, slope), (normed2, activated, heads), send, fed, last
 
 
 def pieces(value):
@@ -584,16 +653,16 @@
     )
     grad_heads, send, low_near, fed, output = tie(grad_heads, send, low_near, fed, output)
     pair = rows_to_pair(place, to_heads(place, grad_heads))
-    grad_attended, send = tie(pair_to_heads(place, pair), send)
-    near = place.dp(send, 1)
+    grad_attended, send, mid_low = tie(pair_to_heads(place, pair), send, mid_low)
+    near, mid_near = place.dp(send, 1), place.dp(mid_low, 1)
     grad_qkv, qkv_sums, parts = attend_back(scalars, qkv, grad_attended, log_sums, w["qkv"])
-    parts, near = tie(parts, near)
+    parts, near, mid_near = tie(parts, near, mid_near)
     parts = parts.reshape(4, -1, parts.shape[1])
     moved = place.dp(jnp.stack([parts[1], parts[3]]), 1)
     far = place.tensor(plus(parts[2], moved[1]), 1)
     own = parts[0].astype(F32) + moved[0].astype(F32)
     gradient_in, low_in, norms = norm_back(own, far, grad_middle, stream, w["ln1_gain"])
-    later = (low, low_near, grad_pre, mid_low, near, grad_qkv, rows)
+    later = (low, low_near, grad_pre, mid_low, near, mid_near, grad_qkv, rows)
     return gradient_in, low_in, later, (norms, sums, bias, qkv_sums), output, fed
 
 
@@ -614,7 +683,7 @@
 def first_backward(place, gradient, low, scalars, w, cache, products, later, later_small):
     stream, rows, qkv, log_sums, middle, slope = cache
     (norm_one, act_one, heads_one, near_one), (norm_two, act_two, heads_two, near_two) = products
-    low_two, low_near_two, pre_two, mid_two, back_two, grad_qkv_two, rows_two = later
+    low_two, low_near_two, pre_two, mid_two, pre_near_two, mid_near_two, grad_qkv_two, rows_two = later
     hidden = act_one.shape[1]
     width = low.shape[1]
     heads = qkv.shape[0] // 3
@@ -632,18 +701,18 @@
 
     grad_heads, send, grad_pre, mid_low, *proj_moved = tie(grad_heads, send, grad_pre, mid_low, *proj_moved)
     pair = rows_to_pair(place, to_heads(place, grad_heads))
-    near = place.dp(send, 1)
+    near, mid_near = place.dp(send, 1), place.dp(mid_low, 1)
     proj1, proj0, over_y, over_x = step_two(place, proj, proj_moved)
-    pair, over_y, over_x, near = tie(pair, over_y, over_x, near)
+    pair, over_y, over_x, near, mid_near = tie(pair, over_y, over_x, near, mid_near)
     grad_attended = pair_to_heads(place, pair)
     proj_moved = place.dp(over_y, 4), place.dp(over_x, 2)
     fc = over_tokens(
-        (grad_pre, near[:, :hidden], pre_two, back_two[:, :hidden]),
+        (grad_pre, near, pre_two, pre_near_two),
         (norm_one, near_one[:, hidden : hidden + width], norm_two, near_two[:, hidden : hidden + width]),
     )
     out = over_tokens(
         (heads_one, near_one[:, hidden + width :], heads_two, near_two[:, hidden + width :]),
-        (mid_low, near[:, hidden:], mid_two, back_two[:, hidden:]),
+        (mid_low, mid_near, mid_two, mid_near_two),
     )
     fc = jnp.concatenate([pieces(fc), pieces(out)], 4)
     send_x, send_y = first_step(place, fc)
@@ -679,21 +748,19 @@
     fc1, own = tie(fc1, own)
     fc_t = place.tensor(fc1, 1)
     gradient_in, low, norms = norm_back(own, far, grad_middle, stream, w["ln1_gain"])
-    low, proj_t, qkv_x, qkv_y, bias, qkv_sums, sums = tie(low, proj_t, qkv_x, qkv_y, bias, qkv_sums, sums)
+    fc_t, proj, proj_t, low, bias, qkv_sums, sums = tie(fc_t, proj, proj_t, low, bias, qkv_sums, sums)
+    fc = plus(fc0, fc_t)
+    fc_send, qkv_x, qkv_y = tie(fc[1], qkv_x, qkv_y)
+    fc_t = place.tensor(fc_send, 2)
     keep_x, send_x = choose(place.d & 4, plus(keep_x, qkv_x))
     qkv_x = place.dp(send_x, 4)
     keep_y, send_y = choose(place.d & 2, plus(keep_y, qkv_y))
     qkv_y = place.dp(send_y, 2)
-    fc_t, proj, proj_t, low = tie(fc_t, proj, proj_t, low)
-    fc = plus(fc0, fc_t)
-    fc_t = place.tensor(fc[1], 2)
     low, sums, bias, qkv_sums, qkv_x, qkv_y = tie(low, sums, bias, qkv_sums, qkv_x, qkv_y)
     both = jnp.stack([plus(keep_x, qkv_x), plus(keep_y, qkv_y)])
     for bit in place.extra:
         both = plus(both, place.dp(both, bit))
     both_far = place.cross(both, False)
-    both, low = tie(both, low)
-    placed = place.unplace(low)
     small = [a + b for a, b in zip((norms, sums, bias, qkv_sums), later_small)]
     small = pack_small(place, small, heads)
     small = small + place.dp(small, 1)
@@ -703,36 +770,33 @@
     for bit in place.extra:
         large = plus(large, place.dp(large, bit))
     both = plus(both, both_far)
-    count = large.shape[0] // 16 * 8
+    out_rows = width // (4 * BLOCKS)
+    count = (large.shape[0] - out_rows) // 2 + 8
     one = jnp.concatenate([large[:count], both[0]])[None]
     two = jnp.concatenate([large[count:], both[1]])[None]
-    one, two, small, small_far = tie(one, two, small, small_far)
+    one, two, small, small_far, low = tie(one, two, small, small_far, low)
     one_far, two_far = place.dp(one, 4), place.dp(two, 2)
+    placed = place.unplace(low)
     small = small + small_far
     small_far = place.dp(small, 4)
-    one, two, one_far, two_far, small_far, placed = tie(one, two, one_far, two_far, small_far, placed)
+    one, two, one_far, two_far, small_far = tie(one, two, one_far, two_far, small_far)
     small = small + small_far
     one = ordered(place.d & 4, one, one_far)
     two = ordered(place.d & 2, two, two_far)
     one_far, two_far = place.dp(one, 2), place.dp(two, 4)
     small_far = [place.tensor(small, bit) for bit in (1, 2, 3)]
-    one, two, one_far, two_far, *small_far = tie(one, two, one_far, two_far, *small_far)
+    one, two, one_far, two_far, placed, *small_far = tie(one, two, one_far, two_far, placed, *small_far)
     small = small + small_far[0] + small_far[1] + small_far[2]
     bit = 8
     while bit < place.members:
         small = small + place.dp(small, bit)
         bit *= 2
-    one = ordered(place.d & 2, one[None], one_far[None]).swapaxes(0, 1)
+    one = ordered(place.d & 2, one[None], one_far[None])
     two = ordered(place.d & 4, two[None], two_far[None])
-    one, two, one_far, two_far = tie(one, two, place.dp(one, 1), place.dp(two, 1))
-    rest = large.shape[0] - count
-    mine = place.seq == place.core
-    first = jnp.where(mine, one[:, :, count:], one_far[:, :, count:])
-    second = jnp.where(mine, two[:, :, rest:], two_far[:, :, rest:])
-    full = jnp.concatenate([first.swapaxes(0, 1).reshape(-1, width), second.reshape(-1, width)])
-    one = ordered(place.d & 1, one[:, :, None, :count], one_far[:, :, None, :count], 2)
-    two = ordered(place.d & 1, two[:, :, None, :rest], two_far[:, :, None, :rest], 2)
-    return placed, one.reshape(BLOCKS, count, width), two.reshape(BLOCKS, rest, width), full, small
+    scalars = jnp.stack([place.d & 1, (place.seq == place.core).astype(jnp.int32)])
+    units = count - 8
+    results = finish(scalars, one, two, place.dp(one, 1), place.dp(two, 1), placed, units, out_rows)
+    return results, small
 
 
 def pack_small(place, small, heads):
@@ -792,29 +856,25 @@
     )
     scalars = jnp.concatenate([length, place.quarter[None]])
     normed = normalize(stream, ln1_gain, ln1_shift).astype(BF)
-    layer_one, normed, cache_first, one, fed, _ = layer_forward(place, stream, normed, scalars, w, None)
-    layer_two, _, cache_second, two, fed_two, near_one = layer_forward(place, layer_one, normed, scalars, w, fed)
+    layer_one, normed, cache_first, one, fed, _, _ = layer_forward(place, stream, normed, scalars, w, None)
+    _, _, cache_second, two, fed_two, near_one, last = layer_forward(
+        place, layer_one, normed, scalars, w, fed
+    )
     position = place.quarter * row_total + lax.broadcasted_iota(jnp.int32, (row_total, 1), 0)
     gradient = jnp.where(position < length[0], place.place(cotangent).astype(F32), 0.0)
     gradient, low, later, later_small, output, near_two = second_backward(
-        place, gradient, scalars, w, cache_second, layer_two.astype(BF), fed_two
+        place, gradient, scalars, w, cache_second, last, fed_two
     )
     products = (*one, near_one), (*two, near_two)
-    placed, one, two, g_qkv, packed = first_backward(
+    (g_fc, g_out, g_proj, g_qkv, grad_tokens), packed = first_backward(
         place, gradient, low, scalars, w, cache_first, products, later, later_small
     )
-    grad_tokens = placed.astype(F32)
     g_qkv = g_qkv.reshape(3, heads, width).transpose(0, 2, 1)
-    total = units + w_out.shape[0] // BLOCKS
-    split_at = one.shape[1]
-    g_fc = one[:, :units].reshape(-1, width)
-    g_out = jnp.concatenate([one[:, units:], two[:, : total - split_at]], 1).reshape(-1, width)
-    g_proj = two[:, total - split_at :].reshape(-1, width)
     grad_bfc = lax.dynamic_index_in_dim(packed, 6 + place.t, 0, keepdims=False)
     grad_bqv = lax.dynamic_index_in_dim(packed[10:].reshape(2, 4, -1), place.t, 1, keepdims=False)
     return (
-        output, grad_tokens, packed[0], packed[1], g_qkv.astype(F32), grad_bqv, g_out.astype(F32),
-        packed[2], packed[3], packed[4], g_fc.T.astype(F32), grad_bfc, g_proj.astype(F32), packed[5],
+        output, grad_tokens, packed[0], packed[1], g_qkv, grad_bqv, g_out,
+        packed[2], packed[3], packed[4], g_fc, grad_bfc, g_proj, packed[5],
     )
 
 

time: 410 us -> 395 us (0.963)
  other arithmetic: 65.4 us -> 51.7 us
  local copies, waits for them, and re-layouts: 48.5 us -> 37.7 us
  waiting for transfers between devices: 88.3 us -> 95.4 us
  starting transfers between devices: 84.9 us -> 79.7 us
  Pallas kernels: 102 us -> 107 us
    convert_element_type x6 -> x0, other arithmetic: 7.96 us -> none  [the longest x1 1.93 us: on_device(): grad_tokens = placed.astype(F32)]
    slice x9 -> x0, local copies, waits for them, and re-layouts: 5.45 us -> none  [the longest x1 2.08 us: first_backward(): back_two[:, :hidden]]
    ppermute x2, waiting for transfers between devices: 0.01 us -> 4.98 us  [cross(): return lax.ppermute(value, ('dp', 'tensor'), pairs)]
    pallas_call x0 -> x1, Pallas kernels: none -> 4.97 us  [finish(): pl.pallas_call(finish_kernel, grid=(2,), in_specs=[SM] + [block(one, True...]
    ppermute x19, starting transfers between devices: 37.6 us -> 32.9 us  [tensor(): lax.ppermute(value, 'tensor', [(i, i ^ bit) for i in range(self.shards)])]
    unnamed x159 -> x138, local copies, waits for them, and re-layouts: 13.6 us -> 11.1 us
    ppermute x46 -> x48, waiting for transfers between devices: 36.7 us -> 35.4 us  [dp(): lax.ppermute(value, 'dp', [(i, i ^ bit) for i in range(self.members)])]
    ppermute x46 -> x48, starting transfers between devices: 35.8 us -> 35.3 us  [dp(): lax.ppermute(value, 'dp', [(i, i ^ bit) for i in range(self.members)])]
  transfers between devices with their start and end apart: 71 -> 73, of which waited for: 26 -> 30; matrix products, arithmetic and copies ran while one was open for 18% -> 18% of each run, Pallas kernels for 18% -> 19%
where the time goes in v2:
time: 395 us; the launch traced here: 387 us
  Pallas kernels  107 us (27%)
  waiting for transfers between devices  95.4 us (24%)
  starting transfers between devices  79.7 us (20%)
  other arithmetic  51.7 us (13%)
  local copies, waits for them, and re-layouts  37.7 us (10%)
  matrix products  11.4 us (3%)
  between operations  4.11 us (1%)
    ppermute x19, waiting for transfers between devices, tensor(): lax.ppermute(value, 'tensor', [(i, i ^ bit) for i in range(self.shards)])  55 us
    ppermute x48, waiting for transfers between devices, dp(): lax.ppermute(value, 'dp', [(i, i ^ bit) for i in range(self.members)])  35.4 us
    ppermute x48, starting transfers between devices, dp(): lax.ppermute(value, 'dp', [(i, i ^ bit) for i in range(self.members)])  35.3 us
    ppermute x19, starting transfers between devices, tensor(): lax.ppermute(value, 'tensor', [(i, i ^ bit) for i in range(self.shards)])  32.9 us
    pallas_call x2, Pallas kernels, feed(): pl.pallas_call(feed_kernel, grid=(hidden // step_size,), in_specs=[whole(...  25.9 us
    pallas_call x2, Pallas kernels, attend_back(): pl.pallas_call(attend_back_kernel, in_specs=[SM] + [VM] * 4, out_specs=[V...  25.2 us
    pallas_call x2, Pallas kernels, feed_back(): pl.pallas_call(feed_back_kernel, grid=(hidden // step_size,), in_specs=[w...  23.8 us
    pallas_call x2, Pallas kernels, attend(): pl.pallas_call(attend_kernel, in_specs=[SM] + [VM] * 6, out_specs=[VM] *...  20.7 us
  transfers between devices with their start and end apart: 73, of which 30 were waited for; matrix products, arithmetic and copies ran while one was open for 18% of the time, Pallas kernels for 19%

profile of v2, /device:TPU:0, one launch (start us, length us, event | category | flops | bytes accessed | tf_op | source)
XLA Modules:
  0.0 387.3 jit_solution(13323239149083018028)
XLA Ops:
  0.7 1.6 copy.94
  2.6 4.1 %collective-permute-start.16 = (bf16[104,768]{1,0:T(8,128)(2,1)S(1)}, bf16[104,768]{1,0:T(8,128)(2,1)S(1)}, u32[]{:S(2)}, u32[]{:S(2)}) collective-permute-start(bf16[104,768]{1,0:T(8,128)(2,1)S(1)} %concatenate.170), channel_id=1, source_target_pairs={{0,2},{1,3},{2,0},{3,1},{4,6},{5,7},{6,4},{7,5},{8,10},{9,11},{10,... | collective-permute-start | bytes 479240 | tf_op jit(solution)/shard_map/ppermute | solution.py:480
  10.3 5.5 %collective-permute-start.6 = (bf16[152,768]{1,0:T(8,128)(2,1)}, bf16[152,768]{1,0:T(8,128)(2,1)}, u32[]{:S(2)}, u32[]{:S(2)}) collective-permute-start(bf16[152,768]{1,0:T(8,128)(2,1)} %fusion.86), channel_id=1, source_target_pairs={{0,2},{1,3},{6,4},{7,5},{8,10},{9,11},{14,12},{15,13},{16,18},{17,... | collective-permute-start | bytes 700424 | tf_op jit(solution)/shard_map/ppermute | solution.py:505
  15.8 1.6 collective-permute-start.2
  17.7 2.0 reverse_select_fusion.2
  27.4 2.5 collective-permute-start.17
  30.0 1.7 collective-permute-start.7
  33.1 4.5 %collective-permute-start.4 = (bf16[256,768]{1,0:T(8,128)(2,1)}, bf16[256,768]{1,0:T(8,128)(2,1)}, u32[]{:S(2)}, u32[]{:S(2)}) collective-permute-start(bf16[256,768]{1,0:T(8,128)(2,1)} %add_convert_fusion.own_ref), channel_id=1, source_target_pairs={{0,1},{1,0},{2,3},{3,2},{4,5},{5,4},{6,7},{7,6},{8,9},{9,8},{10,11... | collective-permute-start | bytes 1179656 | tf_op jit(solution)/shard_map/ppermute | solution.py:480
  38.6 2.0 maximum_select_fusion.5
  44.6 2.4 collective-permute-done.12
  49.6 1.8 constant_dynamic-update-slice_fusion.4
  51.5 3.7 collective-permute-done.4.far_ref
  57.6 1.9 fusion.57
  59.6 6.6 %collective-permute-done.13 = bf16[3,120,768]{2,1,0:T(8,128)(2,1)S(1)} collective-permute-done((bf16[3,120,768]{2,1,0:T(8,128)(2,1)S(1)}, bf16[3,120,768]{2,1,0:T(8,128)(2,1)S(1)}, u32[]{:S(2)}, u32[]{:S(2)}) %collective-permute-start.13) | collective-permute-done | bytes 552992 | tf_op jit(solution)/shard_map/ppermute | solution.py:477
  70.7 10.5 %attend.2 = (bf16[1024,768]{1,0:T(8,128)(2,1)}, bf16[576,1024]{1,0:T(8,128)(2,1)}, bf16[192,1024]{1,0:T(8,128)(2,1)}, f32[3,1024]{1,0:T(4,128)}) custom-call(s32[2]{0:T(128)} %pad_add_fusion.scalar_ref, bf16[256,768]{1,0:T(8,128)(2,1)} %add_convert_fusion.own_ref, bf16[256,768]{1,0:T(8,128)(2,1)} %collective-permute-done.3.near_ref, ...), custom_call_target="tpu_custom_call" | custom-call | flops 2113929216 | bytes 4718592 | tf_op jit(solution)/shard_map/attend/pallas_call | solution.py:113
  82.2 2.5 collective-permute-start.9
  85.7 2.7 collective-permute-done.9
  89.1 2.5 pad_maximum_fusion.2
  93.1 2.1 fusion.105
  95.3 1.6 pad_maximum_fusion.1
  101.1 4.6 %maximum_maximum_fusion = bf16[8,4,96,768]{3,2,1,0:T(8,128)(2,1)} fusion(bf16[4,3,96,768]{3,2,1,0:T(8,128)(2,1)} %collective-permute-done.20, bf16[2,3,96,768]{3,2,1,0:T(8,128)(2,1)} %collective-permute-done.19, bf16[1,3,96,768]{3,2,1,0:T(8,128)(2,1)S(1)} %bitcast.258, bf16[1,3,96,768]{3,2,1,0:T(8,128)(2,1)S(1)} %fusion.113, ...), kind=kLoop, calls=%fused_computation | loop fusion | flops 9437184 | bytes 9437184 | tf_op jit(solution)/shard_map/concatenate | solution.py:847
  105.8 1.8 constant_dynamic-update-slice_fusion
  108.0 2.6 pad_maximum_fusion
  111.8 13.0 %feed.2 = (f32[256,768]{1,0:T(8,128)}, bf16[256,768]{1,0:T(8,128)(2,1)}, bf16[256,1536]{1,0:T(8,128)(2,1)}, bf16[256,384]{1,0:T(8,128)(2,1)}, bf16[256,2688]{1,0...) custom-call(bf16[768,256]{1,0:T(8,128)(2,1)} %bitcast.273, ...), custom_call_target="tpu_custom_call" | custom-call | flops 2415919104 | bytes 14155776 | tf_op jit(solution)/shard_map/feed/pallas_call | solution.py:271
  126.1 10.5 %collective-permute-done.22.far_ref = bf16[256,768]{1,0:T(8,128)(2,1)S(1)} collective-permute-done((bf16[256,768]{1,0:T(8,128)(2,1)}, bf16[256,768]{1,0:T(8,128)(2,1)S(1)}, u32[]{:S(2)}, u32[]{:S(2)}) %collective-permute-start.22) | collective-permute-done | bytes 393248 | tf_op jit(solution)/shard_map/ppermute | solution.py:480
  136.6 1.7 collective-permute-done.23.both_ref
  139.1 10.1 %attend.3 = (bf16[1024,768]{1,0:T(8,128)(2,1)}, bf16[576,1024]{1,0:T(8,128)(2,1)}, bf16[192,1024]{1,0:T(8,128)(2,1)}, f32[3,1024]{1,0:T(4,128)}) custom-call(s32[2]{0:T(128)} %pad_add_fusion.scalar_ref, bf16[256,768]{1,0:T(8,128)(2,1)} %get-tuple-element.194.own_ref, bf16[256,768]{1,0:T(8,128)(2,1)} %copy-done.57, bf16[256,768]{1,0:T(8,128)(2,1)} %copy-done.56, ...), custom_call_target="tpu_custom_call" | custom-call | flops 2113929216 | bytes 4718592 | tf_op jit(solution)/shard_map/attend/pallas_call | solution.py:113
  150.4 3.3 collective-permute-start.25
  154.7 3.3 collective-permute-done.25
  158.0 1.8 collective-permute-start.26
  162.0 12.9 %feed.3 = (f32[256,768]{1,0:T(8,128)}, bf16[256,768]{1,0:T(8,128)(2,1)}, bf16[256,1536]{1,0:T(8,128)(2,1)}, bf16[256,384]{1,0:T(8,128)(2,1)}, bf16[256,2688]{1,0...) custom-call(bf16[768,256]{1,0:T(8,128)(2,1)} %bitcast.274, ...), custom_call_target="tpu_custom_call" | custom-call | flops 2415919104 | bytes 14155776 | tf_op jit(solution)/shard_map/feed/pallas_call | solution.py:271
  175.5 1.6 collective-permute-start.29
  177.2 11.9 %feed_back.2 = (bf16[256,1536]{1,0:T(8,128)(2,1)}, bf16[256,1536]{1,0:T(8,128)(2,1)}, f32[1,3072]{1,0:T(1,128)}, f32[256,768]{1,0:T(8,128)}, bf16[256,768]{1,0:T...) custom-call(f32[256,768]{1,0:T(8,128)} %get-tuple-element.204.grad_ref, ...), custom_call_target="tpu_custom_call" | custom-call | flops 2415919104 | bytes 14155776 | tf_op jit(solution)/shard_map/feed_back/pallas_call | solution.py:340
  190.8 2.1 collective-permute-start.30
  194.0 2.6 collective-permute-start.31
  196.6 5.3 %collective-permute-done.31 = bf16[192,512]{1,0:T(8,128)(2,1)S(1)} collective-permute-done((bf16[192,512]{1,0:T(8,128)(2,1)S(1)}, bf16[192,512]{1,0:T(8,128)(2,1)S(1)}, u32[]{:S(2)}, u32[]{:S(2)}) %collective-permute-start.31) | collective-permute-done | bytes 196640 | tf_op jit(solution)/shard_map/ppermute | solution.py:480
  203.2 12.5 %attend_back.2 = (bf16[576,1024]{1,0:T(8,128)(2,1)}, f32[576,1]{1,0:T(8,128)}, bf16[1024,768]{1,0:T(8,128)(2,1)}) custom-call(s32[2]{0:T(128)} %pad_add_fusion.scalar_ref, bf16[576,1024]{1,0:T(8,128)(2,1)} %get-tuple-element.213.qkv_ref, bf16[192,1024]{1,0:T(8,128)(2,1)} %pad_maximum_fusion.14.grad_ref, f32[3,1024]{1,0:T(4,128)} %get-tuple-element.218.lse_ref, ...), custom_call_target="tpu_custom_call" | custom-call | flops 3321888768 | bytes 5898240 | tf_op jit(solution)/shard_map/attend_back/pallas_call | solution.py:190
  217.2 2.3 collective-permute-done.34
  220.6 1.7 collective-permute-start.35
  222.3 9.4 %collective-permute-done.35.far_ref = bf16[256,768]{1,0:T(8,128)(2,1)S(1)} collective-permute-done((bf16[256,768]{1,0:T(8,128)(2,1)S(1)}, bf16[256,768]{1,0:T(8,128)(2,1)S(1)}, u32[]{:S(2)}, u32[]{:S(2)}) %collective-permute-start.35) | collective-permute-done | bytes 393248 | tf_op jit(solution)/shard_map/ppermute | solution.py:480
  232.5 3.4 norm_back.2
  236.0 1.8 collective-permute-done.36
  237.8 3.7 convolution_convert_fusion.1
  246.2 12.0 %feed_back.3 = (bf16[256,1536]{1,0:T(8,128)(2,1)}, bf16[256,1536]{1,0:T(8,128)(2,1)}, f32[1,3072]{1,0:T(1,128)}, f32[256,768]{1,0:T(8,128)}, bf16[256,768]{1,0:T...) custom-call(f32[256,768]{1,0:T(8,128)} %get-tuple-element.231.grad_ref, ...), custom_call_target="tpu_custom_call" | custom-call | flops 2415919104 | bytes 14155776 | tf_op jit(solution)/shard_map/feed_back/pallas_call | solution.py:340
  268.1 1.8 collective-permute-start.42
  270.0 3.9 %convolution_convert_fusion = bf16[1536,768]{1,0:T(8,128)(2,1)S(1)} fusion(bf16[256,1536]{1,0:T(8,128)(2,1)} %collective-permute-done.32, bf16[256,1536]{1,0:T(8,128)(2,1)S(1)} %copy-done.45, bf16[256,1536]{1,0:T(8,128)(2,1)S(1)} %collective-permute-done.40, bf16[256,1536]{1,0:T(8,128)(2,1)S(1)} %copy-done.47, bf16[256,768]{1,0:T(8,128)(2,1)S(1)} %slice-done.3, ...), kind=kOutput, calls=%fused_computation.5 | convolution fusion | flops 2435973120 | bytes 7077888 | tf_op jit(solution)/shard_map/dot_general | solution.py:21
  274.0 1.8 fusion.50
  281.5 12.7 %attend_back.3 = (bf16[576,1024]{1,0:T(8,128)(2,1)}, f32[576,1]{1,0:T(8,128)}, bf16[1024,768]{1,0:T(8,128)(2,1)}) custom-call(s32[2]{0:T(128)} %pad_add_fusion.scalar_ref, bf16[576,1024]{1,0:T(8,128)(2,1)} %get-tuple-element.255.qkv_ref, bf16[192,1024]{1,0:T(8,128)(2,1)} %pad_maximum_fusion.16.grad_ref, f32[3,1024]{1,0:T(4,128)} %get-tuple-element.264.lse_ref, ...), custom_call_target="tpu_custom_call" | custom-call | flops 3321888768 | bytes 5898240 | tf_op jit(solution)/shard_map/attend_back/pallas_call | solution.py:190
  297.3 1.8 fusion.44
  304.0 2.0 fusion.45
  307.2 5.8 %collective-permute-done.49 = bf16[2,120,768]{2,1,0:T(8,128)(2,1)S(1)} collective-permute-done((bf16[2,120,768]{2,1,0:T(8,128)(2,1)S(1)}, bf16[2,120,768]{2,1,0:T(8,128)(2,1)S(1)}, u32[]{:S(2)}, u32[]{:S(2)}) %collective-permute-start.49) | collective-permute-done | bytes 368672 | tf_op jit(solution)/shard_map/ppermute | solution.py:477
  319.3 3.3 norm_back.3
  322.6 3.5 collective-permute-done.52
  326.0 2.0 collective-permute-done.51
  332.8 2.2 collective-permute-start.56
  339.7 3.2 collective-permute-done.56
  342.9 5.0 %collective-permute-done.59 = bf16[2,72,768]{2,1,0:T(8,128)(2,1)S(1)} collective-permute-done((bf16[2,72,768]{2,1,0:T(8,128)(2,1)S(1)}, bf16[2,72,768]{2,1,0:T(8,128)(2,1)S(1)}, u32[]{:S(2)}, u32[]{:S(2)}) %collective-permute-start.59) | collective-permute-done | bytes 221216 | tf_op jit(solution)/shard_map/ppermute | solution.py:505
  351.7 8.0 %collective-permute-done.64 = f32[12,768]{1,0:T(8,128)S(1)} collective-permute-done((f32[12,768]{1,0:T(8,128)S(1)}, f32[12,768]{1,0:T(8,128)S(1)}, u32[]{:S(2)}, u32[]{:S(2)}) %collective-permute-start.64) | collective-permute-done | bytes 36896 | tf_op jit(solution)/shard_map/ppermute | solution.py:477
  359.8 1.6 collective-permute-start.66
  362.9 3.9 %collective-permute-done.68 = f32[12,768]{1,0:T(8,128)S(1)} collective-permute-done((f32[12,768]{1,0:T(8,128)S(1)}, f32[12,768]{1,0:T(8,128)S(1)}, u32[]{:S(2)}, u32[]{:S(2)}) %collective-permute-start.68) | collective-permute-done | bytes 36896 | tf_op jit(solution)/shard_map/ppermute | solution.py:480
  366.9 1.7 collective-permute-start.70
  368.5 5.1 %collective-permute-done.69 = f32[12,768]{1,0:T(8,128)S(1)} collective-permute-done((f32[12,768]{1,0:T(8,128)S(1)}, f32[12,768]{1,0:T(8,128)S(1)}, u32[]{:S(2)}, u32[]{:S(2)}) %collective-permute-start.69) | collective-permute-done | bytes 36896 | tf_op jit(solution)/shard_map/ppermute | solution.py:480
  380.1 5.0 %finish.1 = (f32[768,768]{1,0:T(8,128)}, f32[192,768]{1,0:T(8,128)}, f32[768,768]{1,0:T(8,128)}, f32[576,768]{1,0:T(8,128)}, f32[256,768]{1,0:T(8,128)}) custom-call(s32[2]{0:T(128)} %pad_add_fusion.1.scalar_ref, bf16[2,2,176,768]{3,2,1,0:T(8,128)(2,1)} %copy-done.3, bf16[2,2,184,768]{3,2,1,0:T(8,128)(2,1)} %copy-done.2, ...), custom_call_target="tpu_custom_call" | custom-call | bytes 9437184 | tf_op jit(solution)/shard_map/finish/pallas_call | solution.py:441
  385.1 1.8 copy.143
  (434 shorter events, 107.1 us)
Async XLA Ops:
  2.6 24.8 %collective-permute-start.16 = (bf16[104,768]{1,0:T(8,128)(2,1)S(1)}, bf16[104,768]{1,0:T(8,128)(2,1)S(1)}, u32[]{:S(2)}, u32[]{:S(2)}) collective-permute-start(bf16[104,768]{1,0:T(8,128)(2,1)S(1)} %concatenate.170), channel_id=1, source_target_pairs={{0,2},{1,3},{2,0},{3,1},{4,6},{5,7},{6,4},{7,5},{8,10},{9,11},{10,... | collective-permute-start | bytes 479240 | tf_op jit(solution)/shard_map/ppermute | solution.py:480
  9.1 20.8 %collective-permute-start.11 = (bf16[120,768]{1,0:T(8,128)(2,1)}, bf16[120,768]{1,0:T(8,128)(2,1)S(1)}, u32[]{:S(2)}, u32[]{:S(2)}) collective-permute-start(bf16[120,768]{1,0:T(8,128)(2,1)} %get-tuple-element.395), channel_id=1, source_target_pairs={{0,2},{1,3},{2,0},{3,1},{4,6},{5,7},{6,4},{7,5},{8,10},{9,11},{10,... | collective-permute-start | bytes 552968 | tf_op jit(solution)/shard_map/ppermute | solution.py:480
  10.3 19.7 %collective-permute-start.6 = (bf16[152,768]{1,0:T(8,128)(2,1)}, bf16[152,768]{1,0:T(8,128)(2,1)}, u32[]{:S(2)}, u32[]{:S(2)}) collective-permute-start(bf16[152,768]{1,0:T(8,128)(2,1)} %fusion.86), channel_id=1, source_target_pairs={{0,2},{1,3},{6,4},{7,5},{8,10},{9,11},{14,12},{15,13},{16,18},{17,... | collective-permute-start | bytes 700424 | tf_op jit(solution)/shard_map/ppermute | solution.py:505
  15.8 10.3 %collective-permute-start = (s32[1]{0:T(128)}, s32[1]{0:T(128)}, u32[]{:S(2)}, u32[]{:S(2)}) collective-permute-start(s32[1]{0:T(128)} %param.20), channel_id=1, source_target_pairs={{0,4},{4,0},{8,12},{12,8},{16,20},{20,16},{24,28},{28,24},{1,5},{5... | collective-permute-start | bytes 20 | tf_op jit(solution)/shard_map/ppermute | solution.py:477
  15.8 15.9 %collective-permute-start.2 = (bf16[256,768]{1,0:T(8,128)(2,1)}, bf16[256,768]{1,0:T(8,128)(2,1)S(1)}, u32[]{:S(2)}, u32[]{:S(2)}) collective-permute-start(bf16[256,768]{1,0:T(8,128)(2,1)} %param.19), channel_id=1, source_target_pairs={{0,0},{1,4},{2,1},{3,5},{4,2},{5,6},{6,3},{7,7},{8,8},{9,12},{10,9... | collective-permute-start | bytes 1179656 | tf_op jit(solution)/shard_map/ppermute | solution.py:491
  27.4 14.7 %collective-permute-start.17 = (bf16[2,104,768]{2,1,0:T(8,128)(2,1)S(1)}, bf16[2,104,768]{2,1,0:T(8,128)(2,1)S(1)}, u32[]{:S(2)}, u32[]{:S(2)}) collective-permute-start(bf16[2,104,768]{2,1,0:T(8,128)(2,1)S(1)} %pad_maximum_fusion.18), channel_id=1, source_target_pairs={{0,1},{1,0},{2,3},{3,2},{4,5},{5,4},{6,7},{7,6},{8,9},{9,8},{10,11... | collective-permute-start | bytes 958472 | tf_op jit(solution)/shard_map/ppermute | solution.py:480
  29.9 17.2 %collective-permute-start.12 = (bf16[2,120,768]{2,1,0:T(8,128)(2,1)S(1)}, bf16[2,120,768]{2,1,0:T(8,128)(2,1)}, u32[]{:S(2)}, u32[]{:S(2)}) collective-permute-start(bf16[2,120,768]{2,1,0:T(8,128)(2,1)S(1)} %pad_maximum_fusion.17), channel_id=1, source_target_pairs={{0,1},{1,0},{2,3},{3,2},{4,5},{5,4},{6,7},{7,6},{8,9},{9,8},{10,11... | collective-permute-start | bytes 1105928 | tf_op jit(solution)/shard_map/ppermute | solution.py:480
  30.0 8.6 %collective-permute-start.7 = (bf16[152,768]{1,0:T(8,128)(2,1)}, bf16[152,768]{1,0:T(8,128)(2,1)S(1)}, u32[]{:S(2)}, u32[]{:S(2)}) collective-permute-start(bf16[152,768]{1,0:T(8,128)(2,1)} %collective-permute-done.6), channel_id=1, source_target_pairs={{0,8},{4,12},{8,0},{12,4},{16,24},{20,28},{24,16},{28,20},{1,9},{5... | collective-permute-start | bytes 700424 | tf_op jit(solution)/shard_map/ppermute | solution.py:477
  33.1 22.1 %collective-permute-start.4 = (bf16[256,768]{1,0:T(8,128)(2,1)}, bf16[256,768]{1,0:T(8,128)(2,1)}, u32[]{:S(2)}, u32[]{:S(2)}) collective-permute-start(bf16[256,768]{1,0:T(8,128)(2,1)} %add_convert_fusion.own_ref), channel_id=1, source_target_pairs={{0,1},{1,0},{2,3},{3,2},{4,5},{5,4},{6,7},{7,6},{8,9},{9,8},{10,11... | collective-permute-start | bytes 1179656 | tf_op jit(solution)/shard_map/ppermute | solution.py:480
  37.7 33.0 %collective-permute-start.3 = (bf16[256,768]{1,0:T(8,128)(2,1)}, bf16[256,768]{1,0:T(8,128)(2,1)}, u32[]{:S(2)}, u32[]{:S(2)}) collective-permute-start(bf16[256,768]{1,0:T(8,128)(2,1)} %add_convert_fusion.own_ref), channel_id=1, source_target_pairs={{0,4},{4,0},{8,12},{12,8},{16,20},{20,16},{24,28},{28,24},{1,5},{5... | collective-permute-start | bytes 1179656 | tf_op jit(solution)/shard_map/ppermute | solution.py:477
  40.6 17.0 %collective-permute-start.8 = (bf16[304,768]{1,0:T(8,128)(2,1)}, bf16[304,768]{1,0:T(8,128)(2,1)}, u32[]{:S(2)}, u32[]{:S(2)}) collective-permute-start(bf16[304,768]{1,0:T(8,128)(2,1)} %maximum_select_fusion.5), channel_id=1, source_target_pairs={{0,16},{4,20},{8,24},{12,28},{16,0},{20,4},{24,8},{28,12},{1,17},{... | collective-permute-start | bytes 1400840 | tf_op jit(solution)/shard_map/ppermute | solution.py:477
  42.9 12.6 %collective-permute-start.18 = (bf16[3,96,768]{2,1,0:T(8,128)(2,1)}, bf16[3,96,768]{2,1,0:T(8,128)(2,1)S(1)}, u32[]{:S(2)}, u32[]{:S(2)}) collective-permute-start(bf16[3,96,768]{2,1,0:T(8,128)(2,1)} %pad_maximum_fusion.11), channel_id=1, source_target_pairs={{0,8},{4,12},{8,0},{12,4},{16,24},{20,28},{24,16},{28,20},{1,9},{5... | collective-permute-start | bytes 1327112 | tf_op jit(solution)/shard_map/ppermute | solution.py:477
  48.2 18.1 %collective-permute-start.13 = (bf16[3,120,768]{2,1,0:T(8,128)(2,1)S(1)}, bf16[3,120,768]{2,1,0:T(8,128)(2,1)S(1)}, u32[]{:S(2)}, u32[]{:S(2)}) collective-permute-start(bf16[3,120,768]{2,1,0:T(8,128)(2,1)S(1)} %get-tuple-element.373), channel_id=1, source_target_pairs={{0,16},{4,20},{8,24},{12,28},{16,0},{20,4},{24,8},{28,12},{1,17},{... | collective-permute-start | bytes 1658888 | tf_op jit(solution)/shard_map/ppermute | solution.py:477
  55.2 15.5 %collective-permute-start.5 = (bf16[256,768]{1,0:T(8,128)(2,1)}, bf16[256,768]{1,0:T(8,128)(2,1)}, u32[]{:S(2)}, u32[]{:S(2)}) collective-permute-start(bf16[256,768]{1,0:T(8,128)(2,1)} %collective-permute-done.4.far_ref), channel_id=1, source_target_pairs={{0,4},{4,0},{8,12},{12,8},{16,20},{20,16},{24,28},{28,24},{1,5},{5... | collective-permute-start | bytes 1179656 | tf_op jit(solution)/shard_map/ppermute | solution.py:477
  56.5 32.6 %collective-permute-start.19 = (bf16[2,3,96,768]{3,2,1,0:T(8,128)(2,1)}, bf16[2,3,96,768]{3,2,1,0:T(8,128)(2,1)}, u32[]{:S(2)}, u32[]{:S(2)}) collective-permute-start(bf16[2,3,96,768]{3,2,1,0:T(8,128)(2,1)} %pad_maximum_fusion.6), channel_id=1, source_target_pairs={{0,16},{4,20},{8,24},{12,28},{16,0},{20,4},{24,8},{28,12},{1,17},{... | collective-permute-start | bytes 2654216 | tf_op jit(solution)/shard_map/ppermute | solution.py:477
  67.3 25.8 %collective-permute-start.14 = (bf16[2,3,120,768]{3,2,1,0:T(8,128)(2,1)}, bf16[2,3,120,768]{3,2,1,0:T(8,128)(2,1)}, u32[]{:S(2)}, u32[]{:S(2)}) collective-permute-start(bf16[2,3,120,768]{3,2,1,0:T(8,128)(2,1)} %pad_maximum_fusion.5), channel_id=1, source_target_pairs={{0,8},{4,12},{8,0},{12,4},{16,24},{20,28},{24,16},{28,20},{1,9},{5... | collective-permute-start | bytes 3317768 | tf_op jit(solution)/shard_map/ppermute | solution.py:477
  82.2 6.2 %collective-permute-start.9 = (bf16[192,512]{1,0:T(8,128)(2,1)S(1)}, bf16[192,512]{1,0:T(8,128)(2,1)S(1)}, u32[]{:S(2)}, u32[]{:S(2)}) collective-permute-start(bf16[192,512]{1,0:T(8,128)(2,1)S(1)} %slice.383), channel_id=1, source_target_pairs={{0,1},{1,0},{2,3},{3,2},{4,5},{5,4},{6,7},{7,6},{8,9},{9,8},{10,11... | collective-permute-start | bytes 589832 | tf_op jit(solution)/shard_map/ppermute | solution.py:480
  89.1 8.6 %collective-permute-start.10 = (bf16[384,256]{1,0:T(8,128)(2,1)}, bf16[384,256]{1,0:T(8,128)(2,1)}, u32[]{:S(2)}, u32[]{:S(2)}) collective-permute-start(bf16[384,256]{1,0:T(8,128)(2,1)} %pad_maximum_fusion.22), channel_id=1, source_target_pairs={{0,4},{4,0},{8,12},{12,8},{16,20},{20,16},{24,28},{28,24},{1,5},{5... | collective-permute-start | bytes 589832 | tf_op jit(solution)/shard_map/ppermute | solution.py:477
  91.6 9.5 %collective-permute-start.20 = (bf16[4,3,96,768]{3,2,1,0:T(8,128)(2,1)}, bf16[4,3,96,768]{3,2,1,0:T(8,128)(2,1)}, u32[]{:S(2)}, u32[]{:S(2)}) collective-permute-start(bf16[4,3,96,768]{3,2,1,0:T(8,128)(2,1)} %pad_maximum_fusion.2), channel_id=1, source_target_pairs={{0,4},{4,0},{8,12},{12,8},{16,20},{20,16},{24,28},{28,24},{1,5},{5... | collective-permute-start | bytes 5308424 | tf_op jit(solution)/shard_map/ppermute | solution.py:477
  96.9 8.9 %collective-permute-start.15 = (bf16[4,3,120,768]{3,2,1,0:T(8,128)(2,1)}, bf16[4,3,120,768]{3,2,1,0:T(8,128)(2,1)}, u32[]{:S(2)}, u32[]{:S(2)}) collective-permute-start(bf16[4,3,120,768]{3,2,1,0:T(8,128)(2,1)} %pad_maximum_fusion.1), channel_id=1, source_target_pairs={{0,4},{4,0},{8,12},{12,8},{16,20},{20,16},{24,28},{28,24},{1,5},{5... | collective-permute-start | bytes 6635528 | tf_op jit(solution)/shard_map/ppermute | solution.py:477
  124.7 11.8 %collective-permute-start.22 = (bf16[256,768]{1,0:T(8,128)(2,1)}, bf16[256,768]{1,0:T(8,128)(2,1)S(1)}, u32[]{:S(2)}, u32[]{:S(2)}) collective-permute-start(bf16[256,768]{1,0:T(8,128)(2,1)} %get-tuple-element.194.own_ref), channel_id=1, source_target_pairs={{0,1},{1,0},{2,3},{3,2},{4,5},{5,4},{6,7},{7,6},{8,9},{9,8},{10,11... | collective-permute-start | bytes 1179656 | tf_op jit(solution)/shard_map/ppermute | solution.py:480
  125.8 10.7 %collective-permute-start.21 = (bf16[256,768]{1,0:T(8,128)(2,1)}, bf16[256,768]{1,0:T(8,128)(2,1)S(1)}, u32[]{:S(2)}, u32[]{:S(2)}) collective-permute-start(bf16[256,768]{1,0:T(8,128)(2,1)} %get-tuple-element.194.own_ref), channel_id=1, source_target_pairs={{0,4},{4,0},{8,12},{12,8},{16,20},{20,16},{24,28},{28,24},{1,5},{5... | collective-permute-start | bytes 1179656 | tf_op jit(solution)/shard_map/ppermute | solution.py:477
  138.3 11.0 %collective-permute-start.24 = (bf16[256,2688]{1,0:T(8,128)(2,1)}, bf16[256,2688]{1,0:T(8,128)(2,1)S(1)}, u32[]{:S(2)}, u32[]{:S(2)}) collective-permute-start(bf16[256,2688]{1,0:T(8,128)(2,1)} %get-tuple-element.199), channel_id=1, source_target_pairs={{0,4},{4,0},{8,12},{12,8},{16,20},{20,16},{24,28},{28,24},{1,5},{5... | collective-permute-start | bytes 4128776 | tf_op jit(solution)/shard_map/ppermute | solution.py:477
  138.4 21.4 %collective-permute-start.1 = (bf16[256,768]{1,0:T(8,128)(2,1)S(1)}, bf16[256,768]{1,0:T(8,128)(2,1)S(1)}, u32[]{:S(2)}, u32[]{:S(2)}) collective-permute-start(bf16[256,768]{1,0:T(8,128)(2,1)S(1)} %copy-done.49), channel_id=1, source_target_pairs={{0,0},{1,4},{2,1},{3,5},{4,2},{5,6},{6,3},{7,7},{8,8},{9,12},{10,9... | collective-permute-start | bytes 1179656 | tf_op jit(solution)/shard_map/ppermute | solution.py:491
  150.4 7.6 %collective-permute-start.25 = (bf16[192,512]{1,0:T(8,128)(2,1)S(1)}, bf16[192,512]{1,0:T(8,128)(2,1)S(1)}, u32[]{:S(2)}, u32[]{:S(2)}) collective-permute-start(bf16[192,512]{1,0:T(8,128)(2,1)S(1)} %slice.396), channel_id=1, source_target_pairs={{0,1},{1,0},{2,3},{3,2},{4,5},{5,4},{6,7},{7,6},{8,9},{9,8},{10,11... | collective-permute-start | bytes 589832 | tf_op jit(solution)/shard_map/ppermute | solution.py:480
  175.0 14.1 %collective-permute-start.28 = (bf16[256,2688]{1,0:T(8,128)(2,1)}, bf16[256,2688]{1,0:T(8,128)(2,1)S(1)}, u32[]{:S(2)}, u32[]{:S(2)}) collective-permute-start(bf16[256,2688]{1,0:T(8,128)(2,1)} %get-tuple-element.210), channel_id=1, source_target_pairs={{0,4},{4,0},{8,12},{12,8},{16,20},{20,16},{24,28},{28,24},{1,5},{5... | collective-permute-start | bytes 4128776 | tf_op jit(solution)/shard_map/ppermute | solution.py:477
  175.4 13.7 %collective-permute-start.27 = (bf16[256,768]{1,0:T(8,128)(2,1)S(1)}, bf16[256,768]{1,0:T(8,128)(2,1)}, u32[]{:S(2)}, u32[]{:S(2)}) collective-permute-start(bf16[256,768]{1,0:T(8,128)(2,1)S(1)} %get-tuple-element.209), channel_id=1, source_target_pairs={{0,4},{4,0},{8,12},{12,8},{16,20},{20,16},{24,28},{28,24},{1,5},{5... | collective-permute-start | bytes 1179656 | tf_op jit(solution)/shard_map/ppermute | solution.py:477
  175.5 13.5 %collective-permute-start.29 = (bf16[256,768]{1,0:T(8,128)(2,1)}, bf16[256,768]{1,0:T(8,128)(2,1)S(1)}, u32[]{:S(2)}, u32[]{:S(2)}) collective-permute-start(bf16[256,768]{1,0:T(8,128)(2,1)} %get-tuple-element.211), channel_id=1, source_target_pairs={{0,0},{4,1},{1,2},{5,3},{2,4},{6,5},{3,6},{7,7},{8,8},{12,9},{9,10... | collective-permute-start | bytes 1179656 | tf_op jit(solution)/shard_map/ppermute | solution.py:494
  194.0 7.9 %collective-permute-start.31 = (bf16[192,512]{1,0:T(8,128)(2,1)S(1)}, bf16[192,512]{1,0:T(8,128)(2,1)S(1)}, u32[]{:S(2)}, u32[]{:S(2)}) collective-permute-start(bf16[192,512]{1,0:T(8,128)(2,1)S(1)} %get-tuple-element.381), channel_id=1, source_target_pairs={{0,1},{1,0},{2,3},{3,2},{4,5},{5,4},{6,7},{7,6},{8,9},{9,8},{10,11... | collective-permute-start | bytes 589832 | tf_op jit(solution)/shard_map/ppermute | solution.py:480
  202.7 13.0 %collective-permute-start.32 = (bf16[256,1536]{1,0:T(8,128)(2,1)}, bf16[256,1536]{1,0:T(8,128)(2,1)}, u32[]{:S(2)}, u32[]{:S(2)}) collective-permute-start(bf16[256,1536]{1,0:T(8,128)(2,1)} %get-tuple-element.220), channel_id=1, source_target_pairs={{0,4},{4,0},{8,12},{12,8},{16,20},{20,16},{24,28},{28,24},{1,5},{5... | collective-permute-start | bytes 2359304 | tf_op jit(solution)/shard_map/ppermute | solution.py:477
  202.7 13.0 %collective-permute-start.33 = (bf16[256,768]{1,0:T(8,128)(2,1)}, bf16[256,768]{1,0:T(8,128)(2,1)S(1)}, u32[]{:S(2)}, u32[]{:S(2)}) collective-permute-start(bf16[256,768]{1,0:T(8,128)(2,1)} %get-tuple-element.221), channel_id=1, source_target_pairs={{0,4},{4,0},{8,12},{12,8},{16,20},{20,16},{24,28},{28,24},{1,5},{5... | collective-permute-start | bytes 1179656 | tf_op jit(solution)/shard_map/ppermute | solution.py:477
  220.6 11.2 %collective-permute-start.35 = (bf16[256,768]{1,0:T(8,128)(2,1)S(1)}, bf16[256,768]{1,0:T(8,128)(2,1)S(1)}, u32[]{:S(2)}, u32[]{:S(2)}) collective-permute-start(bf16[256,768]{1,0:T(8,128)(2,1)S(1)} %get-tuple-element.359), channel_id=1, source_target_pairs={{0,1},{1,0},{2,3},{3,2},{4,5},{5,4},{6,7},{7,6},{8,9},{9,8},{10,11... | collective-permute-start | bytes 1179656 | tf_op jit(solution)/shard_map/ppermute | solution.py:480
  243.2 15.6 %collective-permute-start.37 = (bf16[2,2,96,768]{3,2,1,0:T(8,128)(2,1)}, bf16[2,2,96,768]{3,2,1,0:T(8,128)(2,1)S(1)}, u32[]{:S(2)}, u32[]{:S(2)}) collective-permute-start(bf16[2,2,96,768]{3,2,1,0:T(8,128)(2,1)} %slice_bitcast_fusion.3), channel_id=1, source_target_pairs={{0,8},{4,12},{8,0},{12,4},{16,24},{20,28},{24,16},{28,20},{1,9},{5... | collective-permute-start | bytes 1769480 | tf_op jit(solution)/shard_map/ppermute | solution.py:477
  244.7 15.3 %collective-permute-start.38 = (bf16[2,2,96,768]{3,2,1,0:T(8,128)(2,1)}, bf16[2,2,96,768]{3,2,1,0:T(8,128)(2,1)S(1)}, u32[]{:S(2)}, u32[]{:S(2)}) collective-permute-start(bf16[2,2,96,768]{3,2,1,0:T(8,128)(2,1)} %slice_bitcast_fusion.2), channel_id=1, source_target_pairs={{0,16},{4,20},{8,24},{12,28},{16,0},{20,4},{24,8},{28,12},{1,17},{... | collective-permute-start | bytes 1769480 | tf_op jit(solution)/shard_map/ppermute | solution.py:477
  262.4 3.5 collective-permute-start.40
  265.9 11.7 %collective-permute-start.43 = (bf16[2,96,768]{2,1,0:T(8,128)(2,1)S(1)}, bf16[2,96,768]{2,1,0:T(8,128)(2,1)S(1)}, u32[]{:S(2)}, u32[]{:S(2)}) collective-permute-start(bf16[2,96,768]{2,1,0:T(8,128)(2,1)S(1)} %slice_bitcast_fusion.19), channel_id=1, source_target_pairs={{0,16},{4,20},{8,24},{12,28},{16,0},{20,4},{24,8},{28,12},{1,17},{... | collective-permute-start | bytes 884744 | tf_op jit(solution)/shard_map/ppermute | solution.py:477
  267.5 10.1 %collective-permute-start.44 = (bf16[2,96,768]{2,1,0:T(8,128)(2,1)S(1)}, bf16[2,96,768]{2,1,0:T(8,128)(2,1)S(1)}, u32[]{:S(2)}, u32[]{:S(2)}) collective-permute-start(bf16[2,96,768]{2,1,0:T(8,128)(2,1)S(1)} %slice_bitcast_fusion.18), channel_id=1, source_target_pairs={{0,8},{4,12},{8,0},{12,4},{16,24},{20,28},{24,16},{28,20},{1,9},{5... | collective-permute-start | bytes 884744 | tf_op jit(solution)/shard_map/ppermute | solution.py:477
  268.1 10.7 %collective-permute-start.42 = (bf16[192,512]{1,0:T(8,128)(2,1)S(1)}, bf16[192,512]{1,0:T(8,128)(2,1)S(1)}, u32[]{:S(2)}, u32[]{:S(2)}) collective-permute-start(bf16[192,512]{1,0:T(8,128)(2,1)S(1)} %get-tuple-element.377), channel_id=1, source_target_pairs={{0,1},{1,0},{2,3},{3,2},{4,5},{5,4},{6,7},{7,6},{8,9},{9,8},{10,11... | collective-permute-start | bytes 589832 | tf_op jit(solution)/shard_map/ppermute | solution.py:480
  277.6 18.1 %collective-permute-start.46 = (bf16[2,2,120,768]{3,2,1,0:T(8,128)(2,1)}, bf16[2,2,120,768]{3,2,1,0:T(8,128)(2,1)}, u32[]{:S(2)}, u32[]{:S(2)}) collective-permute-start(bf16[2,2,120,768]{3,2,1,0:T(8,128)(2,1)} %fusion.72), channel_id=1, source_target_pairs={{0,8},{4,12},{8,0},{12,4},{16,24},{20,28},{24,16},{28,20},{1,9},{5... | collective-permute-start | bytes 2211848 | tf_op jit(solution)/shard_map/ppermute | solution.py:477
  278.2 17.7 %collective-permute-start.47 = (bf16[2,2,120,768]{3,2,1,0:T(8,128)(2,1)}, bf16[2,2,120,768]{3,2,1,0:T(8,128)(2,1)}, u32[]{:S(2)}, u32[]{:S(2)}) collective-permute-start(bf16[2,2,120,768]{3,2,1,0:T(8,128)(2,1)} %fusion.68), channel_id=1, source_target_pairs={{0,16},{4,20},{8,24},{12,28},{16,0},{20,4},{24,8},{28,12},{1,17},{... | collective-permute-start | bytes 2211848 | tf_op jit(solution)/shard_map/ppermute | solution.py:477
  280.3 14.0 %collective-permute-start.45 = (bf16[2,96,768]{2,1,0:T(8,128)(2,1)}, bf16[2,96,768]{2,1,0:T(8,128)(2,1)}, u32[]{:S(2)}, u32[]{:S(2)}) collective-permute-start(bf16[2,96,768]{2,1,0:T(8,128)(2,1)} %fusion.77), channel_id=1, source_target_pairs={{0,1},{1,0},{2,3},{3,2},{4,5},{5,4},{6,7},{7,6},{8,9},{9,8},{10,11... | collective-permute-start | bytes 884744 | tf_op jit(solution)/shard_map/ppermute | solution.py:480
  302.0 11.0 %collective-permute-start.49 = (bf16[2,120,768]{2,1,0:T(8,128)(2,1)S(1)}, bf16[2,120,768]{2,1,0:T(8,128)(2,1)S(1)}, u32[]{:S(2)}, u32[]{:S(2)}) collective-permute-start(bf16[2,120,768]{2,1,0:T(8,128)(2,1)S(1)} %slice_bitcast_fusion.14), channel_id=1, source_target_pairs={{0,16},{4,20},{8,24},{12,28},{16,0},{20,4},{24,8},{28,12},{1,17},{... | collective-permute-start | bytes 1105928 | tf_op jit(solution)/shard_map/ppermute | solution.py:477
  302.5 10.7 %collective-permute-start.50 = (bf16[2,120,768]{2,1,0:T(8,128)(2,1)S(1)}, bf16[2,120,768]{2,1,0:T(8,128)(2,1)S(1)}, u32[]{:S(2)}, u32[]{:S(2)}) collective-permute-start(bf16[2,120,768]{2,1,0:T(8,128)(2,1)S(1)} %slice_bitcast_fusion.13), channel_id=1, source_target_pairs={{0,8},{4,12},{8,0},{12,4},{16,24},{20,28},{24,16},{28,20},{1,9},{5... | collective-permute-start | bytes 1105928 | tf_op jit(solution)/shard_map/ppermute | solution.py:477
  306.0 12.5 %collective-permute-start.53 = (bf16[256,768]{1,0:T(8,128)(2,1)S(1)}, bf16[256,768]{1,0:T(8,128)(2,1)S(1)}, u32[]{:S(2)}, u32[]{:S(2)}) collective-permute-start(bf16[256,768]{1,0:T(8,128)(2,1)S(1)} %get-tuple-element.289), channel_id=1, source_target_pairs={{0,1},{1,0},{2,3},{3,2},{4,5},{5,4},{6,7},{7,6},{8,9},{9,8},{10,11... | collective-permute-start | bytes 1179656 | tf_op jit(solution)/shard_map/ppermute | solution.py:480
  313.3 14.8 %collective-permute-start.51 = (bf16[2,120,768]{2,1,0:T(8,128)(2,1)S(1)}, bf16[2,120,768]{2,1,0:T(8,128)(2,1)S(1)}, u32[]{:S(2)}, u32[]{:S(2)}) collective-permute-start(bf16[2,120,768]{2,1,0:T(8,128)(2,1)S(1)} %fusion.74), channel_id=1, source_target_pairs={{0,1},{1,0},{2,3},{3,2},{4,5},{5,4},{6,7},{7,6},{8,9},{9,8},{10,11... | collective-permute-start | bytes 1105928 | tf_op jit(solution)/shard_map/ppermute | solution.py:480
  315.2 10.8 %collective-permute-start.52 = (bf16[96,768]{1,0:T(8,128)(2,1)}, bf16[96,768]{1,0:T(8,128)(2,1)S(1)}, u32[]{:S(2)}, u32[]{:S(2)}) collective-permute-start(bf16[96,768]{1,0:T(8,128)(2,1)} %slice_bitcast_fusion.22), channel_id=1, source_target_pairs={{0,2},{1,3},{2,0},{3,1},{4,6},{5,7},{6,4},{7,5},{8,10},{9,11},{10,... | collective-permute-start | bytes 442376 | tf_op jit(solution)/shard_map/ppermute | solution.py:480
  316.5 11.8 %collective-permute-start.54 = (bf16[2,72,768]{2,1,0:T(8,128)(2,1)}, bf16[2,72,768]{2,1,0:T(8,128)(2,1)}, u32[]{:S(2)}, u32[]{:S(2)}) collective-permute-start(bf16[2,72,768]{2,1,0:T(8,128)(2,1)} %bitcast.293), channel_id=1, source_target_pairs={{0,8},{4,12},{8,0},{12,4},{16,24},{20,28},{24,16},{28,20},{1,9},{5... | collective-permute-start | bytes 663560 | tf_op jit(solution)/shard_map/ppermute | solution.py:477
  317.0 11.3 %collective-permute-start.55 = (bf16[2,72,768]{2,1,0:T(8,128)(2,1)}, bf16[2,72,768]{2,1,0:T(8,128)(2,1)}, u32[]{:S(2)}, u32[]{:S(2)}) collective-permute-start(bf16[2,72,768]{2,1,0:T(8,128)(2,1)} %bitcast.292), channel_id=1, source_target_pairs={{0,16},{4,20},{8,24},{12,28},{16,0},{20,4},{24,8},{28,12},{1,17},{... | collective-permute-start | bytes 663560 | tf_op jit(solution)/shard_map/ppermute | solution.py:477
  329.4 5.6 %collective-permute-start.58 = (bf16[72,768]{1,0:T(8,128)(2,1)S(1)}, bf16[72,768]{1,0:T(8,128)(2,1)S(1)}, u32[]{:S(2)}, u32[]{:S(2)}) collective-permute-start(bf16[72,768]{1,0:T(8,128)(2,1)S(1)} %select_bitcast_fusion), channel_id=1, source_target_pairs={{0,8},{4,12},{8,0},{12,4},{16,24},{20,28},{24,16},{28,20},{1,9},{5... | collective-permute-start | bytes 331784 | tf_op jit(solution)/shard_map/ppermute | solution.py:477
  331.0 4.8 %collective-permute-start.57 = (bf16[72,768]{1,0:T(8,128)(2,1)S(1)}, bf16[72,768]{1,0:T(8,128)(2,1)S(1)}, u32[]{:S(2)}, u32[]{:S(2)}) collective-permute-start(bf16[72,768]{1,0:T(8,128)(2,1)S(1)} %select_bitcast_fusion.1), channel_id=1, source_target_pairs={{0,16},{4,20},{8,24},{12,28},{16,0},{20,4},{24,8},{28,12},{1,17},{... | collective-permute-start | bytes 331784 | tf_op jit(solution)/shard_map/ppermute | solution.py:477
  332.8 10.1 %collective-permute-start.56 = (bf16[120,768]{1,0:T(8,128)(2,1)S(1)}, bf16[120,768]{1,0:T(8,128)(2,1)S(1)}, u32[]{:S(2)}, u32[]{:S(2)}) collective-permute-start(bf16[120,768]{1,0:T(8,128)(2,1)S(1)} %slice_bitcast_fusion.20), channel_id=1, source_target_pairs={{0,2},{1,3},{2,0},{3,1},{4,6},{5,7},{6,4},{7,5},{8,10},{9,11},{10,... | collective-permute-start | bytes 552968 | tf_op jit(solution)/shard_map/ppermute | solution.py:480
  336.8 11.1 %collective-permute-start.59 = (bf16[2,72,768]{2,1,0:T(8,128)(2,1)S(1)}, bf16[2,72,768]{2,1,0:T(8,128)(2,1)S(1)}, u32[]{:S(2)}, u32[]{:S(2)}) collective-permute-start(bf16[2,72,768]{2,1,0:T(8,128)(2,1)S(1)} %pad_maximum_fusion.20), channel_id=1, source_target_pairs={{2,0},{3,1},{4,6},{5,7},{10,8},{11,9},{12,14},{13,15},{18,16},{19,... | collective-permute-start | bytes 663560 | tf_op jit(solution)/shard_map/ppermute | solution.py:505
  338.1 4.8 %collective-permute-start.61 = (f32[12,768]{1,0:T(8,128)S(1)}, f32[12,768]{1,0:T(8,128)S(1)}, u32[]{:S(2)}, u32[]{:S(2)}) collective-permute-start(f32[12,768]{1,0:T(8,128)S(1)} %fusion.101), channel_id=1, source_target_pairs={{0,8},{4,12},{8,0},{12,4},{16,24},{20,28},{24,16},{28,20},{1,9},{5... | collective-permute-start | bytes 110600 | tf_op jit(solution)/shard_map/ppermute | solution.py:477
  348.1 11.6 %collective-permute-start.63 = (bf16[1,184,768]{2,1,0:T(8,128)(2,1)S(1)}, bf16[1,184,768]{2,1,0:T(8,128)(2,1)S(1)}, u32[]{:S(2)}, u32[]{:S(2)}) collective-permute-start(bf16[1,184,768]{2,1,0:T(8,128)(2,1)S(1)} %fusion.85), channel_id=1, source_target_pairs={{0,8},{4,12},{8,0},{12,4},{16,24},{20,28},{24,16},{28,20},{1,9},{5... | collective-permute-start | bytes 847880 | tf_op jit(solution)/shard_map/ppermute | solution.py:477
  349.6 10.0 %collective-permute-start.62 = (bf16[1,176,768]{2,1,0:T(8,128)(2,1)S(1)}, bf16[1,176,768]{2,1,0:T(8,128)(2,1)S(1)}, u32[]{:S(2)}, u32[]{:S(2)}) collective-permute-start(bf16[1,176,768]{2,1,0:T(8,128)(2,1)S(1)} %maximum_bitcast_fusion), channel_id=1, source_target_pairs={{0,16},{4,20},{8,24},{12,28},{16,0},{20,4},{24,8},{28,12},{1,17},{... | collective-permute-start | bytes 811016 | tf_op jit(solution)/shard_map/ppermute | solution.py:477
  351.2 8.5 %collective-permute-start.64 = (f32[12,768]{1,0:T(8,128)S(1)}, f32[12,768]{1,0:T(8,128)S(1)}, u32[]{:S(2)}, u32[]{:S(2)}) collective-permute-start(f32[12,768]{1,0:T(8,128)S(1)} %add.209), channel_id=1, source_target_pairs={{0,16},{4,20},{8,24},{12,28},{16,0},{20,4},{24,8},{28,12},{1,17},{... | collective-permute-start | bytes 110600 | tf_op jit(solution)/shard_map/ppermute | solution.py:477
  359.8 13.9 %collective-permute-start.66 = (bf16[2,184,768]{2,1,0:T(8,128)(2,1)S(1)}, bf16[2,184,768]{2,1,0:T(8,128)(2,1)S(1)}, u32[]{:S(2)}, u32[]{:S(2)}) collective-permute-start(bf16[2,184,768]{2,1,0:T(8,128)(2,1)S(1)} %maximum_select_fusion.3), channel_id=1, source_target_pairs={{0,16},{4,20},{8,24},{12,28},{16,0},{20,4},{24,8},{28,12},{1,17},{... | collective-permute-start | bytes 1695752 | tf_op jit(solution)/shard_map/ppermute | solution.py:477
  361.5 12.2 %collective-permute-start.65 = (bf16[2,176,768]{2,1,0:T(8,128)(2,1)S(1)}, bf16[2,176,768]{2,1,0:T(8,128)(2,1)S(1)}, u32[]{:S(2)}, u32[]{:S(2)}) collective-permute-start(bf16[2,176,768]{2,1,0:T(8,128)(2,1)S(1)} %maximum_select_fusion.4), channel_id=1, source_target_pairs={{0,8},{4,12},{8,0},{12,4},{16,24},{20,28},{24,16},{28,20},{1,9},{5... | collective-permute-start | bytes 1622024 | tf_op jit(solution)/shard_map/ppermute | solution.py:477
  361.6 12.1 %collective-permute-start.67 = (bf16[256,768]{1,0:T(8,128)(2,1)S(1)}, bf16[256,768]{1,0:T(8,128)(2,1)S(1)}, u32[]{:S(2)}, u32[]{:S(2)}) collective-permute-start(bf16[256,768]{1,0:T(8,128)(2,1)S(1)} %copy-done.52), channel_id=1, source_target_pairs={{0,0},{4,1},{1,2},{5,3},{2,4},{6,5},{3,6},{7,7},{8,8},{12,9},{9,10... | collective-permute-start | bytes 1179656 | tf_op jit(solution)/shard_map/ppermute | solution.py:494
  362.3 4.6 %collective-permute-start.68 = (f32[12,768]{1,0:T(8,128)S(1)}, f32[12,768]{1,0:T(8,128)S(1)}, u32[]{:S(2)}, u32[]{:S(2)}) collective-permute-start(f32[12,768]{1,0:T(8,128)S(1)} %add.210), channel_id=1, source_target_pairs={{0,1},{1,0},{2,3},{3,2},{4,5},{5,4},{6,7},{7,6},{8,9},{9,8},{10,11... | collective-permute-start | bytes 110600 | tf_op jit(solution)/shard_map/ppermute | solution.py:480
  362.9 10.7 %collective-permute-start.69 = (f32[12,768]{1,0:T(8,128)S(1)}, f32[12,768]{1,0:T(8,128)S(1)}, u32[]{:S(2)}, u32[]{:S(2)}) collective-permute-start(f32[12,768]{1,0:T(8,128)S(1)} %add.210), channel_id=1, source_target_pairs={{0,2},{1,3},{2,0},{3,1},{4,6},{5,7},{6,4},{7,5},{8,10},{9,11},{10,... | collective-permute-start | bytes 110600 | tf_op jit(solution)/shard_map/ppermute | solution.py:480
  366.9 6.8 %collective-permute-start.70 = (f32[12,768]{1,0:T(8,128)S(1)}, f32[12,768]{1,0:T(8,128)S(1)}, u32[]{:S(2)}, u32[]{:S(2)}) collective-permute-start(f32[12,768]{1,0:T(8,128)S(1)} %add.210), channel_id=1, source_target_pairs={{0,3},{1,2},{2,1},{3,0},{4,7},{5,6},{6,5},{7,4},{8,11},{9,10},{10,... | collective-permute-start | bytes 110600 | tf_op jit(solution)/shard_map/ppermute | solution.py:480
  374.6 4.5 %collective-permute-start.72 = (bf16[2,2,184,768]{3,2,1,0:T(8,128)(2,1)S(1)}, bf16[2,2,184,768]{3,2,1,0:T(8,128)(2,1)S(1)}, u32[]{:S(2)}, u32[]{:S(2)}) collective-permute-start(bf16[2,2,184,768]{3,2,1,0:T(8,128)(2,1)S(1)} %maximum_select_fusion.two_ref), channel_id=1, source_target_pairs={{0,4},{4,0},{8,12},{12,8},{16,20},{20,16},{24,28},{28,24},{1,5},{5... | collective-permute-start | bytes 3391496 | tf_op jit(solution)/shard_map/ppermute | solution.py:477
  374.9 4.2 %collective-permute-start.71 = (bf16[2,2,176,768]{3,2,1,0:T(8,128)(2,1)S(1)}, bf16[2,2,176,768]{3,2,1,0:T(8,128)(2,1)}, u32[]{:S(2)}, u32[]{:S(2)}) collective-permute-start(bf16[2,2,176,768]{3,2,1,0:T(8,128)(2,1)S(1)} %maximum_select_fusion.1.one_ref), channel_id=1, source_target_pairs={{0,4},{4,0},{8,12},{12,8},{16,20},{20,16},{24,28},{28,24},{1,5},{5... | collective-permute-start | bytes 3244040 | tf_op jit(solution)/shard_map/ppermute | solution.py:477
  (79 other events, 483.8 us)

commit v3 on v2

--- a/solution.py
+++ b/solution.py
@@ -253,7 +253,8 @@
     half = 0.5 * (1.0 + bent)
     act = (value * half).astype(BF)
     keep_or_send(step_at, act, act_ref, send_ref)
-    slope_ref[...] = half + (0.5 * value) * (1.0 - bent * bent) * (CURVE + 3.0 * CURVE * CUBE * square)
+    slope = half + (0.5 * value) * (1.0 - bent * bent) * (CURVE + 3.0 * CURVE * CUBE * square)
+    slope_ref[...] = slope.astype(BF)
     next_ref[...] += dot(act, proj_ref[...], 1, 0)
 
     @pl.when(step_at == pl.num_programs(0) - 1)
@@ -265,7 +266,7 @@
 def feed(attended, stream, w, vectors):
     rows, width = stream.shape
     hidden = w["fc"].shape[0]
-    step_size = 768
+    step_size = hidden // 4
     block = pl.BlockSpec((rows, step_size), lambda j: (0, j))
     weight = pl.BlockSpec((step_size, width), lambda j: (j, 0))
     return pl.pallas_call(
@@ -286,7 +287,7 @@
             jax.ShapeDtypeStruct((rows, hidden // 2), BF),
             jax.ShapeDtypeStruct((rows, width // 2), BF),
             jax.ShapeDtypeStruct((rows, hidden // 2 + width + width // 2), BF),
-            jax.ShapeDtypeStruct((rows, hidden), F32),
+            jax.ShapeDtypeStruct((rows, hidden), BF),
             jax.ShapeDtypeStruct((rows, width), F32),
             jax.ShapeDtypeStruct((rows, width), BF),
             jax.ShapeDtypeStruct((rows, width), BF),
@@ -303,7 +304,7 @@
     pre_ref, send_ref, bias_ref, back_ref, low_ref, heads_ref, sums_ref, acc_ref,
 ):
     step_at = pl.program_id(0)
-    pre = (dot(grad_ref[...].astype(BF), proj_ref[...], 1, 1) * slope_ref[...]).astype(BF)
+    pre = (dot(grad_ref[...].astype(BF), proj_ref[...], 1, 1) * slope_ref[...].astype(F32)).astype(BF)
     keep_or_send(step_at, pre, pre_ref, send_ref)
     bias_ref[...] = jnp.sum(pre.astype(F32), axis=0, keepdims=True)
     part = dot(pre, fc_ref[...], 1, 0)
@@ -334,7 +335,7 @@
 def feed_back(gradient, slope, middle, w, gain):
     rows, width = gradient.shape
     hidden = w["fc"].shape[0]
-    step_size = 768
+    step_size = hidden // 2
     block = pl.BlockSpec((rows, step_size), lambda j: (0, j))
     weight = pl.BlockSpec((step_size, width), lambda j: (j, 0))
     return pl.pallas_call(
@@ -395,8 +396,8 @@
 
 
 def finish_kernel(
-    scalar_ref, one_ref, two_ref, one_far_ref, two_far_ref, low_ref,
-    fc_ref, out_ref, proj_ref, qkv_ref, tokens_ref,
+    scalar_ref, one_ref, two_ref, one_far_ref, two_far_ref, low_ref, last_ref,
+    fc_ref, out_ref, proj_ref, qkv_ref, tokens_ref, output_ref,
 ):
     units = fc_ref.shape[1] // 4
     count = units + 8
@@ -427,9 +428,10 @@
             proj_ref[piece * units : (piece + 1) * units, :] = right[middle:]
     fc_ref[...] = jnp.concatenate(fc).T
     tokens_ref[...] = low_ref[...].astype(F32)
-
-
-def finish(scalars, one, two, one_far, two_far, low, units, outs):
+    output_ref[...] = last_ref[...]
+
+
+def finish(scalars, one, two, one_far, two_far, low, last, units, outs):
     tokens, width = low.shape
     size = one.shape[2] - (units + 8)
 
@@ -442,13 +444,14 @@
         finish_kernel,
         grid=(2,),
         in_specs=[SM] + [block(one, True), block(two, False), block(one_far, True), block(two_far, False)]
-        + [pl.BlockSpec((tokens // 2, width), lambda y: (y, 0))],
+        + [pl.BlockSpec((tokens // 2, width), lambda y: (y, 0))] * 2,
         out_specs=[
             pl.BlockSpec((width, 4 * units), lambda y: (0, y)),
             pl.BlockSpec((4 * outs, width), lambda y: (y, 0)),
             pl.BlockSpec((4 * units, width), lambda y: (y, 0)),
             whole((8 * size, width)),
             pl.BlockSpec((tokens // 2, width), lambda y: (y, 0)),
+            pl.BlockSpec((tokens // 2, width), lambda y: (y, 0)),
         ],
         out_shape=[
             jax.ShapeDtypeStruct((width, 8 * units), F32),
@@ -456,10 +459,11 @@
             jax.ShapeDtypeStruct((8 * units, width), F32),
             jax.ShapeDtypeStruct((8 * size, width), F32),
             jax.ShapeDtypeStruct((tokens, width), F32),
+            jax.ShapeDtypeStruct((tokens, width), BF),
         ],
         cost_estimate=pl.CostEstimate(flops=0, bytes_accessed=16 * 8 * units * width, transcendentals=0),
         name="finish",
-    )(scalars, one, two, one_far, two_far, low)
+    )(scalars, one, two, one_far, two_far, low, last)
 
 
 class Place:
@@ -680,7 +684,7 @@
     return one[0], other[0], one[1], other[1]
 
 
-def first_backward(place, gradient, low, scalars, w, cache, products, later, later_small):
+def first_backward(place, gradient, low, scalars, w, cache, products, later, later_small, output):
     stream, rows, qkv, log_sums, middle, slope = cache
     (norm_one, act_one, heads_one, near_one), (norm_two, act_two, heads_two, near_two) = products
     low_two, low_near_two, pre_two, mid_two, pre_near_two, mid_near_two, grad_qkv_two, rows_two = later
@@ -774,19 +778,21 @@
     count = (large.shape[0] - out_rows) // 2 + 8
     one = jnp.concatenate([large[:count], both[0]])[None]
     two = jnp.concatenate([large[count:], both[1]])[None]
-    one, two, small, small_far, low = tie(one, two, small, small_far, low)
+    one, two, small, small_far = tie(one, two, small, small_far)
     one_far, two_far = place.dp(one, 4), place.dp(two, 2)
-    placed = place.unplace(low)
     small = small + small_far
-    small_far = place.dp(small, 4)
-    one, two, one_far, two_far, small_far = tie(one, two, one_far, two_far, small_far)
-    small = small + small_far
+    small_far = [place.tensor(small, bit) for bit in (1, 2, 3)]
+    one, two, one_far, two_far, *small_far = tie(one, two, one_far, two_far, *small_far)
+    small = small + small_far[0] + small_far[1] + small_far[2]
     one = ordered(place.d & 4, one, one_far)
     two = ordered(place.d & 2, two, two_far)
+    one, two, low, small = tie(one, two, low, small)
     one_far, two_far = place.dp(one, 2), place.dp(two, 4)
-    small_far = [place.tensor(small, bit) for bit in (1, 2, 3)]
-    one, two, one_far, two_far, placed, *small_far = tie(one, two, one_far, two_far, placed, *small_far)
-    small = small + small_far[0] + small_far[1] + small_far[2]
+    placed = place.unplace(low)
+    one, two, one_far, two_far, placed, small, small_far = tie(
+        one, two, one_far, two_far, placed, small, place.dp(small, 4)
+    )
+    small = small + small_far
     bit = 8
     while bit < place.members:
         small = small + place.dp(small, bit)
@@ -795,7 +801,7 @@
     two = ordered(place.d & 4, two[None], two_far[None])
     scalars = jnp.stack([place.d & 1, (place.seq == place.core).astype(jnp.int32)])
     units = count - 8
-    results = finish(scalars, one, two, place.dp(one, 1), place.dp(two, 1), placed, units, out_rows)
+    results = finish(scalars, one, two, place.dp(one, 1), place.dp(two, 1), placed, output, units, out_rows)
     return results, small
 
 
@@ -817,6 +823,11 @@
     place = Place(members, shards)
     place.extra = [1 << bit for bit in range(3, members.bit_length() - 1)]
     row_total, width = tokens.shape
+    fc_rows = w_fc.T
+    units = w_fc.shape[1] // BLOCKS
+    biases = jnp.stack(split(b_fc) + (jnp.zeros((width,), BF),) * 6)
+    mine = jnp.concatenate([my_piece(place, fc_rows), biases])
+    mine, tokens, w_qkv, w_proj, lengths = tie(mine, tokens, w_qkv, w_proj, lengths)
     stream = place.place(tokens).astype(F32)
     length = jnp.where(place.seq == place.core, lengths, place.dp(lengths, 1))
 
@@ -830,10 +841,6 @@
     b_low = (b_low[0] + b_low[1])[:, None]
     b_qkv = jnp.concatenate([b_low[:heads], jnp.zeros((heads, 1), F32), b_low[heads:]])
 
-    fc_rows = w_fc.T
-    units = w_fc.shape[1] // BLOCKS
-    biases = jnp.stack(split(b_fc) + (jnp.zeros((width,), BF),) * 6)
-    mine = jnp.concatenate([my_piece(place, fc_rows), biases])
     zero = over_tensor(place, mine)
     bias = jnp.concatenate([mine[None], zero])[:, units : units + 2].astype(F32)
     bias = (bias[:, 0] + bias[:, 1]).reshape(4, width)
@@ -866,8 +873,8 @@
         place, gradient, scalars, w, cache_second, last, fed_two
     )
     products = (*one, near_one), (*two, near_two)
-    (g_fc, g_out, g_proj, g_qkv, grad_tokens), packed = first_backward(
-        place, gradient, low, scalars, w, cache_first, products, later, later_small
+    (g_fc, g_out, g_proj, g_qkv, grad_tokens, output), packed = first_backward(
+        place, gradient, low, scalars, w, cache_first, products, later, later_small, output
     )
     g_qkv = g_qkv.reshape(3, heads, width).transpose(0, 2, 1)
     grad_bfc = lax.dynamic_index_in_dim(packed, 6 + place.t, 0, keepdims=False)

time: 395 us -> 390 us (0.987)
    ppermute x19, waiting for transfers between devices: 55 us -> 49 us  [tensor(): lax.ppermute(value, 'tensor', [(i, i ^ bit) for i in range(self.shards)])]
    ppermute x48, waiting for transfers between devices: 35.4 us -> 39.6 us  [dp(): lax.ppermute(value, 'dp', [(i, i ^ bit) for i in range(self.members)])]
    unnamed x138 -> x127, local copies, waits for them, and re-layouts: 11.1 us -> 8.97 us
  transfers between devices with their start and end apart: 73 -> 73, of which waited for: 30 -> 32; matrix products, arithmetic and copies ran while one was open for 18% -> 18% of each run, Pallas kernels for 19% -> 19%
where the time goes in v3:
time: 390 us; the launch traced here: 383 us
  Pallas kernels  106 us (27%)
  waiting for transfers between devices  94.3 us (24%)
  starting transfers between devices  79.9 us (20%)
  other arithmetic  51.1 us (13%)
  local copies, waits for them, and re-layouts  36.6 us (9%)
  matrix products  11.5 us (3%)
  between operations  4.11 us (1%)
    ppermute x19, waiting for transfers between devices, tensor(): lax.ppermute(value, 'tensor', [(i, i ^ bit) for i in range(self.shards)])  49 us
    ppermute x48, waiting for transfers between devices, dp(): lax.ppermute(value, 'dp', [(i, i ^ bit) for i in range(self.members)])  39.6 us
    ppermute x19, starting transfers between devices, tensor(): lax.ppermute(value, 'tensor', [(i, i ^ bit) for i in range(self.shards)])  33.3 us
    ppermute x48, starting transfers between devices, dp(): lax.ppermute(value, 'dp', [(i, i ^ bit) for i in range(self.members)])  32.2 us
    pallas_call x2, Pallas kernels, feed(): pl.pallas_call(feed_kernel, grid=(hidden // step_size,), in_specs=[whole(...  25.4 us
    pallas_call x2, Pallas kernels, attend_back(): pl.pallas_call(attend_back_kernel, in_specs=[SM] + [VM] * 4, out_specs=[V...  25.3 us
    pallas_call x2, Pallas kernels, feed_back(): pl.pallas_call(feed_back_kernel, grid=(hidden // step_size,), in_specs=[w...  22.6 us
    pallas_call x2, Pallas kernels, attend(): pl.pallas_call(attend_kernel, in_specs=[SM] + [VM] * 6, out_specs=[VM] *...  20.6 us
  transfers between devices with their start and end apart: 73, of which 32 were waited for; matrix products, arithmetic and copies ran while one was open for 18% of the time, Pallas kernels for 19%

profile of v3, /device:TPU:0, one launch (start us, length us, event | category | flops | bytes accessed | tf_op | source)
XLA Modules:
  0.0 383.3 jit_solution(18160644157095752537)
XLA Ops:
  1.4 1.6 copy.90
  3.8 3.7 collective-permute-start.15
  11.7 5.6 %collective-permute-start.5 = (bf16[152,768]{1,0:T(8,128)(2,1)}, bf16[152,768]{1,0:T(8,128)(2,1)}, u32[]{:S(2)}, u32[]{:S(2)}) collective-permute-start(bf16[152,768]{1,0:T(8,128)(2,1)} %fusion.86), channel_id=1, source_target_pairs={{0,2},{1,3},{6,4},{7,5},{8,10},{9,11},{14,12},{15,13},{16,18},{17,... | collective-permute-start | bytes 700424 | tf_op jit(solution)/shard_map/ppermute | solution.py:509
  17.3 1.6 collective-permute-start.1
  29.0 1.9 collective-permute-start.16
  34.1 4.8 %collective-permute-start.3 = (bf16[256,768]{1,0:T(8,128)(2,1)}, bf16[256,768]{1,0:T(8,128)(2,1)}, u32[]{:S(2)}, u32[]{:S(2)}) collective-permute-start(bf16[256,768]{1,0:T(8,128)(2,1)} %add_convert_fusion.own_ref), channel_id=1, source_target_pairs={{0,1},{1,0},{2,3},{3,2},{4,5},{5,4},{6,7},{7,6},{8,9},{9,8},{10,11... | collective-permute-start | bytes 1179656 | tf_op jit(solution)/shard_map/ppermute | solution.py:484
  39.9 1.9 maximum_select_fusion.5
  45.9 4.0 %collective-permute-done.11 = bf16[2,120,768]{2,1,0:T(8,128)(2,1)} collective-permute-done((bf16[2,120,768]{2,1,0:T(8,128)(2,1)S(1)}, bf16[2,120,768]{2,1,0:T(8,128)(2,1)}, u32[]{:S(2)}, u32[]{:S(2)}) %collective-permute-start.11) | collective-permute-done | bytes 368672 | tf_op jit(solution)/shard_map/ppermute | solution.py:484
  51.0 1.7 collective-permute-start.12
  52.8 1.8 constant_dynamic-update-slice_fusion.4
  54.6 2.6 collective-permute-done.3.far_ref
  58.2 1.6 collective-permute-start.18
  59.8 2.0 fusion.57
  61.9 5.6 %collective-permute-done.12 = bf16[3,120,768]{2,1,0:T(8,128)(2,1)S(1)} collective-permute-done((bf16[3,120,768]{2,1,0:T(8,128)(2,1)S(1)}, bf16[3,120,768]{2,1,0:T(8,128)(2,1)S(1)}, u32[]{:S(2)}, u32[]{:S(2)}) %collective-permute-start.12) | collective-permute-done | bytes 552992 | tf_op jit(solution)/shard_map/ppermute | solution.py:481
  72.0 10.5 %attend.2 = (bf16[1024,768]{1,0:T(8,128)(2,1)}, bf16[576,1024]{1,0:T(8,128)(2,1)}, bf16[192,1024]{1,0:T(8,128)(2,1)}, f32[3,1024]{1,0:T(4,128)}) custom-call(s32[2]{0:T(128)} %pad_add_fusion.1.scalar_ref, bf16[256,768]{1,0:T(8,128)(2,1)} %add_convert_fusion.own_ref, bf16[256,768]{1,0:T(8,128)(2,1)} %collective-permute-done.2.near_ref, ...), custom_call_target="tpu_custom_call" | custom-call | flops 2113929216 | bytes 4718592 | tf_op jit(solution)/shard_map/attend/pallas_call | solution.py:113
  83.5 2.5 collective-permute-start.8
  86.9 2.7 collective-permute-done.8
  90.3 2.5 pad_maximum_fusion.2
  94.3 2.1 fusion.105
  96.5 1.6 pad_maximum_fusion.1
  102.3 4.5 %maximum_maximum_fusion = bf16[8,4,96,768]{3,2,1,0:T(8,128)(2,1)} fusion(bf16[4,3,96,768]{3,2,1,0:T(8,128)(2,1)} %collective-permute-done.19, bf16[2,3,96,768]{3,2,1,0:T(8,128)(2,1)} %collective-permute-done.18, bf16[1,3,96,768]{3,2,1,0:T(8,128)(2,1)S(1)} %bitcast.258, bf16[1,3,96,768]{3,2,1,0:T(8,128)(2,1)S(1)} %fusion.113, ...), kind=kLoop, calls=%fused_computation | loop fusion | flops 9437184 | bytes 9437184 | tf_op jit(solution)/shard_map/concatenate | solution.py:854
  106.9 1.8 constant_dynamic-update-slice_fusion
  109.1 2.6 pad_maximum_fusion
  112.9 12.7 %feed.2 = (f32[256,768]{1,0:T(8,128)}, bf16[256,768]{1,0:T(8,128)(2,1)}, bf16[256,1536]{1,0:T(8,128)(2,1)}, bf16[256,384]{1,0:T(8,128)(2,1)}, bf16[256,2688]{1,0...) custom-call(bf16[768,256]{1,0:T(8,128)(2,1)} %bitcast.273, ...), custom_call_target="tpu_custom_call" | custom-call | flops 2415919104 | bytes 14155776 | tf_op jit(solution)/shard_map/feed/pallas_call | solution.py:272
  127.0 10.4 %collective-permute-done.21.far_ref = bf16[256,768]{1,0:T(8,128)(2,1)S(1)} collective-permute-done((bf16[256,768]{1,0:T(8,128)(2,1)}, bf16[256,768]{1,0:T(8,128)(2,1)S(1)}, u32[]{:S(2)}, u32[]{:S(2)}) %collective-permute-start.21) | collective-permute-done | bytes 393248 | tf_op jit(solution)/shard_map/ppermute | solution.py:484
  137.5 1.7 collective-permute-done.22.both_ref
  140.0 10.1 %attend.3 = (bf16[1024,768]{1,0:T(8,128)(2,1)}, bf16[576,1024]{1,0:T(8,128)(2,1)}, bf16[192,1024]{1,0:T(8,128)(2,1)}, f32[3,1024]{1,0:T(4,128)}) custom-call(s32[2]{0:T(128)} %pad_add_fusion.1.scalar_ref, bf16[256,768]{1,0:T(8,128)(2,1)} %get-tuple-element.209.own_ref, bf16[256,768]{1,0:T(8,128)(2,1)} %copy-done.52, bf16[256,768]{1,0:T(8,128)(2,1)} %copy-done.51, ...), custom_call_target="tpu_custom_call" | custom-call | flops 2113929216 | bytes 4718592 | tf_op jit(solution)/shard_map/attend/pallas_call | solution.py:113
  151.3 3.3 collective-permute-start.25
  155.5 3.3 collective-permute-done.25
  158.8 1.9 collective-permute-start.26
  163.0 12.7 %feed.3 = (f32[256,768]{1,0:T(8,128)}, bf16[256,768]{1,0:T(8,128)(2,1)}, bf16[256,1536]{1,0:T(8,128)(2,1)}, bf16[256,384]{1,0:T(8,128)(2,1)}, bf16[256,2688]{1,0...) custom-call(bf16[768,256]{1,0:T(8,128)(2,1)} %bitcast.274, ...), custom_call_target="tpu_custom_call" | custom-call | flops 2415919104 | bytes 14155776 | tf_op jit(solution)/shard_map/feed/pallas_call | solution.py:272
  176.0 4.5 %collective-permute-start.29 = (bf16[256,768]{1,0:T(8,128)(2,1)}, bf16[256,768]{1,0:T(8,128)(2,1)}, u32[]{:S(2)}, u32[]{:S(2)}) collective-permute-start(bf16[256,768]{1,0:T(8,128)(2,1)} %get-tuple-element.227), channel_id=1, source_target_pairs={{0,0},{4,1},{1,2},{5,3},{2,4},{6,5},{3,6},{7,7},{8,8},{12,9},{9,10... | collective-permute-start | bytes 1179656 | tf_op jit(solution)/shard_map/ppermute | solution.py:498
  180.5 11.3 %feed_back.2 = (bf16[256,1536]{1,0:T(8,128)(2,1)}, bf16[256,1536]{1,0:T(8,128)(2,1)}, f32[1,3072]{1,0:T(1,128)}, f32[256,768]{1,0:T(8,128)}, bf16[256,768]{1,0:T...) custom-call(f32[256,768]{1,0:T(8,128)} %get-tuple-element.220.grad_ref, ...), custom_call_target="tpu_custom_call" | custom-call | flops 2415919104 | bytes 14155776 | tf_op jit(solution)/shard_map/feed_back/pallas_call | solution.py:341
  196.6 5.8 %collective-permute-done.31 = bf16[192,512]{1,0:T(8,128)(2,1)S(1)} collective-permute-done((bf16[192,512]{1,0:T(8,128)(2,1)S(1)}, bf16[192,512]{1,0:T(8,128)(2,1)S(1)}, u32[]{:S(2)}, u32[]{:S(2)}) %collective-permute-start.31) | collective-permute-done | bytes 196640 | tf_op jit(solution)/shard_map/ppermute | solution.py:484
  203.8 12.6 %attend_back.2 = (bf16[576,1024]{1,0:T(8,128)(2,1)}, f32[576,1]{1,0:T(8,128)}, bf16[1024,768]{1,0:T(8,128)(2,1)}) custom-call(s32[2]{0:T(128)} %pad_add_fusion.1.scalar_ref, bf16[576,1024]{1,0:T(8,128)(2,1)} %get-tuple-element.213.qkv_ref, bf16[192,1024]{1,0:T(8,128)(2,1)} %pad_maximum_fusion.14.grad_ref, f32[3,1024]{1,0:T(4,128)} %get-tuple-element.232.lse_ref, ...), custom_call_target="tpu_custom_call" | custom-call | flops 3321888768 | bytes 5898240 | tf_op jit(solution)/shard_map/attend_back/pallas_call | solution.py:190
  217.8 2.3 collective-permute-done.34
  222.4 10.1 %collective-permute-done.35.far_ref = bf16[256,768]{1,0:T(8,128)(2,1)} collective-permute-done((bf16[256,768]{1,0:T(8,128)(2,1)S(1)}, bf16[256,768]{1,0:T(8,128)(2,1)}, u32[]{:S(2)}, u32[]{:S(2)}) %collective-permute-start.35) | collective-permute-done | bytes 393248 | tf_op jit(solution)/shard_map/ppermute | solution.py:484
  232.4 3.3 norm_back.2
  236.0 1.8 collective-permute-done.36
  237.8 3.7 convolution_convert_fusion.1
  244.2 1.5 collective-permute-start.38
  245.7 11.3 %feed_back.3 = (bf16[256,1536]{1,0:T(8,128)(2,1)}, bf16[256,1536]{1,0:T(8,128)(2,1)}, f32[1,3072]{1,0:T(1,128)}, f32[256,768]{1,0:T(8,128)}, bf16[256,768]{1,0:T...) custom-call(f32[256,768]{1,0:T(8,128)} %get-tuple-element.245.grad_ref, ...), custom_call_target="tpu_custom_call" | custom-call | flops 2415919104 | bytes 14155776 | tf_op jit(solution)/shard_map/feed_back/pallas_call | solution.py:341
  257.1 1.7 collective-permute-done.37
  264.7 1.5 collective-permute-start.43
  268.5 3.9 %convolution_convert_fusion = bf16[1536,768]{1,0:T(8,128)(2,1)S(1)} fusion(bf16[256,1536]{1,0:T(8,128)(2,1)} %collective-permute-done.32, bf16[256,1536]{1,0:T(8,128)(2,1)S(1)} %copy-done.42, bf16[256,1536]{1,0:T(8,128)(2,1)S(1)} %collective-permute-done.40, bf16[256,1536]{1,0:T(8,128)(2,1)S(1)} %copy-done.44, bf16[256,768]{1,0:T(8,128)(2,1)S(1)} %slice-done.3, ...), kind=kOutput, calls=%fused_computation.5 | convolution fusion | flops 2435973120 | bytes 7077888 | tf_op jit(solution)/shard_map/dot_general | solution.py:21
  272.5 1.9 fusion.50
  280.3 12.7 %attend_back.3 = (bf16[576,1024]{1,0:T(8,128)(2,1)}, f32[576,1]{1,0:T(8,128)}, bf16[1024,768]{1,0:T(8,128)(2,1)}) custom-call(s32[2]{0:T(128)} %pad_add_fusion.1.scalar_ref, bf16[576,1024]{1,0:T(8,128)(2,1)} %get-tuple-element.269.qkv_ref, bf16[192,1024]{1,0:T(8,128)(2,1)} %pad_maximum_fusion.16.grad_ref, f32[3,1024]{1,0:T(4,128)} %get-tuple-element.278.lse_ref, ...), custom_call_target="tpu_custom_call" | custom-call | flops 3321888768 | bytes 5898240 | tf_op jit(solution)/shard_map/attend_back/pallas_call | solution.py:190
  295.9 1.8 fusion.44
  302.7 2.0 fusion.45
  306.9 4.7 %collective-permute-done.49 = bf16[2,120,768]{2,1,0:T(8,128)(2,1)S(1)} collective-permute-done((bf16[2,120,768]{2,1,0:T(8,128)(2,1)S(1)}, bf16[2,120,768]{2,1,0:T(8,128)(2,1)S(1)}, u32[]{:S(2)}, u32[]{:S(2)}) %collective-permute-start.49) | collective-permute-done | bytes 368672 | tf_op jit(solution)/shard_map/ppermute | solution.py:481
  314.5 2.1 collective-permute-start.52
  318.6 3.3 norm_back.3
  321.9 3.8 collective-permute-done.52
  329.0 1.5 collective-permute-start.58
  331.3 1.8 collective-permute-start.56
  338.3 3.0 collective-permute-done.56
  341.8 5.6 %collective-permute-done.59 = bf16[2,72,768]{2,1,0:T(8,128)(2,1)S(1)} collective-permute-done((bf16[2,72,768]{2,1,0:T(8,128)(2,1)S(1)}, bf16[2,72,768]{2,1,0:T(8,128)(2,1)S(1)}, u32[]{:S(2)}, u32[]{:S(2)}) %collective-permute-start.59) | collective-permute-done | bytes 221216 | tf_op jit(solution)/shard_map/ppermute | solution.py:509
  348.8 1.8 collective-permute-start.65
  350.6 2.6 collective-permute-start.64
  353.2 1.6 collective-permute-done.66
  355.6 1.6 collective-permute-start.68
  359.9 11.1 %collective-permute-done.70 = f32[12,768]{1,0:T(8,128)S(1)} collective-permute-done((f32[12,768]{1,0:T(8,128)S(1)}, f32[12,768]{1,0:T(8,128)S(1)}, u32[]{:S(2)}, u32[]{:S(2)}) %collective-permute-start.70) | collective-permute-done | bytes 36896 | tf_op jit(solution)/shard_map/ppermute | solution.py:481
  374.9 1.7 collective-permute-done.71.one_far_ref
  377.6 5.2 %finish.1 = (f32[768,768]{1,0:T(8,128)}, f32[192,768]{1,0:T(8,128)}, f32[768,768]{1,0:T(8,128)}, f32[576,768]{1,0:T(8,128)}, f32[256,768]{1,0:T(8,128)}, /*index=5*/bf16[256,768]{1,0:T(8,128)(2,1)}) custom-call(s32[2]{0:T(128)} %pad_add_fusion.scalar_ref, bf16[2,2,176,768]{3,2,1,0:T(8,128)(2,1)} %copy-done.4, bf16[2,2,184,768]{3,2,1,0:T(8,128)(2,1)} %copy-done.3, ...), custom_call_target="tpu_custom_call" | custom-call | bytes 9437184 | tf_op jit(solution)/shard_map/finish/pallas_call | solution.py:443
  (423 shorter events, 106.3 us)
Async XLA Ops:
  3.2 24.5 %collective-permute-start = (s32[1]{0:T(128)}, s32[1]{0:T(128)}, u32[]{:S(2)}, u32[]{:S(2)}) collective-permute-start(s32[1]{0:T(128)} %param.20), channel_id=1, source_target_pairs={{0,4},{4,0},{8,12},{12,8},{16,20},{20,16},{24,28},{28,24},{1,5},{5... | collective-permute-start | bytes 20 | tf_op jit(solution)/shard_map/ppermute | solution.py:481
  3.8 25.2 %collective-permute-start.15 = (bf16[104,768]{1,0:T(8,128)(2,1)S(1)}, bf16[104,768]{1,0:T(8,128)(2,1)S(1)}, u32[]{:S(2)}, u32[]{:S(2)}) collective-permute-start(bf16[104,768]{1,0:T(8,128)(2,1)S(1)} %concatenate.157), channel_id=1, source_target_pairs={{0,2},{1,3},{2,0},{3,1},{4,6},{5,7},{6,4},{7,5},{8,10},{9,11},{10,... | collective-permute-start | bytes 479240 | tf_op jit(solution)/shard_map/ppermute | solution.py:484
  9.8 21.2 %collective-permute-start.10 = (bf16[120,768]{1,0:T(8,128)(2,1)}, bf16[120,768]{1,0:T(8,128)(2,1)S(1)}, u32[]{:S(2)}, u32[]{:S(2)}) collective-permute-start(bf16[120,768]{1,0:T(8,128)(2,1)} %get-tuple-element.415), channel_id=1, source_target_pairs={{0,2},{1,3},{2,0},{3,1},{4,6},{5,7},{6,4},{7,5},{8,10},{9,11},{10,... | collective-permute-start | bytes 552968 | tf_op jit(solution)/shard_map/ppermute | solution.py:484
  11.7 19.5 %collective-permute-start.5 = (bf16[152,768]{1,0:T(8,128)(2,1)}, bf16[152,768]{1,0:T(8,128)(2,1)}, u32[]{:S(2)}, u32[]{:S(2)}) collective-permute-start(bf16[152,768]{1,0:T(8,128)(2,1)} %fusion.86), channel_id=1, source_target_pairs={{0,2},{1,3},{6,4},{7,5},{8,10},{9,11},{14,12},{15,13},{16,18},{17,... | collective-permute-start | bytes 700424 | tf_op jit(solution)/shard_map/ppermute | solution.py:509
  17.3 15.4 %collective-permute-start.1 = (bf16[256,768]{1,0:T(8,128)(2,1)}, bf16[256,768]{1,0:T(8,128)(2,1)S(1)}, u32[]{:S(2)}, u32[]{:S(2)}) collective-permute-start(bf16[256,768]{1,0:T(8,128)(2,1)} %param.19), channel_id=1, source_target_pairs={{0,0},{1,4},{2,1},{3,5},{4,2},{5,6},{6,3},{7,7},{8,8},{9,12},{10,9... | collective-permute-start | bytes 1179656 | tf_op jit(solution)/shard_map/ppermute | solution.py:495
  29.0 14.3 %collective-permute-start.16 = (bf16[2,104,768]{2,1,0:T(8,128)(2,1)S(1)}, bf16[2,104,768]{2,1,0:T(8,128)(2,1)S(1)}, u32[]{:S(2)}, u32[]{:S(2)}) collective-permute-start(bf16[2,104,768]{2,1,0:T(8,128)(2,1)S(1)} %pad_maximum_fusion.18), channel_id=1, source_target_pairs={{0,1},{1,0},{2,3},{3,2},{4,5},{5,4},{6,7},{7,6},{8,9},{9,8},{10,11... | collective-permute-start | bytes 958472 | tf_op jit(solution)/shard_map/ppermute | solution.py:484
  31.0 18.9 %collective-permute-start.11 = (bf16[2,120,768]{2,1,0:T(8,128)(2,1)S(1)}, bf16[2,120,768]{2,1,0:T(8,128)(2,1)}, u32[]{:S(2)}, u32[]{:S(2)}) collective-permute-start(bf16[2,120,768]{2,1,0:T(8,128)(2,1)S(1)} %pad_maximum_fusion.17), channel_id=1, source_target_pairs={{0,1},{1,0},{2,3},{3,2},{4,5},{5,4},{6,7},{7,6},{8,9},{9,8},{10,11... | collective-permute-start | bytes 1105928 | tf_op jit(solution)/shard_map/ppermute | solution.py:484
  31.2 8.6 %collective-permute-start.6 = (bf16[152,768]{1,0:T(8,128)(2,1)}, bf16[152,768]{1,0:T(8,128)(2,1)S(1)}, u32[]{:S(2)}, u32[]{:S(2)}) collective-permute-start(bf16[152,768]{1,0:T(8,128)(2,1)} %collective-permute-done.5), channel_id=1, source_target_pairs={{0,8},{4,12},{8,0},{12,4},{16,24},{20,28},{24,16},{28,20},{1,9},{5... | collective-permute-start | bytes 700424 | tf_op jit(solution)/shard_map/ppermute | solution.py:481
  34.1 23.1 %collective-permute-start.3 = (bf16[256,768]{1,0:T(8,128)(2,1)}, bf16[256,768]{1,0:T(8,128)(2,1)}, u32[]{:S(2)}, u32[]{:S(2)}) collective-permute-start(bf16[256,768]{1,0:T(8,128)(2,1)} %add_convert_fusion.own_ref), channel_id=1, source_target_pairs={{0,1},{1,0},{2,3},{3,2},{4,5},{5,4},{6,7},{7,6},{8,9},{9,8},{10,11... | collective-permute-start | bytes 1179656 | tf_op jit(solution)/shard_map/ppermute | solution.py:484
  38.9 33.1 %collective-permute-start.2 = (bf16[256,768]{1,0:T(8,128)(2,1)}, bf16[256,768]{1,0:T(8,128)(2,1)}, u32[]{:S(2)}, u32[]{:S(2)}) collective-permute-start(bf16[256,768]{1,0:T(8,128)(2,1)} %add_convert_fusion.own_ref), channel_id=1, source_target_pairs={{0,4},{4,0},{8,12},{12,8},{16,20},{20,16},{24,28},{28,24},{1,5},{5... | collective-permute-start | bytes 1179656 | tf_op jit(solution)/shard_map/ppermute | solution.py:481
  41.8 18.0 %collective-permute-start.7 = (bf16[304,768]{1,0:T(8,128)(2,1)}, bf16[304,768]{1,0:T(8,128)(2,1)}, u32[]{:S(2)}, u32[]{:S(2)}) collective-permute-start(bf16[304,768]{1,0:T(8,128)(2,1)} %maximum_select_fusion.5), channel_id=1, source_target_pairs={{0,16},{4,20},{8,24},{12,28},{16,0},{20,4},{24,8},{28,12},{1,17},{... | collective-permute-start | bytes 1400840 | tf_op jit(solution)/shard_map/ppermute | solution.py:481
  44.3 12.9 %collective-permute-start.17 = (bf16[3,96,768]{2,1,0:T(8,128)(2,1)}, bf16[3,96,768]{2,1,0:T(8,128)(2,1)S(1)}, u32[]{:S(2)}, u32[]{:S(2)}) collective-permute-start(bf16[3,96,768]{2,1,0:T(8,128)(2,1)} %pad_maximum_fusion.11), channel_id=1, source_target_pairs={{0,8},{4,12},{8,0},{12,4},{16,24},{20,28},{24,16},{28,20},{1,9},{5... | collective-permute-start | bytes 1327112 | tf_op jit(solution)/shard_map/ppermute | solution.py:481
  51.0 16.4 %collective-permute-start.12 = (bf16[3,120,768]{2,1,0:T(8,128)(2,1)S(1)}, bf16[3,120,768]{2,1,0:T(8,128)(2,1)S(1)}, u32[]{:S(2)}, u32[]{:S(2)}) collective-permute-start(bf16[3,120,768]{2,1,0:T(8,128)(2,1)S(1)} %get-tuple-element.393), channel_id=1, source_target_pairs={{0,16},{4,20},{8,24},{12,28},{16,0},{20,4},{24,8},{28,12},{1,17},{... | collective-permute-start | bytes 1658888 | tf_op jit(solution)/shard_map/ppermute | solution.py:481
  57.3 14.7 %collective-permute-start.4 = (bf16[256,768]{1,0:T(8,128)(2,1)}, bf16[256,768]{1,0:T(8,128)(2,1)}, u32[]{:S(2)}, u32[]{:S(2)}) collective-permute-start(bf16[256,768]{1,0:T(8,128)(2,1)} %collective-permute-done.3.far_ref), channel_id=1, source_target_pairs={{0,4},{4,0},{8,12},{12,8},{16,20},{20,16},{24,28},{28,24},{1,5},{5... | collective-permute-start | bytes 1179656 | tf_op jit(solution)/shard_map/ppermute | solution.py:481
  58.2 32.1 %collective-permute-start.18 = (bf16[2,3,96,768]{3,2,1,0:T(8,128)(2,1)}, bf16[2,3,96,768]{3,2,1,0:T(8,128)(2,1)}, u32[]{:S(2)}, u32[]{:S(2)}) collective-permute-start(bf16[2,3,96,768]{3,2,1,0:T(8,128)(2,1)} %pad_maximum_fusion.6), channel_id=1, source_target_pairs={{0,16},{4,20},{8,24},{12,28},{16,0},{20,4},{24,8},{28,12},{1,17},{... | collective-permute-start | bytes 2654216 | tf_op jit(solution)/shard_map/ppermute | solution.py:481
  68.5 25.8 %collective-permute-start.13 = (bf16[2,3,120,768]{3,2,1,0:T(8,128)(2,1)}, bf16[2,3,120,768]{3,2,1,0:T(8,128)(2,1)}, u32[]{:S(2)}, u32[]{:S(2)}) collective-permute-start(bf16[2,3,120,768]{3,2,1,0:T(8,128)(2,1)} %pad_maximum_fusion.5), channel_id=1, source_target_pairs={{0,8},{4,12},{8,0},{12,4},{16,24},{20,28},{24,16},{28,20},{1,9},{5... | collective-permute-start | bytes 3317768 | tf_op jit(solution)/shard_map/ppermute | solution.py:481
  83.5 6.2 %collective-permute-start.8 = (bf16[192,512]{1,0:T(8,128)(2,1)S(1)}, bf16[192,512]{1,0:T(8,128)(2,1)S(1)}, u32[]{:S(2)}, u32[]{:S(2)}) collective-permute-start(bf16[192,512]{1,0:T(8,128)(2,1)S(1)} %slice.383), channel_id=1, source_target_pairs={{0,1},{1,0},{2,3},{3,2},{4,5},{5,4},{6,7},{7,6},{8,9},{9,8},{10,11... | collective-permute-start | bytes 589832 | tf_op jit(solution)/shard_map/ppermute | solution.py:484
  90.3 8.5 %collective-permute-start.9 = (bf16[384,256]{1,0:T(8,128)(2,1)}, bf16[384,256]{1,0:T(8,128)(2,1)}, u32[]{:S(2)}, u32[]{:S(2)}) collective-permute-start(bf16[384,256]{1,0:T(8,128)(2,1)} %pad_maximum_fusion.22), channel_id=1, source_target_pairs={{0,4},{4,0},{8,12},{12,8},{16,20},{20,16},{24,28},{28,24},{1,5},{5... | collective-permute-start | bytes 589832 | tf_op jit(solution)/shard_map/ppermute | solution.py:481
  92.9 9.5 %collective-permute-start.19 = (bf16[4,3,96,768]{3,2,1,0:T(8,128)(2,1)}, bf16[4,3,96,768]{3,2,1,0:T(8,128)(2,1)}, u32[]{:S(2)}, u32[]{:S(2)}) collective-permute-start(bf16[4,3,96,768]{3,2,1,0:T(8,128)(2,1)} %pad_maximum_fusion.2), channel_id=1, source_target_pairs={{0,4},{4,0},{8,12},{12,8},{16,20},{20,16},{24,28},{28,24},{1,5},{5... | collective-permute-start | bytes 5308424 | tf_op jit(solution)/shard_map/ppermute | solution.py:481
  98.1 8.8 %collective-permute-start.14 = (bf16[4,3,120,768]{3,2,1,0:T(8,128)(2,1)}, bf16[4,3,120,768]{3,2,1,0:T(8,128)(2,1)}, u32[]{:S(2)}, u32[]{:S(2)}) collective-permute-start(bf16[4,3,120,768]{3,2,1,0:T(8,128)(2,1)} %pad_maximum_fusion.1), channel_id=1, source_target_pairs={{0,4},{4,0},{8,12},{12,8},{16,20},{20,16},{24,28},{28,24},{1,5},{5... | collective-permute-start | bytes 6635528 | tf_op jit(solution)/shard_map/ppermute | solution.py:481
  125.6 11.8 %collective-permute-start.21 = (bf16[256,768]{1,0:T(8,128)(2,1)}, bf16[256,768]{1,0:T(8,128)(2,1)S(1)}, u32[]{:S(2)}, u32[]{:S(2)}) collective-permute-start(bf16[256,768]{1,0:T(8,128)(2,1)} %get-tuple-element.209.own_ref), channel_id=1, source_target_pairs={{0,1},{1,0},{2,3},{3,2},{4,5},{5,4},{6,7},{7,6},{8,9},{9,8},{10,11... | collective-permute-start | bytes 1179656 | tf_op jit(solution)/shard_map/ppermute | solution.py:484
  126.8 10.7 %collective-permute-start.20 = (bf16[256,768]{1,0:T(8,128)(2,1)}, bf16[256,768]{1,0:T(8,128)(2,1)S(1)}, u32[]{:S(2)}, u32[]{:S(2)}) collective-permute-start(bf16[256,768]{1,0:T(8,128)(2,1)} %get-tuple-element.209.own_ref), channel_id=1, source_target_pairs={{0,4},{4,0},{8,12},{12,8},{16,20},{20,16},{24,28},{28,24},{1,5},{5... | collective-permute-start | bytes 1179656 | tf_op jit(solution)/shard_map/ppermute | solution.py:481
  139.2 10.9 %collective-permute-start.24 = (bf16[256,2688]{1,0:T(8,128)(2,1)}, bf16[256,2688]{1,0:T(8,128)(2,1)S(1)}, u32[]{:S(2)}, u32[]{:S(2)}) collective-permute-start(bf16[256,2688]{1,0:T(8,128)(2,1)} %get-tuple-element.215), channel_id=1, source_target_pairs={{0,4},{4,0},{8,12},{12,8},{16,20},{20,16},{24,28},{28,24},{1,5},{5... | collective-permute-start | bytes 4128776 | tf_op jit(solution)/shard_map/ppermute | solution.py:481
  139.3 21.4 %collective-permute-start.23 = (bf16[256,768]{1,0:T(8,128)(2,1)S(1)}, bf16[256,768]{1,0:T(8,128)(2,1)S(1)}, u32[]{:S(2)}, u32[]{:S(2)}) collective-permute-start(bf16[256,768]{1,0:T(8,128)(2,1)S(1)} %copy-done.46), channel_id=1, source_target_pairs={{0,0},{1,4},{2,1},{3,5},{4,2},{5,6},{6,3},{7,7},{8,8},{9,12},{10,9... | collective-permute-start | bytes 1179656 | tf_op jit(solution)/shard_map/ppermute | solution.py:495
  151.3 7.5 %collective-permute-start.25 = (bf16[192,512]{1,0:T(8,128)(2,1)S(1)}, bf16[192,512]{1,0:T(8,128)(2,1)S(1)}, u32[]{:S(2)}, u32[]{:S(2)}) collective-permute-start(bf16[192,512]{1,0:T(8,128)(2,1)S(1)} %slice.396), channel_id=1, source_target_pairs={{0,1},{1,0},{2,3},{3,2},{4,5},{5,4},{6,7},{7,6},{8,9},{9,8},{10,11... | collective-permute-start | bytes 589832 | tf_op jit(solution)/shard_map/ppermute | solution.py:484
  175.7 16.2 %collective-permute-start.28 = (bf16[256,2688]{1,0:T(8,128)(2,1)}, bf16[256,2688]{1,0:T(8,128)(2,1)S(1)}, u32[]{:S(2)}, u32[]{:S(2)}) collective-permute-start(bf16[256,2688]{1,0:T(8,128)(2,1)} %get-tuple-element.226), channel_id=1, source_target_pairs={{0,4},{4,0},{8,12},{12,8},{16,20},{20,16},{24,28},{28,24},{1,5},{5... | collective-permute-start | bytes 4128776 | tf_op jit(solution)/shard_map/ppermute | solution.py:481
  176.0 15.8 %collective-permute-start.29 = (bf16[256,768]{1,0:T(8,128)(2,1)}, bf16[256,768]{1,0:T(8,128)(2,1)}, u32[]{:S(2)}, u32[]{:S(2)}) collective-permute-start(bf16[256,768]{1,0:T(8,128)(2,1)} %get-tuple-element.227), channel_id=1, source_target_pairs={{0,0},{4,1},{1,2},{5,3},{2,4},{6,5},{3,6},{7,7},{8,8},{12,9},{9,10... | collective-permute-start | bytes 1179656 | tf_op jit(solution)/shard_map/ppermute | solution.py:498
  180.5 11.3 %collective-permute-start.27 = (bf16[256,768]{1,0:T(8,128)(2,1)S(1)}, bf16[256,768]{1,0:T(8,128)(2,1)}, u32[]{:S(2)}, u32[]{:S(2)}) collective-permute-start(bf16[256,768]{1,0:T(8,128)(2,1)S(1)} %get-tuple-element.225), channel_id=1, source_target_pairs={{0,4},{4,0},{8,12},{12,8},{16,20},{20,16},{24,28},{28,24},{1,5},{5... | collective-permute-start | bytes 1179656 | tf_op jit(solution)/shard_map/ppermute | solution.py:481
  195.2 7.2 %collective-permute-start.31 = (bf16[192,512]{1,0:T(8,128)(2,1)S(1)}, bf16[192,512]{1,0:T(8,128)(2,1)S(1)}, u32[]{:S(2)}, u32[]{:S(2)}) collective-permute-start(bf16[192,512]{1,0:T(8,128)(2,1)S(1)} %get-tuple-element.401), channel_id=1, source_target_pairs={{0,1},{1,0},{2,3},{3,2},{4,5},{5,4},{6,7},{7,6},{8,9},{9,8},{10,11... | collective-permute-start | bytes 589832 | tf_op jit(solution)/shard_map/ppermute | solution.py:484
  203.2 13.1 %collective-permute-start.32 = (bf16[256,1536]{1,0:T(8,128)(2,1)}, bf16[256,1536]{1,0:T(8,128)(2,1)}, u32[]{:S(2)}, u32[]{:S(2)}) collective-permute-start(bf16[256,1536]{1,0:T(8,128)(2,1)} %get-tuple-element.234), channel_id=1, source_target_pairs={{0,4},{4,0},{8,12},{12,8},{16,20},{20,16},{24,28},{28,24},{1,5},{5... | collective-permute-start | bytes 2359304 | tf_op jit(solution)/shard_map/ppermute | solution.py:481
  203.2 13.1 %collective-permute-start.33 = (bf16[256,768]{1,0:T(8,128)(2,1)}, bf16[256,768]{1,0:T(8,128)(2,1)}, u32[]{:S(2)}, u32[]{:S(2)}) collective-permute-start(bf16[256,768]{1,0:T(8,128)(2,1)} %get-tuple-element.235), channel_id=1, source_target_pairs={{0,4},{4,0},{8,12},{12,8},{16,20},{20,16},{24,28},{28,24},{1,5},{5... | collective-permute-start | bytes 1179656 | tf_op jit(solution)/shard_map/ppermute | solution.py:481
  221.2 11.3 %collective-permute-start.35 = (bf16[256,768]{1,0:T(8,128)(2,1)S(1)}, bf16[256,768]{1,0:T(8,128)(2,1)}, u32[]{:S(2)}, u32[]{:S(2)}) collective-permute-start(bf16[256,768]{1,0:T(8,128)(2,1)S(1)} %get-tuple-element.379), channel_id=1, source_target_pairs={{0,1},{1,0},{2,3},{3,2},{4,5},{5,4},{6,7},{7,6},{8,9},{9,8},{10,11... | collective-permute-start | bytes 1179656 | tf_op jit(solution)/shard_map/ppermute | solution.py:484
  243.2 15.6 %collective-permute-start.37 = (bf16[2,2,96,768]{3,2,1,0:T(8,128)(2,1)}, bf16[2,2,96,768]{3,2,1,0:T(8,128)(2,1)S(1)}, u32[]{:S(2)}, u32[]{:S(2)}) collective-permute-start(bf16[2,2,96,768]{3,2,1,0:T(8,128)(2,1)} %slice_bitcast_fusion.3), channel_id=1, source_target_pairs={{0,8},{4,12},{8,0},{12,4},{16,24},{20,28},{24,16},{28,20},{1,9},{5... | collective-permute-start | bytes 1769480 | tf_op jit(solution)/shard_map/ppermute | solution.py:481
  244.2 15.3 %collective-permute-start.38 = (bf16[2,2,96,768]{3,2,1,0:T(8,128)(2,1)}, bf16[2,2,96,768]{3,2,1,0:T(8,128)(2,1)S(1)}, u32[]{:S(2)}, u32[]{:S(2)}) collective-permute-start(bf16[2,2,96,768]{3,2,1,0:T(8,128)(2,1)} %slice_bitcast_fusion.2), channel_id=1, source_target_pairs={{0,16},{4,20},{8,24},{12,28},{16,0},{20,4},{24,8},{28,12},{1,17},{... | collective-permute-start | bytes 1769480 | tf_op jit(solution)/shard_map/ppermute | solution.py:481
  264.7 11.6 %collective-permute-start.43 = (bf16[2,96,768]{2,1,0:T(8,128)(2,1)S(1)}, bf16[2,96,768]{2,1,0:T(8,128)(2,1)S(1)}, u32[]{:S(2)}, u32[]{:S(2)}) collective-permute-start(bf16[2,96,768]{2,1,0:T(8,128)(2,1)S(1)} %slice_bitcast_fusion.19), channel_id=1, source_target_pairs={{0,16},{4,20},{8,24},{12,28},{16,0},{20,4},{24,8},{28,12},{1,17},{... | collective-permute-start | bytes 884744 | tf_op jit(solution)/shard_map/ppermute | solution.py:481
  266.2 10.1 %collective-permute-start.44 = (bf16[2,96,768]{2,1,0:T(8,128)(2,1)S(1)}, bf16[2,96,768]{2,1,0:T(8,128)(2,1)S(1)}, u32[]{:S(2)}, u32[]{:S(2)}) collective-permute-start(bf16[2,96,768]{2,1,0:T(8,128)(2,1)S(1)} %slice_bitcast_fusion.18), channel_id=1, source_target_pairs={{0,8},{4,12},{8,0},{12,4},{16,24},{20,28},{24,16},{28,20},{1,9},{5... | collective-permute-start | bytes 884744 | tf_op jit(solution)/shard_map/ppermute | solution.py:481
  267.2 10.2 %collective-permute-start.42 = (bf16[192,512]{1,0:T(8,128)(2,1)S(1)}, bf16[192,512]{1,0:T(8,128)(2,1)S(1)}, u32[]{:S(2)}, u32[]{:S(2)}) collective-permute-start(bf16[192,512]{1,0:T(8,128)(2,1)S(1)} %get-tuple-element.397), channel_id=1, source_target_pairs={{0,1},{1,0},{2,3},{3,2},{4,5},{5,4},{6,7},{7,6},{8,9},{9,8},{10,11... | collective-permute-start | bytes 589832 | tf_op jit(solution)/shard_map/ppermute | solution.py:484
  276.3 18.1 %collective-permute-start.47 = (bf16[2,2,120,768]{3,2,1,0:T(8,128)(2,1)}, bf16[2,2,120,768]{3,2,1,0:T(8,128)(2,1)}, u32[]{:S(2)}, u32[]{:S(2)}) collective-permute-start(bf16[2,2,120,768]{3,2,1,0:T(8,128)(2,1)} %fusion.68), channel_id=1, source_target_pairs={{0,16},{4,20},{8,24},{12,28},{16,0},{20,4},{24,8},{28,12},{1,17},{... | collective-permute-start | bytes 2211848 | tf_op jit(solution)/shard_map/ppermute | solution.py:481
  276.9 17.7 %collective-permute-start.46 = (bf16[2,2,120,768]{3,2,1,0:T(8,128)(2,1)}, bf16[2,2,120,768]{3,2,1,0:T(8,128)(2,1)}, u32[]{:S(2)}, u32[]{:S(2)}) collective-permute-start(bf16[2,2,120,768]{3,2,1,0:T(8,128)(2,1)} %fusion.72), channel_id=1, source_target_pairs={{0,8},{4,12},{8,0},{12,4},{16,24},{20,28},{24,16},{28,20},{1,9},{5... | collective-permute-start | bytes 2211848 | tf_op jit(solution)/shard_map/ppermute | solution.py:481
  279.0 14.1 %collective-permute-start.45 = (bf16[2,96,768]{2,1,0:T(8,128)(2,1)}, bf16[2,96,768]{2,1,0:T(8,128)(2,1)}, u32[]{:S(2)}, u32[]{:S(2)}) collective-permute-start(bf16[2,96,768]{2,1,0:T(8,128)(2,1)} %fusion.77), channel_id=1, source_target_pairs={{0,1},{1,0},{2,3},{3,2},{4,5},{5,4},{6,7},{7,6},{8,9},{9,8},{10,11... | collective-permute-start | bytes 884744 | tf_op jit(solution)/shard_map/ppermute | solution.py:484
  295.8 3.5 collective-permute-start.48
  300.6 11.0 %collective-permute-start.49 = (bf16[2,120,768]{2,1,0:T(8,128)(2,1)S(1)}, bf16[2,120,768]{2,1,0:T(8,128)(2,1)S(1)}, u32[]{:S(2)}, u32[]{:S(2)}) collective-permute-start(bf16[2,120,768]{2,1,0:T(8,128)(2,1)S(1)} %slice_bitcast_fusion.14), channel_id=1, source_target_pairs={{0,16},{4,20},{8,24},{12,28},{16,0},{20,4},{24,8},{28,12},{1,17},{... | collective-permute-start | bytes 1105928 | tf_op jit(solution)/shard_map/ppermute | solution.py:481
  302.1 10.7 %collective-permute-start.50 = (bf16[2,120,768]{2,1,0:T(8,128)(2,1)S(1)}, bf16[2,120,768]{2,1,0:T(8,128)(2,1)S(1)}, u32[]{:S(2)}, u32[]{:S(2)}) collective-permute-start(bf16[2,120,768]{2,1,0:T(8,128)(2,1)S(1)} %slice_bitcast_fusion.13), channel_id=1, source_target_pairs={{0,8},{4,12},{8,0},{12,4},{16,24},{20,28},{24,16},{28,20},{1,9},{5... | collective-permute-start | bytes 1105928 | tf_op jit(solution)/shard_map/ppermute | solution.py:481
  304.7 13.2 %collective-permute-start.53 = (bf16[256,768]{1,0:T(8,128)(2,1)S(1)}, bf16[256,768]{1,0:T(8,128)(2,1)S(1)}, u32[]{:S(2)}, u32[]{:S(2)}) collective-permute-start(bf16[256,768]{1,0:T(8,128)(2,1)S(1)} %get-tuple-element.303), channel_id=1, source_target_pairs={{0,1},{1,0},{2,3},{3,2},{4,5},{5,4},{6,7},{7,6},{8,9},{9,8},{10,11... | collective-permute-start | bytes 1179656 | tf_op jit(solution)/shard_map/ppermute | solution.py:484
  312.9 13.8 %collective-permute-start.51 = (bf16[2,120,768]{2,1,0:T(8,128)(2,1)S(1)}, bf16[2,120,768]{2,1,0:T(8,128)(2,1)S(1)}, u32[]{:S(2)}, u32[]{:S(2)}) collective-permute-start(bf16[2,120,768]{2,1,0:T(8,128)(2,1)S(1)} %fusion.74), channel_id=1, source_target_pairs={{0,1},{1,0},{2,3},{3,2},{4,5},{5,4},{6,7},{7,6},{8,9},{9,8},{10,11... | collective-permute-start | bytes 1105928 | tf_op jit(solution)/shard_map/ppermute | solution.py:484
  314.5 11.2 %collective-permute-start.52 = (bf16[96,768]{1,0:T(8,128)(2,1)}, bf16[96,768]{1,0:T(8,128)(2,1)S(1)}, u32[]{:S(2)}, u32[]{:S(2)}) collective-permute-start(bf16[96,768]{1,0:T(8,128)(2,1)} %slice_bitcast_fusion.22), channel_id=1, source_target_pairs={{0,2},{1,3},{2,0},{3,1},{4,6},{5,7},{6,4},{7,5},{8,10},{9,11},{10,... | collective-permute-start | bytes 442376 | tf_op jit(solution)/shard_map/ppermute | solution.py:484
  316.6 10.4 %collective-permute-start.54 = (bf16[2,72,768]{2,1,0:T(8,128)(2,1)}, bf16[2,72,768]{2,1,0:T(8,128)(2,1)}, u32[]{:S(2)}, u32[]{:S(2)}) collective-permute-start(bf16[2,72,768]{2,1,0:T(8,128)(2,1)} %bitcast.293), channel_id=1, source_target_pairs={{0,8},{4,12},{8,0},{12,4},{16,24},{20,28},{24,16},{28,20},{1,9},{5... | collective-permute-start | bytes 663560 | tf_op jit(solution)/shard_map/ppermute | solution.py:481
  317.1 9.9 %collective-permute-start.55 = (bf16[2,72,768]{2,1,0:T(8,128)(2,1)}, bf16[2,72,768]{2,1,0:T(8,128)(2,1)}, u32[]{:S(2)}, u32[]{:S(2)}) collective-permute-start(bf16[2,72,768]{2,1,0:T(8,128)(2,1)} %bitcast.292), channel_id=1, source_target_pairs={{0,16},{4,20},{8,24},{12,28},{16,0},{20,4},{24,8},{28,12},{1,17},{... | collective-permute-start | bytes 663560 | tf_op jit(solution)/shard_map/ppermute | solution.py:481
  329.0 4.8 %collective-permute-start.58 = (bf16[72,768]{1,0:T(8,128)(2,1)S(1)}, bf16[72,768]{1,0:T(8,128)(2,1)S(1)}, u32[]{:S(2)}, u32[]{:S(2)}) collective-permute-start(bf16[72,768]{1,0:T(8,128)(2,1)S(1)} %select_bitcast_fusion), channel_id=1, source_target_pairs={{0,8},{4,12},{8,0},{12,4},{16,24},{20,28},{24,16},{28,20},{1,9},{5... | collective-permute-start | bytes 331784 | tf_op jit(solution)/shard_map/ppermute | solution.py:481
  330.6 4.7 %collective-permute-start.57 = (bf16[72,768]{1,0:T(8,128)(2,1)S(1)}, bf16[72,768]{1,0:T(8,128)(2,1)S(1)}, u32[]{:S(2)}, u32[]{:S(2)}) collective-permute-start(bf16[72,768]{1,0:T(8,128)(2,1)S(1)} %select_bitcast_fusion.1), channel_id=1, source_target_pairs={{0,16},{4,20},{8,24},{12,28},{16,0},{20,4},{24,8},{28,12},{1,17},{... | collective-permute-start | bytes 331784 | tf_op jit(solution)/shard_map/ppermute | solution.py:481
  331.3 10.0 %collective-permute-start.56 = (bf16[120,768]{1,0:T(8,128)(2,1)S(1)}, bf16[120,768]{1,0:T(8,128)(2,1)S(1)}, u32[]{:S(2)}, u32[]{:S(2)}) collective-permute-start(bf16[120,768]{1,0:T(8,128)(2,1)S(1)} %slice_bitcast_fusion.20), channel_id=1, source_target_pairs={{0,2},{1,3},{2,0},{3,1},{4,6},{5,7},{6,4},{7,5},{8,10},{9,11},{10,... | collective-permute-start | bytes 552968 | tf_op jit(solution)/shard_map/ppermute | solution.py:484
  336.3 11.1 %collective-permute-start.59 = (bf16[2,72,768]{2,1,0:T(8,128)(2,1)S(1)}, bf16[2,72,768]{2,1,0:T(8,128)(2,1)S(1)}, u32[]{:S(2)}, u32[]{:S(2)}) collective-permute-start(bf16[2,72,768]{2,1,0:T(8,128)(2,1)S(1)} %pad_maximum_fusion.20), channel_id=1, source_target_pairs={{2,0},{3,1},{4,6},{5,7},{10,8},{11,9},{12,14},{13,15},{18,16},{19,... | collective-permute-start | bytes 663560 | tf_op jit(solution)/shard_map/ppermute | solution.py:509
  337.7 4.2 %collective-permute-start.61 = (f32[12,768]{1,0:T(8,128)S(1)}, f32[12,768]{1,0:T(8,128)S(1)}, u32[]{:S(2)}, u32[]{:S(2)}) collective-permute-start(f32[12,768]{1,0:T(8,128)S(1)} %fusion.101), channel_id=1, source_target_pairs={{0,8},{4,12},{8,0},{12,4},{16,24},{20,28},{24,16},{28,20},{1,9},{5... | collective-permute-start | bytes 110600 | tf_op jit(solution)/shard_map/ppermute | solution.py:481
  347.7 7.8 %collective-permute-start.63 = (bf16[1,184,768]{2,1,0:T(8,128)(2,1)S(1)}, bf16[1,184,768]{2,1,0:T(8,128)(2,1)S(1)}, u32[]{:S(2)}, u32[]{:S(2)}) collective-permute-start(bf16[1,184,768]{2,1,0:T(8,128)(2,1)S(1)} %fusion.85), channel_id=1, source_target_pairs={{0,8},{4,12},{8,0},{12,4},{16,24},{20,28},{24,16},{28,20},{1,9},{5... | collective-permute-start | bytes 847880 | tf_op jit(solution)/shard_map/ppermute | solution.py:481
  348.3 7.1 %collective-permute-start.62 = (bf16[1,176,768]{2,1,0:T(8,128)(2,1)S(1)}, bf16[1,176,768]{2,1,0:T(8,128)(2,1)S(1)}, u32[]{:S(2)}, u32[]{:S(2)}) collective-permute-start(bf16[1,176,768]{2,1,0:T(8,128)(2,1)S(1)} %maximum_bitcast_fusion), channel_id=1, source_target_pairs={{0,16},{4,20},{8,24},{12,28},{16,0},{20,4},{24,8},{28,12},{1,17},{... | collective-permute-start | bytes 811016 | tf_op jit(solution)/shard_map/ppermute | solution.py:481
  348.8 6.0 %collective-permute-start.66 = (f32[12,768]{1,0:T(8,128)S(1)}, f32[12,768]{1,0:T(8,128)S(1)}, u32[]{:S(2)}, u32[]{:S(2)}) collective-permute-start(f32[12,768]{1,0:T(8,128)S(1)} %add.209), channel_id=1, source_target_pairs={{0,3},{1,2},{2,1},{3,0},{4,7},{5,6},{6,5},{7,4},{8,11},{9,10},{10,... | collective-permute-start | bytes 110600 | tf_op jit(solution)/shard_map/ppermute | solution.py:484
  348.8 6.1 %collective-permute-start.65 = (f32[12,768]{1,0:T(8,128)S(1)}, f32[12,768]{1,0:T(8,128)S(1)}, u32[]{:S(2)}, u32[]{:S(2)}) collective-permute-start(f32[12,768]{1,0:T(8,128)S(1)} %add.209), channel_id=1, source_target_pairs={{0,2},{1,3},{2,0},{3,1},{4,6},{5,7},{6,4},{7,5},{8,10},{9,11},{10,... | collective-permute-start | bytes 110600 | tf_op jit(solution)/shard_map/ppermute | solution.py:484
  350.6 4.8 %collective-permute-start.64 = (f32[12,768]{1,0:T(8,128)S(1)}, f32[12,768]{1,0:T(8,128)S(1)}, u32[]{:S(2)}, u32[]{:S(2)}) collective-permute-start(f32[12,768]{1,0:T(8,128)S(1)} %add.209), channel_id=1, source_target_pairs={{0,1},{1,0},{2,3},{3,2},{4,5},{5,4},{6,7},{7,6},{8,9},{9,8},{10,11... | collective-permute-start | bytes 110600 | tf_op jit(solution)/shard_map/ppermute | solution.py:484
  355.6 15.4 %collective-permute-start.68 = (bf16[2,184,768]{2,1,0:T(8,128)(2,1)S(1)}, bf16[2,184,768]{2,1,0:T(8,128)(2,1)S(1)}, u32[]{:S(2)}, u32[]{:S(2)}) collective-permute-start(bf16[2,184,768]{2,1,0:T(8,128)(2,1)S(1)} %maximum_select_fusion.3), channel_id=1, source_target_pairs={{0,16},{4,20},{8,24},{12,28},{16,0},{20,4},{24,8},{28,12},{1,17},{... | collective-permute-start | bytes 1695752 | tf_op jit(solution)/shard_map/ppermute | solution.py:481
  357.2 13.9 %collective-permute-start.67 = (bf16[2,176,768]{2,1,0:T(8,128)(2,1)S(1)}, bf16[2,176,768]{2,1,0:T(8,128)(2,1)S(1)}, u32[]{:S(2)}, u32[]{:S(2)}) collective-permute-start(bf16[2,176,768]{2,1,0:T(8,128)(2,1)S(1)} %maximum_select_fusion.4), channel_id=1, source_target_pairs={{0,8},{4,12},{8,0},{12,4},{16,24},{20,28},{24,16},{28,20},{1,9},{5... | collective-permute-start | bytes 1622024 | tf_op jit(solution)/shard_map/ppermute | solution.py:481
  358.7 12.4 %collective-permute-start.69 = (bf16[256,768]{1,0:T(8,128)(2,1)S(1)}, bf16[256,768]{1,0:T(8,128)(2,1)S(1)}, u32[]{:S(2)}, u32[]{:S(2)}) collective-permute-start(bf16[256,768]{1,0:T(8,128)(2,1)S(1)} %copy-done.49), channel_id=1, source_target_pairs={{0,0},{4,1},{1,2},{5,3},{2,4},{6,5},{3,6},{7,7},{8,8},{12,9},{9,10... | collective-permute-start | bytes 1179656 | tf_op jit(solution)/shard_map/ppermute | solution.py:498
  359.4 11.7 %collective-permute-start.70 = (f32[12,768]{1,0:T(8,128)S(1)}, f32[12,768]{1,0:T(8,128)S(1)}, u32[]{:S(2)}, u32[]{:S(2)}) collective-permute-start(f32[12,768]{1,0:T(8,128)S(1)} %add_add_fusion), channel_id=1, source_target_pairs={{0,16},{4,20},{8,24},{12,28},{16,0},{20,4},{24,8},{28,12},{1,17},{... | collective-permute-start | bytes 110600 | tf_op jit(solution)/shard_map/ppermute | solution.py:481
  372.0 4.5 %collective-permute-start.72 = (bf16[2,2,184,768]{3,2,1,0:T(8,128)(2,1)S(1)}, bf16[2,2,184,768]{3,2,1,0:T(8,128)(2,1)S(1)}, u32[]{:S(2)}, u32[]{:S(2)}) collective-permute-start(bf16[2,2,184,768]{3,2,1,0:T(8,128)(2,1)S(1)} %maximum_select_fusion.two_ref), channel_id=1, source_target_pairs={{0,4},{4,0},{8,12},{12,8},{16,20},{20,16},{24,28},{28,24},{1,5},{5... | collective-permute-start | bytes 3391496 | tf_op jit(solution)/shard_map/ppermute | solution.py:481
  372.3 4.2 %collective-permute-start.71 = (bf16[2,2,176,768]{3,2,1,0:T(8,128)(2,1)S(1)}, bf16[2,2,176,768]{3,2,1,0:T(8,128)(2,1)}, u32[]{:S(2)}, u32[]{:S(2)}) collective-permute-start(bf16[2,2,176,768]{3,2,1,0:T(8,128)(2,1)S(1)} %maximum_select_fusion.1.one_ref), channel_id=1, source_target_pairs={{0,4},{4,0},{8,12},{12,8},{16,20},{20,16},{24,28},{28,24},{1,5},{5... | collective-permute-start | bytes 3244040 | tf_op jit(solution)/shard_map/ppermute | solution.py:481
  (74 other events, 446.9 us)

commit v4 on v3

--- a/solution.py
+++ b/solution.py
@@ -253,7 +253,7 @@
     half = 0.5 * (1.0 + bent)
     act = (value * half).astype(BF)
     keep_or_send(step_at, act, act_ref, send_ref)
-    slope = half + (0.5 * value) * (1.0 - bent * bent) * (CURVE + 3.0 * CURVE * CUBE * square)
+    slope = half + half * ((1.0 - bent) * (value * (CURVE + 3.0 * CURVE * CUBE * square)))
     slope_ref[...] = slope.astype(BF)
     next_ref[...] += dot(act, proj_ref[...], 1, 0)
 

time: 390 us -> 390 us (level)
  no operation moved by 1% of the time
where the time goes in v4:
time: 390 us; the launch traced here: 384 us
  Pallas kernels  106 us (27%)
  waiting for transfers between devices  94.3 us (24%)
  starting transfers between devices  79.9 us (20%)
  other arithmetic  51.1 us (13%)
  local copies, waits for them, and re-layouts  36.6 us (9%)
  matrix products  11.5 us (3%)
  between operations  4.11 us (1%)
    ppermute x19, waiting for transfers between devices, tensor(): lax.ppermute(value, 'tensor', [(i, i ^ bit) for i in range(self.shards)])  49 us
    ppermute x48, waiting for transfers between devices, dp(): lax.ppermute(value, 'dp', [(i, i ^ bit) for i in range(self.members)])  39.7 us
    ppermute x19, starting transfers between devices, tensor(): lax.ppermute(value, 'tensor', [(i, i ^ bit) for i in range(self.shards)])  33.3 us
    ppermute x48, starting transfers between devices, dp(): lax.ppermute(value, 'dp', [(i, i ^ bit) for i in range(self.members)])  32.2 us
    pallas_call x2, Pallas kernels, feed(): pl.pallas_call(feed_kernel, grid=(hidden // step_size,), in_specs=[whole(...  25.7 us
    pallas_call x2, Pallas kernels, attend_back(): pl.pallas_call(attend_back_kernel, in_specs=[SM] + [VM] * 4, out_specs=[V...  25.3 us
    pallas_call x2, Pallas kernels, feed_back(): pl.pallas_call(feed_back_kernel, grid=(hidden // step_size,), in_specs=[w...  22.6 us
    pallas_call x2, Pallas kernels, attend(): pl.pallas_call(attend_kernel, in_specs=[SM] + [VM] * 6, out_specs=[VM] *...  20.6 us
  transfers between devices with their start and end apart: 73, of which 32 were waited for; matrix products, arithmetic and copies ran while one was open for 18% of the time, Pallas kernels for 19%

profile of v4, /device:TPU:0, one launch (start us, length us, event | category | flops | bytes accessed | tf_op | source)
XLA Modules:
  0.0 383.6 jit_solution(10853336067582773944)
XLA Ops:
  1.4 1.6 copy.90
  3.8 3.7 collective-permute-start.15
  11.7 5.6 %collective-permute-start.5 = (bf16[152,768]{1,0:T(8,128)(2,1)}, bf16[152,768]{1,0:T(8,128)(2,1)}, u32[]{:S(2)}, u32[]{:S(2)}) collective-permute-start(bf16[152,768]{1,0:T(8,128)(2,1)} %fusion.86), channel_id=1, source_target_pairs={{0,2},{1,3},{6,4},{7,5},{8,10},{9,11},{14,12},{15,13},{16,18},{17,... | collective-permute-start | bytes 700424 | tf_op jit(solution)/shard_map/ppermute | solution.py:509
  17.3 1.6 collective-permute-start.1
  29.0 1.9 collective-permute-start.16
  34.1 4.8 %collective-permute-start.3 = (bf16[256,768]{1,0:T(8,128)(2,1)}, bf16[256,768]{1,0:T(8,128)(2,1)}, u32[]{:S(2)}, u32[]{:S(2)}) collective-permute-start(bf16[256,768]{1,0:T(8,128)(2,1)} %add_convert_fusion.own_ref), channel_id=1, source_target_pairs={{0,1},{1,0},{2,3},{3,2},{4,5},{5,4},{6,7},{7,6},{8,9},{9,8},{10,11... | collective-permute-start | bytes 1179656 | tf_op jit(solution)/shard_map/ppermute | solution.py:484
  39.9 1.9 maximum_select_fusion.5
  41.8 1.5 collective-permute-start.7
  45.9 4.0 %collective-permute-done.11 = bf16[2,120,768]{2,1,0:T(8,128)(2,1)} collective-permute-done((bf16[2,120,768]{2,1,0:T(8,128)(2,1)S(1)}, bf16[2,120,768]{2,1,0:T(8,128)(2,1)}, u32[]{:S(2)}, u32[]{:S(2)}) %collective-permute-start.11) | collective-permute-done | bytes 368672 | tf_op jit(solution)/shard_map/ppermute | solution.py:484
  51.0 1.7 collective-permute-start.12
  52.8 1.8 constant_dynamic-update-slice_fusion.4
  54.6 2.6 collective-permute-done.3.far_ref
  58.2 1.6 collective-permute-start.18
  59.8 2.0 fusion.57
  61.9 5.6 %collective-permute-done.12 = bf16[3,120,768]{2,1,0:T(8,128)(2,1)S(1)} collective-permute-done((bf16[3,120,768]{2,1,0:T(8,128)(2,1)S(1)}, bf16[3,120,768]{2,1,0:T(8,128)(2,1)S(1)}, u32[]{:S(2)}, u32[]{:S(2)}) %collective-permute-start.12) | collective-permute-done | bytes 552992 | tf_op jit(solution)/shard_map/ppermute | solution.py:481
  72.0 10.5 %attend.2 = (bf16[1024,768]{1,0:T(8,128)(2,1)}, bf16[576,1024]{1,0:T(8,128)(2,1)}, bf16[192,1024]{1,0:T(8,128)(2,1)}, f32[3,1024]{1,0:T(4,128)}) custom-call(s32[2]{0:T(128)} %pad_add_fusion.1.scalar_ref, bf16[256,768]{1,0:T(8,128)(2,1)} %add_convert_fusion.own_ref, bf16[256,768]{1,0:T(8,128)(2,1)} %collective-permute-done.2.near_ref, ...), custom_call_target="tpu_custom_call" | custom-call | flops 2113929216 | bytes 4718592 | tf_op jit(solution)/shard_map/attend/pallas_call | solution.py:113
  83.5 2.5 collective-permute-start.8
  86.9 2.7 collective-permute-done.8
  90.3 2.5 pad_maximum_fusion.2
  94.3 2.1 fusion.105
  96.5 1.6 pad_maximum_fusion.1
  102.3 4.5 %maximum_maximum_fusion = bf16[8,4,96,768]{3,2,1,0:T(8,128)(2,1)} fusion(bf16[4,3,96,768]{3,2,1,0:T(8,128)(2,1)} %collective-permute-done.19, bf16[2,3,96,768]{3,2,1,0:T(8,128)(2,1)} %collective-permute-done.18, bf16[1,3,96,768]{3,2,1,0:T(8,128)(2,1)S(1)} %bitcast.258, bf16[1,3,96,768]{3,2,1,0:T(8,128)(2,1)S(1)} %fusion.113, ...), kind=kLoop, calls=%fused_computation | loop fusion | flops 9437184 | bytes 9437184 | tf_op jit(solution)/shard_map/concatenate | solution.py:854
  106.9 1.8 constant_dynamic-update-slice_fusion
  109.1 2.6 pad_maximum_fusion
  112.9 12.9 %feed.2 = (f32[256,768]{1,0:T(8,128)}, bf16[256,768]{1,0:T(8,128)(2,1)}, bf16[256,1536]{1,0:T(8,128)(2,1)}, bf16[256,384]{1,0:T(8,128)(2,1)}, bf16[256,2688]{1,0...) custom-call(bf16[768,256]{1,0:T(8,128)(2,1)} %bitcast.273, ...), custom_call_target="tpu_custom_call" | custom-call | flops 2415919104 | bytes 14155776 | tf_op jit(solution)/shard_map/feed/pallas_call | solution.py:272
  127.1 10.4 %collective-permute-done.21.far_ref = bf16[256,768]{1,0:T(8,128)(2,1)S(1)} collective-permute-done((bf16[256,768]{1,0:T(8,128)(2,1)}, bf16[256,768]{1,0:T(8,128)(2,1)S(1)}, u32[]{:S(2)}, u32[]{:S(2)}) %collective-permute-start.21) | collective-permute-done | bytes 393248 | tf_op jit(solution)/shard_map/ppermute | solution.py:484
  137.6 1.7 collective-permute-done.22.both_ref
  140.2 10.1 %attend.3 = (bf16[1024,768]{1,0:T(8,128)(2,1)}, bf16[576,1024]{1,0:T(8,128)(2,1)}, bf16[192,1024]{1,0:T(8,128)(2,1)}, f32[3,1024]{1,0:T(4,128)}) custom-call(s32[2]{0:T(128)} %pad_add_fusion.1.scalar_ref, bf16[256,768]{1,0:T(8,128)(2,1)} %get-tuple-element.209.own_ref, bf16[256,768]{1,0:T(8,128)(2,1)} %copy-done.52, bf16[256,768]{1,0:T(8,128)(2,1)} %copy-done.51, ...), custom_call_target="tpu_custom_call" | custom-call | flops 2113929216 | bytes 4718592 | tf_op jit(solution)/shard_map/attend/pallas_call | solution.py:113
  151.4 3.3 collective-permute-start.25
  155.6 3.3 collective-permute-done.25
  158.9 1.9 collective-permute-start.26
  163.1 12.8 %feed.3 = (f32[256,768]{1,0:T(8,128)}, bf16[256,768]{1,0:T(8,128)(2,1)}, bf16[256,1536]{1,0:T(8,128)(2,1)}, bf16[256,384]{1,0:T(8,128)(2,1)}, bf16[256,2688]{1,0...) custom-call(bf16[768,256]{1,0:T(8,128)(2,1)} %bitcast.274, ...), custom_call_target="tpu_custom_call" | custom-call | flops 2415919104 | bytes 14155776 | tf_op jit(solution)/shard_map/feed/pallas_call | solution.py:272
  176.3 4.5 %collective-permute-start.29 = (bf16[256,768]{1,0:T(8,128)(2,1)}, bf16[256,768]{1,0:T(8,128)(2,1)}, u32[]{:S(2)}, u32[]{:S(2)}) collective-permute-start(bf16[256,768]{1,0:T(8,128)(2,1)} %get-tuple-element.227), channel_id=1, source_target_pairs={{0,0},{4,1},{1,2},{5,3},{2,4},{6,5},{3,6},{7,7},{8,8},{12,9},{9,10... | collective-permute-start | bytes 1179656 | tf_op jit(solution)/shard_map/ppermute | solution.py:498
  180.8 11.3 %feed_back.2 = (bf16[256,1536]{1,0:T(8,128)(2,1)}, bf16[256,1536]{1,0:T(8,128)(2,1)}, f32[1,3072]{1,0:T(1,128)}, f32[256,768]{1,0:T(8,128)}, bf16[256,768]{1,0:T...) custom-call(f32[256,768]{1,0:T(8,128)} %get-tuple-element.220.grad_ref, ...), custom_call_target="tpu_custom_call" | custom-call | flops 2415919104 | bytes 14155776 | tf_op jit(solution)/shard_map/feed_back/pallas_call | solution.py:341
  196.9 5.8 %collective-permute-done.31 = bf16[192,512]{1,0:T(8,128)(2,1)S(1)} collective-permute-done((bf16[192,512]{1,0:T(8,128)(2,1)S(1)}, bf16[192,512]{1,0:T(8,128)(2,1)S(1)}, u32[]{:S(2)}, u32[]{:S(2)}) %collective-permute-start.31) | collective-permute-done | bytes 196640 | tf_op jit(solution)/shard_map/ppermute | solution.py:484
  204.0 12.6 %attend_back.2 = (bf16[576,1024]{1,0:T(8,128)(2,1)}, f32[576,1]{1,0:T(8,128)}, bf16[1024,768]{1,0:T(8,128)(2,1)}) custom-call(s32[2]{0:T(128)} %pad_add_fusion.1.scalar_ref, bf16[576,1024]{1,0:T(8,128)(2,1)} %get-tuple-element.213.qkv_ref, bf16[192,1024]{1,0:T(8,128)(2,1)} %pad_maximum_fusion.14.grad_ref, f32[3,1024]{1,0:T(4,128)} %get-tuple-element.232.lse_ref, ...), custom_call_target="tpu_custom_call" | custom-call | flops 3321888768 | bytes 5898240 | tf_op jit(solution)/shard_map/attend_back/pallas_call | solution.py:190
  218.1 2.3 collective-permute-done.34
  222.6 10.0 %collective-permute-done.35.far_ref = bf16[256,768]{1,0:T(8,128)(2,1)} collective-permute-done((bf16[256,768]{1,0:T(8,128)(2,1)S(1)}, bf16[256,768]{1,0:T(8,128)(2,1)}, u32[]{:S(2)}, u32[]{:S(2)}) %collective-permute-start.35) | collective-permute-done | bytes 393248 | tf_op jit(solution)/shard_map/ppermute | solution.py:484
  232.7 3.3 norm_back.2
  236.2 1.8 collective-permute-done.36
  238.0 3.7 convolution_convert_fusion.1
  246.0 11.3 %feed_back.3 = (bf16[256,1536]{1,0:T(8,128)(2,1)}, bf16[256,1536]{1,0:T(8,128)(2,1)}, f32[1,3072]{1,0:T(1,128)}, f32[256,768]{1,0:T(8,128)}, bf16[256,768]{1,0:T...) custom-call(f32[256,768]{1,0:T(8,128)} %get-tuple-element.245.grad_ref, ...), custom_call_target="tpu_custom_call" | custom-call | flops 2415919104 | bytes 14155776 | tf_op jit(solution)/shard_map/feed_back/pallas_call | solution.py:341
  257.3 1.6 collective-permute-done.37
  268.8 3.9 %convolution_convert_fusion = bf16[1536,768]{1,0:T(8,128)(2,1)S(1)} fusion(bf16[256,1536]{1,0:T(8,128)(2,1)} %collective-permute-done.32, bf16[256,1536]{1,0:T(8,128)(2,1)S(1)} %copy-done.42, bf16[256,1536]{1,0:T(8,128)(2,1)S(1)} %collective-permute-done.40, bf16[256,1536]{1,0:T(8,128)(2,1)S(1)} %copy-done.44, bf16[256,768]{1,0:T(8,128)(2,1)S(1)} %slice-done.3, ...), kind=kOutput, calls=%fused_computation.5 | convolution fusion | flops 2435973120 | bytes 7077888 | tf_op jit(solution)/shard_map/dot_general | solution.py:21
  272.7 1.9 fusion.50
  280.6 12.7 %attend_back.3 = (bf16[576,1024]{1,0:T(8,128)(2,1)}, f32[576,1]{1,0:T(8,128)}, bf16[1024,768]{1,0:T(8,128)(2,1)}) custom-call(s32[2]{0:T(128)} %pad_add_fusion.1.scalar_ref, bf16[576,1024]{1,0:T(8,128)(2,1)} %get-tuple-element.269.qkv_ref, bf16[192,1024]{1,0:T(8,128)(2,1)} %pad_maximum_fusion.16.grad_ref, f32[3,1024]{1,0:T(4,128)} %get-tuple-element.278.lse_ref, ...), custom_call_target="tpu_custom_call" | custom-call | flops 3321888768 | bytes 5898240 | tf_op jit(solution)/shard_map/attend_back/pallas_call | solution.py:190
  296.2 1.8 fusion.44
  300.9 1.5 collective-permute-start.49
  302.9 2.0 fusion.45
  307.2 4.7 %collective-permute-done.49 = bf16[2,120,768]{2,1,0:T(8,128)(2,1)S(1)} collective-permute-done((bf16[2,120,768]{2,1,0:T(8,128)(2,1)S(1)}, bf16[2,120,768]{2,1,0:T(8,128)(2,1)S(1)}, u32[]{:S(2)}, u32[]{:S(2)}) %collective-permute-start.49) | collective-permute-done | bytes 368672 | tf_op jit(solution)/shard_map/ppermute | solution.py:481
  314.7 2.1 collective-permute-start.52
  318.8 3.3 norm_back.3
  322.2 3.8 collective-permute-done.52
  329.3 1.6 collective-permute-start.58
  331.5 1.8 collective-permute-start.56
  338.6 3.0 collective-permute-done.56
  342.1 5.6 %collective-permute-done.59 = bf16[2,72,768]{2,1,0:T(8,128)(2,1)S(1)} collective-permute-done((bf16[2,72,768]{2,1,0:T(8,128)(2,1)S(1)}, bf16[2,72,768]{2,1,0:T(8,128)(2,1)S(1)}, u32[]{:S(2)}, u32[]{:S(2)}) %collective-permute-start.59) | collective-permute-done | bytes 221216 | tf_op jit(solution)/shard_map/ppermute | solution.py:509
  349.0 1.8 collective-permute-start.65
  350.8 2.6 collective-permute-start.64
  353.4 1.7 collective-permute-done.66
  355.9 1.6 collective-permute-start.68
  360.2 11.2 %collective-permute-done.70 = f32[12,768]{1,0:T(8,128)S(1)} collective-permute-done((f32[12,768]{1,0:T(8,128)S(1)}, f32[12,768]{1,0:T(8,128)S(1)}, u32[]{:S(2)}, u32[]{:S(2)}) %collective-permute-start.70) | collective-permute-done | bytes 36896 | tf_op jit(solution)/shard_map/ppermute | solution.py:481
  375.2 1.7 collective-permute-done.71.one_far_ref
  377.9 5.2 %finish.1 = (f32[768,768]{1,0:T(8,128)}, f32[192,768]{1,0:T(8,128)}, f32[768,768]{1,0:T(8,128)}, f32[576,768]{1,0:T(8,128)}, f32[256,768]{1,0:T(8,128)}, /*index=5*/bf16[256,768]{1,0:T(8,128)(2,1)}) custom-call(s32[2]{0:T(128)} %pad_add_fusion.scalar_ref, bf16[2,2,176,768]{3,2,1,0:T(8,128)(2,1)} %copy-done.4, bf16[2,2,184,768]{3,2,1,0:T(8,128)(2,1)} %copy-done.3, ...), custom_call_target="tpu_custom_call" | custom-call | bytes 9437184 | tf_op jit(solution)/shard_map/finish/pallas_call | solution.py:443
  (423 shorter events, 106.3 us)
Async XLA Ops:
  3.2 24.5 %collective-permute-start = (s32[1]{0:T(128)}, s32[1]{0:T(128)}, u32[]{:S(2)}, u32[]{:S(2)}) collective-permute-start(s32[1]{0:T(128)} %param.20), channel_id=1, source_target_pairs={{0,4},{4,0},{8,12},{12,8},{16,20},{20,16},{24,28},{28,24},{1,5},{5... | collective-permute-start | bytes 20 | tf_op jit(solution)/shard_map/ppermute | solution.py:481
  3.8 25.2 %collective-permute-start.15 = (bf16[104,768]{1,0:T(8,128)(2,1)S(1)}, bf16[104,768]{1,0:T(8,128)(2,1)S(1)}, u32[]{:S(2)}, u32[]{:S(2)}) collective-permute-start(bf16[104,768]{1,0:T(8,128)(2,1)S(1)} %concatenate.157), channel_id=1, source_target_pairs={{0,2},{1,3},{2,0},{3,1},{4,6},{5,7},{6,4},{7,5},{8,10},{9,11},{10,... | collective-permute-start | bytes 479240 | tf_op jit(solution)/shard_map/ppermute | solution.py:484
  9.8 21.2 %collective-permute-start.10 = (bf16[120,768]{1,0:T(8,128)(2,1)}, bf16[120,768]{1,0:T(8,128)(2,1)S(1)}, u32[]{:S(2)}, u32[]{:S(2)}) collective-permute-start(bf16[120,768]{1,0:T(8,128)(2,1)} %get-tuple-element.415), channel_id=1, source_target_pairs={{0,2},{1,3},{2,0},{3,1},{4,6},{5,7},{6,4},{7,5},{8,10},{9,11},{10,... | collective-permute-start | bytes 552968 | tf_op jit(solution)/shard_map/ppermute | solution.py:484
  11.7 19.5 %collective-permute-start.5 = (bf16[152,768]{1,0:T(8,128)(2,1)}, bf16[152,768]{1,0:T(8,128)(2,1)}, u32[]{:S(2)}, u32[]{:S(2)}) collective-permute-start(bf16[152,768]{1,0:T(8,128)(2,1)} %fusion.86), channel_id=1, source_target_pairs={{0,2},{1,3},{6,4},{7,5},{8,10},{9,11},{14,12},{15,13},{16,18},{17,... | collective-permute-start | bytes 700424 | tf_op jit(solution)/shard_map/ppermute | solution.py:509
  17.3 15.4 %collective-permute-start.1 = (bf16[256,768]{1,0:T(8,128)(2,1)}, bf16[256,768]{1,0:T(8,128)(2,1)S(1)}, u32[]{:S(2)}, u32[]{:S(2)}) collective-permute-start(bf16[256,768]{1,0:T(8,128)(2,1)} %param.19), channel_id=1, source_target_pairs={{0,0},{1,4},{2,1},{3,5},{4,2},{5,6},{6,3},{7,7},{8,8},{9,12},{10,9... | collective-permute-start | bytes 1179656 | tf_op jit(solution)/shard_map/ppermute | solution.py:495
  29.0 14.3 %collective-permute-start.16 = (bf16[2,104,768]{2,1,0:T(8,128)(2,1)S(1)}, bf16[2,104,768]{2,1,0:T(8,128)(2,1)S(1)}, u32[]{:S(2)}, u32[]{:S(2)}) collective-permute-start(bf16[2,104,768]{2,1,0:T(8,128)(2,1)S(1)} %pad_maximum_fusion.18), channel_id=1, source_target_pairs={{0,1},{1,0},{2,3},{3,2},{4,5},{5,4},{6,7},{7,6},{8,9},{9,8},{10,11... | collective-permute-start | bytes 958472 | tf_op jit(solution)/shard_map/ppermute | solution.py:484
  31.0 18.9 %collective-permute-start.11 = (bf16[2,120,768]{2,1,0:T(8,128)(2,1)S(1)}, bf16[2,120,768]{2,1,0:T(8,128)(2,1)}, u32[]{:S(2)}, u32[]{:S(2)}) collective-permute-start(bf16[2,120,768]{2,1,0:T(8,128)(2,1)S(1)} %pad_maximum_fusion.17), channel_id=1, source_target_pairs={{0,1},{1,0},{2,3},{3,2},{4,5},{5,4},{6,7},{7,6},{8,9},{9,8},{10,11... | collective-permute-start | bytes 1105928 | tf_op jit(solution)/shard_map/ppermute | solution.py:484
  31.2 8.6 %collective-permute-start.6 = (bf16[152,768]{1,0:T(8,128)(2,1)}, bf16[152,768]{1,0:T(8,128)(2,1)S(1)}, u32[]{:S(2)}, u32[]{:S(2)}) collective-permute-start(bf16[152,768]{1,0:T(8,128)(2,1)} %collective-permute-done.5), channel_id=1, source_target_pairs={{0,8},{4,12},{8,0},{12,4},{16,24},{20,28},{24,16},{28,20},{1,9},{5... | collective-permute-start | bytes 700424 | tf_op jit(solution)/shard_map/ppermute | solution.py:481
  34.1 23.1 %collective-permute-start.3 = (bf16[256,768]{1,0:T(8,128)(2,1)}, bf16[256,768]{1,0:T(8,128)(2,1)}, u32[]{:S(2)}, u32[]{:S(2)}) collective-permute-start(bf16[256,768]{1,0:T(8,128)(2,1)} %add_convert_fusion.own_ref), channel_id=1, source_target_pairs={{0,1},{1,0},{2,3},{3,2},{4,5},{5,4},{6,7},{7,6},{8,9},{9,8},{10,11... | collective-permute-start | bytes 1179656 | tf_op jit(solution)/shard_map/ppermute | solution.py:484
  38.9 33.1 %collective-permute-start.2 = (bf16[256,768]{1,0:T(8,128)(2,1)}, bf16[256,768]{1,0:T(8,128)(2,1)}, u32[]{:S(2)}, u32[]{:S(2)}) collective-permute-start(bf16[256,768]{1,0:T(8,128)(2,1)} %add_convert_fusion.own_ref), channel_id=1, source_target_pairs={{0,4},{4,0},{8,12},{12,8},{16,20},{20,16},{24,28},{28,24},{1,5},{5... | collective-permute-start | bytes 1179656 | tf_op jit(solution)/shard_map/ppermute | solution.py:481
  41.8 18.0 %collective-permute-start.7 = (bf16[304,768]{1,0:T(8,128)(2,1)}, bf16[304,768]{1,0:T(8,128)(2,1)}, u32[]{:S(2)}, u32[]{:S(2)}) collective-permute-start(bf16[304,768]{1,0:T(8,128)(2,1)} %maximum_select_fusion.5), channel_id=1, source_target_pairs={{0,16},{4,20},{8,24},{12,28},{16,0},{20,4},{24,8},{28,12},{1,17},{... | collective-permute-start | bytes 1400840 | tf_op jit(solution)/shard_map/ppermute | solution.py:481
  44.3 12.9 %collective-permute-start.17 = (bf16[3,96,768]{2,1,0:T(8,128)(2,1)}, bf16[3,96,768]{2,1,0:T(8,128)(2,1)S(1)}, u32[]{:S(2)}, u32[]{:S(2)}) collective-permute-start(bf16[3,96,768]{2,1,0:T(8,128)(2,1)} %pad_maximum_fusion.11), channel_id=1, source_target_pairs={{0,8},{4,12},{8,0},{12,4},{16,24},{20,28},{24,16},{28,20},{1,9},{5... | collective-permute-start | bytes 1327112 | tf_op jit(solution)/shard_map/ppermute | solution.py:481
  51.0 16.4 %collective-permute-start.12 = (bf16[3,120,768]{2,1,0:T(8,128)(2,1)S(1)}, bf16[3,120,768]{2,1,0:T(8,128)(2,1)S(1)}, u32[]{:S(2)}, u32[]{:S(2)}) collective-permute-start(bf16[3,120,768]{2,1,0:T(8,128)(2,1)S(1)} %get-tuple-element.393), channel_id=1, source_target_pairs={{0,16},{4,20},{8,24},{12,28},{16,0},{20,4},{24,8},{28,12},{1,17},{... | collective-permute-start | bytes 1658888 | tf_op jit(solution)/shard_map/ppermute | solution.py:481
  57.3 14.7 %collective-permute-start.4 = (bf16[256,768]{1,0:T(8,128)(2,1)}, bf16[256,768]{1,0:T(8,128)(2,1)}, u32[]{:S(2)}, u32[]{:S(2)}) collective-permute-start(bf16[256,768]{1,0:T(8,128)(2,1)} %collective-permute-done.3.far_ref), channel_id=1, source_target_pairs={{0,4},{4,0},{8,12},{12,8},{16,20},{20,16},{24,28},{28,24},{1,5},{5... | collective-permute-start | bytes 1179656 | tf_op jit(solution)/shard_map/ppermute | solution.py:481
  58.2 32.1 %collective-permute-start.18 = (bf16[2,3,96,768]{3,2,1,0:T(8,128)(2,1)}, bf16[2,3,96,768]{3,2,1,0:T(8,128)(2,1)}, u32[]{:S(2)}, u32[]{:S(2)}) collective-permute-start(bf16[2,3,96,768]{3,2,1,0:T(8,128)(2,1)} %pad_maximum_fusion.6), channel_id=1, source_target_pairs={{0,16},{4,20},{8,24},{12,28},{16,0},{20,4},{24,8},{28,12},{1,17},{... | collective-permute-start | bytes 2654216 | tf_op jit(solution)/shard_map/ppermute | solution.py:481
  68.5 25.8 %collective-permute-start.13 = (bf16[2,3,120,768]{3,2,1,0:T(8,128)(2,1)}, bf16[2,3,120,768]{3,2,1,0:T(8,128)(2,1)}, u32[]{:S(2)}, u32[]{:S(2)}) collective-permute-start(bf16[2,3,120,768]{3,2,1,0:T(8,128)(2,1)} %pad_maximum_fusion.5), channel_id=1, source_target_pairs={{0,8},{4,12},{8,0},{12,4},{16,24},{20,28},{24,16},{28,20},{1,9},{5... | collective-permute-start | bytes 3317768 | tf_op jit(solution)/shard_map/ppermute | solution.py:481
  83.5 6.2 %collective-permute-start.8 = (bf16[192,512]{1,0:T(8,128)(2,1)S(1)}, bf16[192,512]{1,0:T(8,128)(2,1)S(1)}, u32[]{:S(2)}, u32[]{:S(2)}) collective-permute-start(bf16[192,512]{1,0:T(8,128)(2,1)S(1)} %slice.383), channel_id=1, source_target_pairs={{0,1},{1,0},{2,3},{3,2},{4,5},{5,4},{6,7},{7,6},{8,9},{9,8},{10,11... | collective-permute-start | bytes 589832 | tf_op jit(solution)/shard_map/ppermute | solution.py:484
  90.3 8.5 %collective-permute-start.9 = (bf16[384,256]{1,0:T(8,128)(2,1)}, bf16[384,256]{1,0:T(8,128)(2,1)}, u32[]{:S(2)}, u32[]{:S(2)}) collective-permute-start(bf16[384,256]{1,0:T(8,128)(2,1)} %pad_maximum_fusion.22), channel_id=1, source_target_pairs={{0,4},{4,0},{8,12},{12,8},{16,20},{20,16},{24,28},{28,24},{1,5},{5... | collective-permute-start | bytes 589832 | tf_op jit(solution)/shard_map/ppermute | solution.py:481
  92.9 9.5 %collective-permute-start.19 = (bf16[4,3,96,768]{3,2,1,0:T(8,128)(2,1)}, bf16[4,3,96,768]{3,2,1,0:T(8,128)(2,1)}, u32[]{:S(2)}, u32[]{:S(2)}) collective-permute-start(bf16[4,3,96,768]{3,2,1,0:T(8,128)(2,1)} %pad_maximum_fusion.2), channel_id=1, source_target_pairs={{0,4},{4,0},{8,12},{12,8},{16,20},{20,16},{24,28},{28,24},{1,5},{5... | collective-permute-start | bytes 5308424 | tf_op jit(solution)/shard_map/ppermute | solution.py:481
  98.1 8.8 %collective-permute-start.14 = (bf16[4,3,120,768]{3,2,1,0:T(8,128)(2,1)}, bf16[4,3,120,768]{3,2,1,0:T(8,128)(2,1)}, u32[]{:S(2)}, u32[]{:S(2)}) collective-permute-start(bf16[4,3,120,768]{3,2,1,0:T(8,128)(2,1)} %pad_maximum_fusion.1), channel_id=1, source_target_pairs={{0,4},{4,0},{8,12},{12,8},{16,20},{20,16},{24,28},{28,24},{1,5},{5... | collective-permute-start | bytes 6635528 | tf_op jit(solution)/shard_map/ppermute | solution.py:481
  125.8 11.8 %collective-permute-start.21 = (bf16[256,768]{1,0:T(8,128)(2,1)}, bf16[256,768]{1,0:T(8,128)(2,1)S(1)}, u32[]{:S(2)}, u32[]{:S(2)}) collective-permute-start(bf16[256,768]{1,0:T(8,128)(2,1)} %get-tuple-element.209.own_ref), channel_id=1, source_target_pairs={{0,1},{1,0},{2,3},{3,2},{4,5},{5,4},{6,7},{7,6},{8,9},{9,8},{10,11... | collective-permute-start | bytes 1179656 | tf_op jit(solution)/shard_map/ppermute | solution.py:484
  126.9 10.7 %collective-permute-start.20 = (bf16[256,768]{1,0:T(8,128)(2,1)}, bf16[256,768]{1,0:T(8,128)(2,1)S(1)}, u32[]{:S(2)}, u32[]{:S(2)}) collective-permute-start(bf16[256,768]{1,0:T(8,128)(2,1)} %get-tuple-element.209.own_ref), channel_id=1, source_target_pairs={{0,4},{4,0},{8,12},{12,8},{16,20},{20,16},{24,28},{28,24},{1,5},{5... | collective-permute-start | bytes 1179656 | tf_op jit(solution)/shard_map/ppermute | solution.py:481
  139.3 10.9 %collective-permute-start.24 = (bf16[256,2688]{1,0:T(8,128)(2,1)}, bf16[256,2688]{1,0:T(8,128)(2,1)S(1)}, u32[]{:S(2)}, u32[]{:S(2)}) collective-permute-start(bf16[256,2688]{1,0:T(8,128)(2,1)} %get-tuple-element.215), channel_id=1, source_target_pairs={{0,4},{4,0},{8,12},{12,8},{16,20},{20,16},{24,28},{28,24},{1,5},{5... | collective-permute-start | bytes 4128776 | tf_op jit(solution)/shard_map/ppermute | solution.py:481
  139.4 21.4 %collective-permute-start.23 = (bf16[256,768]{1,0:T(8,128)(2,1)S(1)}, bf16[256,768]{1,0:T(8,128)(2,1)S(1)}, u32[]{:S(2)}, u32[]{:S(2)}) collective-permute-start(bf16[256,768]{1,0:T(8,128)(2,1)S(1)} %copy-done.46), channel_id=1, source_target_pairs={{0,0},{1,4},{2,1},{3,5},{4,2},{5,6},{6,3},{7,7},{8,8},{9,12},{10,9... | collective-permute-start | bytes 1179656 | tf_op jit(solution)/shard_map/ppermute | solution.py:495
  151.4 7.5 %collective-permute-start.25 = (bf16[192,512]{1,0:T(8,128)(2,1)S(1)}, bf16[192,512]{1,0:T(8,128)(2,1)S(1)}, u32[]{:S(2)}, u32[]{:S(2)}) collective-permute-start(bf16[192,512]{1,0:T(8,128)(2,1)S(1)} %slice.396), channel_id=1, source_target_pairs={{0,1},{1,0},{2,3},{3,2},{4,5},{5,4},{6,7},{7,6},{8,9},{9,8},{10,11... | collective-permute-start | bytes 589832 | tf_op jit(solution)/shard_map/ppermute | solution.py:484
  175.9 16.2 %collective-permute-start.28 = (bf16[256,2688]{1,0:T(8,128)(2,1)}, bf16[256,2688]{1,0:T(8,128)(2,1)S(1)}, u32[]{:S(2)}, u32[]{:S(2)}) collective-permute-start(bf16[256,2688]{1,0:T(8,128)(2,1)} %get-tuple-element.226), channel_id=1, source_target_pairs={{0,4},{4,0},{8,12},{12,8},{16,20},{20,16},{24,28},{28,24},{1,5},{5... | collective-permute-start | bytes 4128776 | tf_op jit(solution)/shard_map/ppermute | solution.py:481
  176.3 15.8 %collective-permute-start.29 = (bf16[256,768]{1,0:T(8,128)(2,1)}, bf16[256,768]{1,0:T(8,128)(2,1)}, u32[]{:S(2)}, u32[]{:S(2)}) collective-permute-start(bf16[256,768]{1,0:T(8,128)(2,1)} %get-tuple-element.227), channel_id=1, source_target_pairs={{0,0},{4,1},{1,2},{5,3},{2,4},{6,5},{3,6},{7,7},{8,8},{12,9},{9,10... | collective-permute-start | bytes 1179656 | tf_op jit(solution)/shard_map/ppermute | solution.py:498
  180.8 11.3 %collective-permute-start.27 = (bf16[256,768]{1,0:T(8,128)(2,1)S(1)}, bf16[256,768]{1,0:T(8,128)(2,1)}, u32[]{:S(2)}, u32[]{:S(2)}) collective-permute-start(bf16[256,768]{1,0:T(8,128)(2,1)S(1)} %get-tuple-element.225), channel_id=1, source_target_pairs={{0,4},{4,0},{8,12},{12,8},{16,20},{20,16},{24,28},{28,24},{1,5},{5... | collective-permute-start | bytes 1179656 | tf_op jit(solution)/shard_map/ppermute | solution.py:481
  195.5 7.2 %collective-permute-start.31 = (bf16[192,512]{1,0:T(8,128)(2,1)S(1)}, bf16[192,512]{1,0:T(8,128)(2,1)S(1)}, u32[]{:S(2)}, u32[]{:S(2)}) collective-permute-start(bf16[192,512]{1,0:T(8,128)(2,1)S(1)} %get-tuple-element.401), channel_id=1, source_target_pairs={{0,1},{1,0},{2,3},{3,2},{4,5},{5,4},{6,7},{7,6},{8,9},{9,8},{10,11... | collective-permute-start | bytes 589832 | tf_op jit(solution)/shard_map/ppermute | solution.py:484
  203.5 13.1 %collective-permute-start.32 = (bf16[256,1536]{1,0:T(8,128)(2,1)}, bf16[256,1536]{1,0:T(8,128)(2,1)}, u32[]{:S(2)}, u32[]{:S(2)}) collective-permute-start(bf16[256,1536]{1,0:T(8,128)(2,1)} %get-tuple-element.234), channel_id=1, source_target_pairs={{0,4},{4,0},{8,12},{12,8},{16,20},{20,16},{24,28},{28,24},{1,5},{5... | collective-permute-start | bytes 2359304 | tf_op jit(solution)/shard_map/ppermute | solution.py:481
  203.5 13.1 %collective-permute-start.33 = (bf16[256,768]{1,0:T(8,128)(2,1)}, bf16[256,768]{1,0:T(8,128)(2,1)}, u32[]{:S(2)}, u32[]{:S(2)}) collective-permute-start(bf16[256,768]{1,0:T(8,128)(2,1)} %get-tuple-element.235), channel_id=1, source_target_pairs={{0,4},{4,0},{8,12},{12,8},{16,20},{20,16},{24,28},{28,24},{1,5},{5... | collective-permute-start | bytes 1179656 | tf_op jit(solution)/shard_map/ppermute | solution.py:481
  221.4 11.3 %collective-permute-start.35 = (bf16[256,768]{1,0:T(8,128)(2,1)S(1)}, bf16[256,768]{1,0:T(8,128)(2,1)}, u32[]{:S(2)}, u32[]{:S(2)}) collective-permute-start(bf16[256,768]{1,0:T(8,128)(2,1)S(1)} %get-tuple-element.379), channel_id=1, source_target_pairs={{0,1},{1,0},{2,3},{3,2},{4,5},{5,4},{6,7},{7,6},{8,9},{9,8},{10,11... | collective-permute-start | bytes 1179656 | tf_op jit(solution)/shard_map/ppermute | solution.py:484
  243.4 15.6 %collective-permute-start.37 = (bf16[2,2,96,768]{3,2,1,0:T(8,128)(2,1)}, bf16[2,2,96,768]{3,2,1,0:T(8,128)(2,1)S(1)}, u32[]{:S(2)}, u32[]{:S(2)}) collective-permute-start(bf16[2,2,96,768]{3,2,1,0:T(8,128)(2,1)} %slice_bitcast_fusion.3), channel_id=1, source_target_pairs={{0,8},{4,12},{8,0},{12,4},{16,24},{20,28},{24,16},{28,20},{1,9},{5... | collective-permute-start | bytes 1769480 | tf_op jit(solution)/shard_map/ppermute | solution.py:481
  244.5 15.3 %collective-permute-start.38 = (bf16[2,2,96,768]{3,2,1,0:T(8,128)(2,1)}, bf16[2,2,96,768]{3,2,1,0:T(8,128)(2,1)S(1)}, u32[]{:S(2)}, u32[]{:S(2)}) collective-permute-start(bf16[2,2,96,768]{3,2,1,0:T(8,128)(2,1)} %slice_bitcast_fusion.2), channel_id=1, source_target_pairs={{0,16},{4,20},{8,24},{12,28},{16,0},{20,4},{24,8},{28,12},{1,17},{... | collective-permute-start | bytes 1769480 | tf_op jit(solution)/shard_map/ppermute | solution.py:481
  264.9 11.6 %collective-permute-start.43 = (bf16[2,96,768]{2,1,0:T(8,128)(2,1)S(1)}, bf16[2,96,768]{2,1,0:T(8,128)(2,1)S(1)}, u32[]{:S(2)}, u32[]{:S(2)}) collective-permute-start(bf16[2,96,768]{2,1,0:T(8,128)(2,1)S(1)} %slice_bitcast_fusion.19), channel_id=1, source_target_pairs={{0,16},{4,20},{8,24},{12,28},{16,0},{20,4},{24,8},{28,12},{1,17},{... | collective-permute-start | bytes 884744 | tf_op jit(solution)/shard_map/ppermute | solution.py:481
  266.5 10.1 %collective-permute-start.44 = (bf16[2,96,768]{2,1,0:T(8,128)(2,1)S(1)}, bf16[2,96,768]{2,1,0:T(8,128)(2,1)S(1)}, u32[]{:S(2)}, u32[]{:S(2)}) collective-permute-start(bf16[2,96,768]{2,1,0:T(8,128)(2,1)S(1)} %slice_bitcast_fusion.18), channel_id=1, source_target_pairs={{0,8},{4,12},{8,0},{12,4},{16,24},{20,28},{24,16},{28,20},{1,9},{5... | collective-permute-start | bytes 884744 | tf_op jit(solution)/shard_map/ppermute | solution.py:481
  267.4 10.2 %collective-permute-start.42 = (bf16[192,512]{1,0:T(8,128)(2,1)S(1)}, bf16[192,512]{1,0:T(8,128)(2,1)S(1)}, u32[]{:S(2)}, u32[]{:S(2)}) collective-permute-start(bf16[192,512]{1,0:T(8,128)(2,1)S(1)} %get-tuple-element.397), channel_id=1, source_target_pairs={{0,1},{1,0},{2,3},{3,2},{4,5},{5,4},{6,7},{7,6},{8,9},{9,8},{10,11... | collective-permute-start | bytes 589832 | tf_op jit(solution)/shard_map/ppermute | solution.py:484
  276.5 18.1 %collective-permute-start.47 = (bf16[2,2,120,768]{3,2,1,0:T(8,128)(2,1)}, bf16[2,2,120,768]{3,2,1,0:T(8,128)(2,1)}, u32[]{:S(2)}, u32[]{:S(2)}) collective-permute-start(bf16[2,2,120,768]{3,2,1,0:T(8,128)(2,1)} %fusion.68), channel_id=1, source_target_pairs={{0,16},{4,20},{8,24},{12,28},{16,0},{20,4},{24,8},{28,12},{1,17},{... | collective-permute-start | bytes 2211848 | tf_op jit(solution)/shard_map/ppermute | solution.py:481
  277.1 17.7 %collective-permute-start.46 = (bf16[2,2,120,768]{3,2,1,0:T(8,128)(2,1)}, bf16[2,2,120,768]{3,2,1,0:T(8,128)(2,1)}, u32[]{:S(2)}, u32[]{:S(2)}) collective-permute-start(bf16[2,2,120,768]{3,2,1,0:T(8,128)(2,1)} %fusion.72), channel_id=1, source_target_pairs={{0,8},{4,12},{8,0},{12,4},{16,24},{20,28},{24,16},{28,20},{1,9},{5... | collective-permute-start | bytes 2211848 | tf_op jit(solution)/shard_map/ppermute | solution.py:481
  279.2 14.1 %collective-permute-start.45 = (bf16[2,96,768]{2,1,0:T(8,128)(2,1)}, bf16[2,96,768]{2,1,0:T(8,128)(2,1)}, u32[]{:S(2)}, u32[]{:S(2)}) collective-permute-start(bf16[2,96,768]{2,1,0:T(8,128)(2,1)} %fusion.77), channel_id=1, source_target_pairs={{0,1},{1,0},{2,3},{3,2},{4,5},{5,4},{6,7},{7,6},{8,9},{9,8},{10,11... | collective-permute-start | bytes 884744 | tf_op jit(solution)/shard_map/ppermute | solution.py:484
  296.1 3.5 collective-permute-start.48
  300.9 11.0 %collective-permute-start.49 = (bf16[2,120,768]{2,1,0:T(8,128)(2,1)S(1)}, bf16[2,120,768]{2,1,0:T(8,128)(2,1)S(1)}, u32[]{:S(2)}, u32[]{:S(2)}) collective-permute-start(bf16[2,120,768]{2,1,0:T(8,128)(2,1)S(1)} %slice_bitcast_fusion.14), channel_id=1, source_target_pairs={{0,16},{4,20},{8,24},{12,28},{16,0},{20,4},{24,8},{28,12},{1,17},{... | collective-permute-start | bytes 1105928 | tf_op jit(solution)/shard_map/ppermute | solution.py:481
  302.4 10.7 %collective-permute-start.50 = (bf16[2,120,768]{2,1,0:T(8,128)(2,1)S(1)}, bf16[2,120,768]{2,1,0:T(8,128)(2,1)S(1)}, u32[]{:S(2)}, u32[]{:S(2)}) collective-permute-start(bf16[2,120,768]{2,1,0:T(8,128)(2,1)S(1)} %slice_bitcast_fusion.13), channel_id=1, source_target_pairs={{0,8},{4,12},{8,0},{12,4},{16,24},{20,28},{24,16},{28,20},{1,9},{5... | collective-permute-start | bytes 1105928 | tf_op jit(solution)/shard_map/ppermute | solution.py:481
  304.9 13.2 %collective-permute-start.53 = (bf16[256,768]{1,0:T(8,128)(2,1)S(1)}, bf16[256,768]{1,0:T(8,128)(2,1)S(1)}, u32[]{:S(2)}, u32[]{:S(2)}) collective-permute-start(bf16[256,768]{1,0:T(8,128)(2,1)S(1)} %get-tuple-element.303), channel_id=1, source_target_pairs={{0,1},{1,0},{2,3},{3,2},{4,5},{5,4},{6,7},{7,6},{8,9},{9,8},{10,11... | collective-permute-start | bytes 1179656 | tf_op jit(solution)/shard_map/ppermute | solution.py:484
  313.2 13.8 %collective-permute-start.51 = (bf16[2,120,768]{2,1,0:T(8,128)(2,1)S(1)}, bf16[2,120,768]{2,1,0:T(8,128)(2,1)S(1)}, u32[]{:S(2)}, u32[]{:S(2)}) collective-permute-start(bf16[2,120,768]{2,1,0:T(8,128)(2,1)S(1)} %fusion.74), channel_id=1, source_target_pairs={{0,1},{1,0},{2,3},{3,2},{4,5},{5,4},{6,7},{7,6},{8,9},{9,8},{10,11... | collective-permute-start | bytes 1105928 | tf_op jit(solution)/shard_map/ppermute | solution.py:484
  314.7 11.2 %collective-permute-start.52 = (bf16[96,768]{1,0:T(8,128)(2,1)}, bf16[96,768]{1,0:T(8,128)(2,1)S(1)}, u32[]{:S(2)}, u32[]{:S(2)}) collective-permute-start(bf16[96,768]{1,0:T(8,128)(2,1)} %slice_bitcast_fusion.22), channel_id=1, source_target_pairs={{0,2},{1,3},{2,0},{3,1},{4,6},{5,7},{6,4},{7,5},{8,10},{9,11},{10,... | collective-permute-start | bytes 442376 | tf_op jit(solution)/shard_map/ppermute | solution.py:484
  316.8 10.4 %collective-permute-start.54 = (bf16[2,72,768]{2,1,0:T(8,128)(2,1)}, bf16[2,72,768]{2,1,0:T(8,128)(2,1)}, u32[]{:S(2)}, u32[]{:S(2)}) collective-permute-start(bf16[2,72,768]{2,1,0:T(8,128)(2,1)} %bitcast.293), channel_id=1, source_target_pairs={{0,8},{4,12},{8,0},{12,4},{16,24},{20,28},{24,16},{28,20},{1,9},{5... | collective-permute-start | bytes 663560 | tf_op jit(solution)/shard_map/ppermute | solution.py:481
  317.3 9.9 %collective-permute-start.55 = (bf16[2,72,768]{2,1,0:T(8,128)(2,1)}, bf16[2,72,768]{2,1,0:T(8,128)(2,1)}, u32[]{:S(2)}, u32[]{:S(2)}) collective-permute-start(bf16[2,72,768]{2,1,0:T(8,128)(2,1)} %bitcast.292), channel_id=1, source_target_pairs={{0,16},{4,20},{8,24},{12,28},{16,0},{20,4},{24,8},{28,12},{1,17},{... | collective-permute-start | bytes 663560 | tf_op jit(solution)/shard_map/ppermute | solution.py:481
  329.3 4.8 %collective-permute-start.58 = (bf16[72,768]{1,0:T(8,128)(2,1)S(1)}, bf16[72,768]{1,0:T(8,128)(2,1)S(1)}, u32[]{:S(2)}, u32[]{:S(2)}) collective-permute-start(bf16[72,768]{1,0:T(8,128)(2,1)S(1)} %select_bitcast_fusion), channel_id=1, source_target_pairs={{0,8},{4,12},{8,0},{12,4},{16,24},{20,28},{24,16},{28,20},{1,9},{5... | collective-permute-start | bytes 331784 | tf_op jit(solution)/shard_map/ppermute | solution.py:481
  330.8 4.7 %collective-permute-start.57 = (bf16[72,768]{1,0:T(8,128)(2,1)S(1)}, bf16[72,768]{1,0:T(8,128)(2,1)S(1)}, u32[]{:S(2)}, u32[]{:S(2)}) collective-permute-start(bf16[72,768]{1,0:T(8,128)(2,1)S(1)} %select_bitcast_fusion.1), channel_id=1, source_target_pairs={{0,16},{4,20},{8,24},{12,28},{16,0},{20,4},{24,8},{28,12},{1,17},{... | collective-permute-start | bytes 331784 | tf_op jit(solution)/shard_map/ppermute | solution.py:481
  331.5 10.0 %collective-permute-start.56 = (bf16[120,768]{1,0:T(8,128)(2,1)S(1)}, bf16[120,768]{1,0:T(8,128)(2,1)S(1)}, u32[]{:S(2)}, u32[]{:S(2)}) collective-permute-start(bf16[120,768]{1,0:T(8,128)(2,1)S(1)} %slice_bitcast_fusion.20), channel_id=1, source_target_pairs={{0,2},{1,3},{2,0},{3,1},{4,6},{5,7},{6,4},{7,5},{8,10},{9,11},{10,... | collective-permute-start | bytes 552968 | tf_op jit(solution)/shard_map/ppermute | solution.py:484
  336.6 11.1 %collective-permute-start.59 = (bf16[2,72,768]{2,1,0:T(8,128)(2,1)S(1)}, bf16[2,72,768]{2,1,0:T(8,128)(2,1)S(1)}, u32[]{:S(2)}, u32[]{:S(2)}) collective-permute-start(bf16[2,72,768]{2,1,0:T(8,128)(2,1)S(1)} %pad_maximum_fusion.20), channel_id=1, source_target_pairs={{2,0},{3,1},{4,6},{5,7},{10,8},{11,9},{12,14},{13,15},{18,16},{19,... | collective-permute-start | bytes 663560 | tf_op jit(solution)/shard_map/ppermute | solution.py:509
  337.9 4.2 %collective-permute-start.61 = (f32[12,768]{1,0:T(8,128)S(1)}, f32[12,768]{1,0:T(8,128)S(1)}, u32[]{:S(2)}, u32[]{:S(2)}) collective-permute-start(f32[12,768]{1,0:T(8,128)S(1)} %fusion.101), channel_id=1, source_target_pairs={{0,8},{4,12},{8,0},{12,4},{16,24},{20,28},{24,16},{28,20},{1,9},{5... | collective-permute-start | bytes 110600 | tf_op jit(solution)/shard_map/ppermute | solution.py:481
  347.9 7.8 %collective-permute-start.63 = (bf16[1,184,768]{2,1,0:T(8,128)(2,1)S(1)}, bf16[1,184,768]{2,1,0:T(8,128)(2,1)S(1)}, u32[]{:S(2)}, u32[]{:S(2)}) collective-permute-start(bf16[1,184,768]{2,1,0:T(8,128)(2,1)S(1)} %fusion.85), channel_id=1, source_target_pairs={{0,8},{4,12},{8,0},{12,4},{16,24},{20,28},{24,16},{28,20},{1,9},{5... | collective-permute-start | bytes 847880 | tf_op jit(solution)/shard_map/ppermute | solution.py:481
  348.5 7.2 %collective-permute-start.62 = (bf16[1,176,768]{2,1,0:T(8,128)(2,1)S(1)}, bf16[1,176,768]{2,1,0:T(8,128)(2,1)S(1)}, u32[]{:S(2)}, u32[]{:S(2)}) collective-permute-start(bf16[1,176,768]{2,1,0:T(8,128)(2,1)S(1)} %maximum_bitcast_fusion), channel_id=1, source_target_pairs={{0,16},{4,20},{8,24},{12,28},{16,0},{20,4},{24,8},{28,12},{1,17},{... | collective-permute-start | bytes 811016 | tf_op jit(solution)/shard_map/ppermute | solution.py:481
  349.0 6.0 %collective-permute-start.66 = (f32[12,768]{1,0:T(8,128)S(1)}, f32[12,768]{1,0:T(8,128)S(1)}, u32[]{:S(2)}, u32[]{:S(2)}) collective-permute-start(f32[12,768]{1,0:T(8,128)S(1)} %add.209), channel_id=1, source_target_pairs={{0,3},{1,2},{2,1},{3,0},{4,7},{5,6},{6,5},{7,4},{8,11},{9,10},{10,... | collective-permute-start | bytes 110600 | tf_op jit(solution)/shard_map/ppermute | solution.py:484
  349.0 6.1 %collective-permute-start.65 = (f32[12,768]{1,0:T(8,128)S(1)}, f32[12,768]{1,0:T(8,128)S(1)}, u32[]{:S(2)}, u32[]{:S(2)}) collective-permute-start(f32[12,768]{1,0:T(8,128)S(1)} %add.209), channel_id=1, source_target_pairs={{0,2},{1,3},{2,0},{3,1},{4,6},{5,7},{6,4},{7,5},{8,10},{9,11},{10,... | collective-permute-start | bytes 110600 | tf_op jit(solution)/shard_map/ppermute | solution.py:484
  350.8 4.9 %collective-permute-start.64 = (f32[12,768]{1,0:T(8,128)S(1)}, f32[12,768]{1,0:T(8,128)S(1)}, u32[]{:S(2)}, u32[]{:S(2)}) collective-permute-start(f32[12,768]{1,0:T(8,128)S(1)} %add.209), channel_id=1, source_target_pairs={{0,1},{1,0},{2,3},{3,2},{4,5},{5,4},{6,7},{7,6},{8,9},{9,8},{10,11... | collective-permute-start | bytes 110600 | tf_op jit(solution)/shard_map/ppermute | solution.py:484
  355.9 15.5 %collective-permute-start.68 = (bf16[2,184,768]{2,1,0:T(8,128)(2,1)S(1)}, bf16[2,184,768]{2,1,0:T(8,128)(2,1)S(1)}, u32[]{:S(2)}, u32[]{:S(2)}) collective-permute-start(bf16[2,184,768]{2,1,0:T(8,128)(2,1)S(1)} %maximum_select_fusion.3), channel_id=1, source_target_pairs={{0,16},{4,20},{8,24},{12,28},{16,0},{20,4},{24,8},{28,12},{1,17},{... | collective-permute-start | bytes 1695752 | tf_op jit(solution)/shard_map/ppermute | solution.py:481
  357.5 13.9 %collective-permute-start.67 = (bf16[2,176,768]{2,1,0:T(8,128)(2,1)S(1)}, bf16[2,176,768]{2,1,0:T(8,128)(2,1)S(1)}, u32[]{:S(2)}, u32[]{:S(2)}) collective-permute-start(bf16[2,176,768]{2,1,0:T(8,128)(2,1)S(1)} %maximum_select_fusion.4), channel_id=1, source_target_pairs={{0,8},{4,12},{8,0},{12,4},{16,24},{20,28},{24,16},{28,20},{1,9},{5... | collective-permute-start | bytes 1622024 | tf_op jit(solution)/shard_map/ppermute | solution.py:481
  358.9 12.4 %collective-permute-start.69 = (bf16[256,768]{1,0:T(8,128)(2,1)S(1)}, bf16[256,768]{1,0:T(8,128)(2,1)S(1)}, u32[]{:S(2)}, u32[]{:S(2)}) collective-permute-start(bf16[256,768]{1,0:T(8,128)(2,1)S(1)} %copy-done.49), channel_id=1, source_target_pairs={{0,0},{4,1},{1,2},{5,3},{2,4},{6,5},{3,6},{7,7},{8,8},{12,9},{9,10... | collective-permute-start | bytes 1179656 | tf_op jit(solution)/shard_map/ppermute | solution.py:498
  359.6 11.7 %collective-permute-start.70 = (f32[12,768]{1,0:T(8,128)S(1)}, f32[12,768]{1,0:T(8,128)S(1)}, u32[]{:S(2)}, u32[]{:S(2)}) collective-permute-start(f32[12,768]{1,0:T(8,128)S(1)} %add_add_fusion), channel_id=1, source_target_pairs={{0,16},{4,20},{8,24},{12,28},{16,0},{20,4},{24,8},{28,12},{1,17},{... | collective-permute-start | bytes 110600 | tf_op jit(solution)/shard_map/ppermute | solution.py:481
  372.3 4.5 %collective-permute-start.72 = (bf16[2,2,184,768]{3,2,1,0:T(8,128)(2,1)S(1)}, bf16[2,2,184,768]{3,2,1,0:T(8,128)(2,1)S(1)}, u32[]{:S(2)}, u32[]{:S(2)}) collective-permute-start(bf16[2,2,184,768]{3,2,1,0:T(8,128)(2,1)S(1)} %maximum_select_fusion.two_ref), channel_id=1, source_target_pairs={{0,4},{4,0},{8,12},{12,8},{16,20},{20,16},{24,28},{28,24},{1,5},{5... | collective-permute-start | bytes 3391496 | tf_op jit(solution)/shard_map/ppermute | solution.py:481
  372.6 4.2 %collective-permute-start.71 = (bf16[2,2,176,768]{3,2,1,0:T(8,128)(2,1)S(1)}, bf16[2,2,176,768]{3,2,1,0:T(8,128)(2,1)}, u32[]{:S(2)}, u32[]{:S(2)}) collective-permute-start(bf16[2,2,176,768]{3,2,1,0:T(8,128)(2,1)S(1)} %maximum_select_fusion.1.one_ref), channel_id=1, source_target_pairs={{0,4},{4,0},{8,12},{12,8},{16,20},{20,16},{24,28},{28,24},{1,5},{5... | collective-permute-start | bytes 3244040 | tf_op jit(solution)/shard_map/ppermute | solution.py:481
  (74 other events, 447.2 us)
